TPU v7x, 512 devices: a whole 4x8x8 slice. The times are simulated.
512 devices in a mesh: orb: 64 (over z, y_hi, core), slab: 8 (over y_lo, x).
Axes of the slice: x: 4, y: 8 (y_hi: 4, y_lo: 2; y = y_hi * 2 + y_lo), z: 8, core: 2. Of those that a mesh axis runs over, the one named last changes fastest.
Arguments:
- orbitals: bfloat16 [64, 64, 4096], P('orb', 'slab'), may hold values from -6 to 6
- partners: int32 [64, 2], P('orb'), may hold values from 0 to 63, as said below
- offsets: int32 [64, 3], P('orb'), may hold values from 0 to 32
- kernel: float32 [128, 128, 128], P(None, 'slab'), may hold values from 0.5 to 8
Outputs:
- exchange: float32 [64, 64, 4096], P('orb', 'slab')
Inputs may be any that keep to these rules, and one draw needn't show every extreme that they name: Orbital i's two partners differ from each other and equal (i + e) mod 64 with 1 <= e <= 4.
All inputs are finite; a program needn't handle non-finite values.
Results may differ from a plain program's by a relative error of at most 0.0042.
Values may be sent and summed in bfloat16 or wider, within the bound.
No kernel may reach another device: no remote copies, remote signals or barrier semaphores. Data moves between devices by JAX's collectives and lax.ppermute only.
A program may use at most 128 MiB of HBM per device.

v0:
```python
from functools import partial
import math

import jax
import jax.numpy as jnp
from jax import lax
from jax.sharding import PartitionSpec as P

REACH = 4


def passed_along(block, axis, distance):
    devices = range(lax.axis_size(axis))
    route = [((i - distance) % len(devices), i) for i in devices]
    return lax.ppermute(block, axis, route)


def from_everyone(shard, axis):
    copies = jnp.broadcast_to(shard, (lax.axis_size(axis), *shard.shape))
    return lax.all_to_all(copies, axis, split_axis=0, concat_axis=0, tiled=True)


def laid_out(parts, dim):
    parts = jnp.moveaxis(parts, 0, dim)
    shape = parts.shape
    return parts.reshape(*shape[:dim], shape[dim] * shape[dim + 1], *shape[dim + 2 :])


def gathered_copies(shard, axis, dim):
    parts = from_everyone(shard, axis)
    return laid_out(parts, dim)


def in_one_piece(arrays, axis, split_dim, concat_dim, along):
    ends, at = ([], 0)
    for a in arrays[:-1]:
        at += a.shape[along]
        ends.append(at)
    both = jnp.concatenate(arrays, axis=along)
    return tuple(
        jnp.split(
            lax.all_to_all(both, axis, split_axis=split_dim, concat_axis=concat_dim, tiled=True),
            ends,
            axis=along,
        )
    )


def phase_table(length, offset, grid_len, signed):
    frequency = jnp.arange(grid_len, dtype=jnp.int32)
    places = offset + jnp.arange(length, dtype=jnp.int32)
    wrapped = places[:, None] * frequency[None, :] % grid_len
    angles = wrapped.astype(jnp.float32) * (2.0 * math.pi / grid_len)
    return (jnp.cos(angles).astype(jnp.bfloat16), (signed * jnp.sin(angles)).astype(jnp.bfloat16))


def move_box(orbital_box, displacement, row_start, row_count):
    box_edge = orbital_box.shape[1]
    rows = row_start + displacement[0] + jnp.arange(row_count, dtype=jnp.int32)
    cols = displacement[1] + jnp.arange(box_edge, dtype=jnp.int32)
    depth = displacement[2] + jnp.arange(box_edge, dtype=jnp.int32)
    picked = jnp.take(orbital_box, jnp.clip(rows, 0, box_edge - 1), axis=0)
    picked = jnp.take(picked, jnp.clip(cols, 0, box_edge - 1), axis=1)
    picked = jnp.take(picked, jnp.clip(depth, 0, box_edge - 1), axis=2)
    row_ok = (rows >= 0) & (rows < box_edge)
    col_ok = (cols >= 0) & (cols < box_edge)
    dep_ok = (depth >= 0) & (depth < box_edge)
    inside = row_ok[:, None, None] & col_ok[None, :, None] & dep_ok[None, None, :]
    return jnp.where(inside, picked, jnp.zeros_like(picked))


def product(form, left_side, right_side):
    return jnp.einsum(form, left_side, right_side, preferred_element_type=jnp.float32)


def complex_pair(form, cos_table, sin_table, real_part, imag_part):
    real_out = product(form, cos_table, real_part) - product(form, sin_table, imag_part)
    imag_out = product(form, cos_table, imag_part) + product(form, sin_table, real_part)
    return (real_out, imag_out)


def box_tables(box_edge, half_edge, grid_len, displace_part):
    own_cos, own_sin = phase_table(box_edge, half_edge, grid_len, 1.0)
    far_cos, far_sin = jax.vmap(
        lambda value: phase_table(box_edge, half_edge + value, grid_len, 1.0)
    )(displace_part)
    cos_stack = jnp.stack([jnp.broadcast_to(own_cos, far_cos.shape), far_cos], 1)
    sin_stack = jnp.stack([jnp.broadcast_to(own_sin, far_sin.shape), far_sin], 1)
    return (cos_stack, sin_stack)


def per_device(orbitals, partners, offsets, kernel):
    orb_dev = orbitals.shape[0]
    slab_rows = orbitals.shape[1]
    box_edge = math.isqrt(orbitals.shape[2])
    grid_len = 2 * box_edge
    half_edge = box_edge // 2
    spread = lax.axis_size("orb")
    orbit_count = orb_dev * spread
    orbit_index = lax.axis_index("orb")
    first_orbit = orbit_index * orb_dev
    slab_index = lax.axis_index("slab")
    row_start = slab_index * slab_rows
    corner_list = [offsets]
    box_list = [orbitals]
    for hop_count in range(1, REACH + 1):
        far_box, far_corner = passed_along((orbitals, offsets), "orb", -hop_count)
        box_list.append(far_box)
        corner_list.append(far_corner)
    candidates = gathered_copies(jnp.concatenate(box_list, 0), "slab", 1)
    corners = jnp.concatenate(corner_list, 0)
    candidates = candidates.reshape(candidates.shape[0], box_edge, box_edge, box_edge)
    pair_count = 2 * orb_dev
    partner_ids = partners.reshape(pair_count)
    owner_slot = jnp.arange(pair_count, dtype=jnp.int32) // 2
    local_slot = (partner_ids - first_orbit) % orbit_count
    displace = corners[local_slot] - offsets[owner_slot]
    fwd_cos, fwd_sin = phase_table(box_edge, half_edge, grid_len, -1.0)
    partner_full = candidates[local_slot]
    own_boxes = candidates[owner_slot]
    own_rows = orbitals.reshape(orb_dev, slab_rows, box_edge, box_edge)[owner_slot]
    mover = jax.vmap(partial(move_box, row_count=slab_rows), in_axes=(0, 0, None))
    partner_here = mover(partner_full, -displace, row_start)
    own_there = mover(own_boxes, displace, row_start)
    density = (own_rows.astype(jnp.float32) * partner_here.astype(jnp.float32)).astype(jnp.bfloat16)
    z_real = product("payz,zk->payk", density, fwd_cos).astype(jnp.bfloat16)
    z_imag = product("payz,zk->payk", density, fwd_sin).astype(jnp.bfloat16)
    y_real, y_imag = complex_pair("yk,payq->pakq", fwd_cos, fwd_sin, z_real, z_imag)
    y_real, y_imag = (y_real.astype(jnp.bfloat16), y_imag.astype(jnp.bfloat16))
    col_real, col_imag = in_one_piece((y_real, y_imag), "slab", 2, 1, 0)
    x_real, x_imag = complex_pair("ak,paqz->pkqz", fwd_cos, fwd_sin, col_real, col_imag)
    w_real = (kernel * x_real).astype(jnp.bfloat16)
    w_imag = (kernel * x_imag).astype(jnp.bfloat16)
    row_cos, row_sin = box_tables(box_edge, half_edge, grid_len, displace[:, 0])
    v_real, v_imag = complex_pair("pmak,pkqz->pmaqz", row_cos, row_sin, w_real, w_imag)
    v_real, v_imag = (v_real.astype(jnp.bfloat16), v_imag.astype(jnp.bfloat16))
    back_real, back_imag = in_one_piece((v_real, v_imag), "slab", 2, 3, 0)
    col_cos, col_sin = box_tables(box_edge, half_edge, grid_len, displace[:, 1])
    u_real, u_imag = complex_pair("pmyk,pmrkz->pmryz", col_cos, col_sin, back_real, back_imag)
    u_real, u_imag = (u_real.astype(jnp.bfloat16), u_imag.astype(jnp.bfloat16))
    dep_cos, dep_sin = box_tables(box_edge, half_edge, grid_len, displace[:, 2])
    field = (
        product("pmzk,pmryk->pmryz", dep_cos, u_real)
        - product("pmzk,pmryk->pmryz", dep_sin, u_imag)
    ) * (1.0 / grid_len**3)
    own_term = field[:, 0] * partner_here.astype(jnp.float32)
    far_term = field[:, 1] * own_there.astype(jnp.float32)
    result = own_term.reshape(orb_dev, 2, slab_rows, box_edge, box_edge).sum(1)
    hop_of_pair = (partner_ids // orb_dev - orbit_index) % spread
    slot_match = (partner_ids % orb_dev)[:, None] == jnp.arange(orb_dev, dtype=jnp.int32)[None, :]
    for hop_count in range(REACH + 1):
        weights = (slot_match & (hop_of_pair == hop_count)[:, None]).astype(jnp.float32)
        bucket = jnp.einsum("po,prst->orst", weights, far_term, precision=lax.Precision.HIGHEST)
        if hop_count == 0:
            result = result + bucket
        else:
            result = result + passed_along(bucket, "orb", hop_count)
    return result.reshape(orb_dev, slab_rows, box_edge * box_edge)


def solution(mesh):
    return jax.shard_map(
        per_device,
        mesh=mesh,
        in_specs=(P("orb", "slab", None), P("orb", None), P("orb", None), P(None, "slab", None)),
        out_specs=P("orb", "slab", None),
        check_vma=False,
    )
```

profile of v0, /device:TPU:8, one launch (start us, length us, event | category | flops | bytes accessed | tf_op | source)
XLA Modules:
  0.0 212.8 jit_solution(16644169327392921975)
XLA Ops:
  0.0 14.7 %collective-permute-start.6 = (bf16[1,8,4096]{2,1,0:T(8,128)(2,1)}, bf16[1,8,4096]{2,1,0:T(8,128)(2,1)S(1)}, u32[]{:S(2)}, u32[]{:S(2)}) collective-permute-start(bf16[1,8,4096]{2,1,0:T(8,128)(2,1)} %param.10), channel_id=1, source_target_pairs={{24,0},{32,8},{40,16},{48,24},{56,32},{64,40},{72,48},{80,56},{88,... | collective-permute-start | bytes 196616 | tf_op jit(solution)/shard_map/ppermute | solution.py:15
  14.7 3.1 %collective-permute-start.5 = (bf16[1,8,4096]{2,1,0:T(8,128)(2,1)}, bf16[1,8,4096]{2,1,0:T(8,128)(2,1)S(1)}, u32[]{:S(2)}, u32[]{:S(2)}) collective-permute-start(bf16[1,8,4096]{2,1,0:T(8,128)(2,1)} %param.10), channel_id=1, source_target_pairs={{16,0},{24,8},{32,16},{40,24},{48,32},{56,40},{64,48},{72,56},{80,... | collective-permute-start | bytes 196616 | tf_op jit(solution)/shard_map/ppermute | solution.py:15
  17.9 2.5 %collective-permute-start.4 = (bf16[1,8,4096]{2,1,0:T(8,128)(2,1)}, bf16[1,8,4096]{2,1,0:T(8,128)(2,1)S(1)}, u32[]{:S(2)}, u32[]{:S(2)}) collective-permute-start(bf16[1,8,4096]{2,1,0:T(8,128)(2,1)} %param.10), channel_id=1, source_target_pairs={{8,0},{16,8},{24,16},{32,24},{40,32},{48,40},{56,48},{64,56},{72,6... | collective-permute-start | bytes 196616 | tf_op jit(solution)/shard_map/ppermute | solution.py:15
  20.4 5.0 %collective-permute-start.7 = (bf16[1,8,4096]{2,1,0:T(8,128)(2,1)}, bf16[1,8,4096]{2,1,0:T(8,128)(2,1)S(1)}, u32[]{:S(2)}, u32[]{:S(2)}) collective-permute-start(bf16[1,8,4096]{2,1,0:T(8,128)(2,1)} %param.10), channel_id=1, source_target_pairs={{32,0},{40,8},{48,16},{56,24},{64,32},{72,40},{80,48},{88,56},{96,... | collective-permute-start | bytes 196616 | tf_op jit(solution)/shard_map/ppermute | solution.py:15
  25.4 0.9 constant_dynamic-update-slice_fusion.4
  26.3 5.7 %collective-permute-done.7 = bf16[1,8,4096]{2,1,0:T(8,128)(2,1)S(1)} collective-permute-done((bf16[1,8,4096]{2,1,0:T(8,128)(2,1)}, bf16[1,8,4096]{2,1,0:T(8,128)(2,1)S(1)}, u32[]{:S(2)}, u32[]{:S(2)}) %collective-permute-start.7) | collective-permute-done | bytes 65568 | tf_op jit(solution)/shard_map/ppermute | solution.py:15
  32.1 1.8 broadcast_in_dim.33
  33.9 5.9 %all-to-all-start = ((bf16[8,5,8,4096]{3,2,1,0:T(8,128)(2,1)}), bf16[8,5,8,4096]{3,2,1,0:T(8,128)(2,1)S(1)}, u32[]{:S(2)}, u32[]{:S(2)}) async-start(bf16[8,5,8,4096]{3,2,1,0:T(8,128)(2,1)} %broadcast_in_dim.33), calls=%async_computation | async-start | bytes 5242880 | tf_op jit(solution)/shard_map/all_to_all | solution.py:20
  39.8 6.4 %collective-permute-start.3 = (s32[1,3]{1,0:T(1,128)S(1)}, s32[1,3]{1,0:T(1,128)S(1)}, u32[]{:S(2)}, u32[]{:S(2)}) collective-permute-start(s32[1,3]{1,0:T(1,128)S(1)} %copy-done.4), channel_id=1, source_target_pairs={{32,0},{40,8},{48,16},{56,24},{64,32},{72,40},{80,48},{88,56},{96,... | collective-permute-start | bytes 44 | tf_op jit(solution)/shard_map/ppermute | solution.py:15
  46.2 1.9 collective-permute-start.2
  48.2 2.3 %collective-permute-start.1 = (s32[1,3]{1,0:T(1,128)S(1)}, s32[1,3]{1,0:T(1,128)S(1)}, u32[]{:S(2)}, u32[]{:S(2)}) collective-permute-start(s32[1,3]{1,0:T(1,128)S(1)} %copy-done.4), channel_id=1, source_target_pairs={{16,0},{24,8},{32,16},{40,24},{48,32},{56,40},{64,48},{72,56},{80,... | collective-permute-start | bytes 44 | tf_op jit(solution)/shard_map/ppermute | solution.py:15
  50.5 3.2 %collective-permute-start = (s32[1,3]{1,0:T(1,128)S(1)}, s32[1,3]{1,0:T(1,128)S(1)}, u32[]{:S(2)}, u32[]{:S(2)}) collective-permute-start(s32[1,3]{1,0:T(1,128)S(1)} %copy-done.4), channel_id=1, source_target_pairs={{8,0},{16,8},{24,16},{32,24},{40,32},{48,40},{56,48},{64,56},{72,6... | collective-permute-start | bytes 44 | tf_op jit(solution)/shard_map/ppermute | solution.py:15
  53.9 16.0 %collective-permute-done.3 = s32[1,3]{1,0:T(1,128)S(1)} collective-permute-done((s32[1,3]{1,0:T(1,128)S(1)}, s32[1,3]{1,0:T(1,128)S(1)}, u32[]{:S(2)}, u32[]{:S(2)}) %collective-permute-start.3) | collective-permute-done | bytes 44 | tf_op jit(solution)/shard_map/ppermute | solution.py:15
  70.0 0.6 gather_fusion
  71.6 1.7 copy.68
  73.3 8.4 %reshape_reshape.3 = bf16[5,64,64,64]{3,2,1,0:T(8,128)(2,1)} reshape(bf16[5,8,8,4096]{3,2,1,0:T(8,128)(2,1)} %copy.68) | data formatting | bytes 5242880 | tf_op jit(solution)/shard_map/reshape;reshape | solution.py:112
  81.7 3.4 %gather_fusion.1 = bf16[2,64,64,64]{3,2,1,0:T(8,128)(2,1)S(1)} fusion(bf16[5,64,64,64]{3,2,1,0:T(8,128)(2,1)} %reshape_reshape.3, s32[1024]{0:T(1024)S(1)} %pad_clamp_fusion.1), kind=kCustom, calls=%fused_computation.7 | custom fusion | bytes 2097160 | tf_op jit(solution)/shard_map/gather | solution.py:119
  85.1 0.6 gather_fusion.3
  85.9 0.9 gather_fusion.4
  87.1 0.9 gather_fusion.5
  88.2 0.5 convolution_convert_fusion
  88.6 0.5 convolution_convert_fusion.1
  89.1 0.5 fusion.93
  89.6 0.5 fusion.91
  90.1 0.5 fusion.12
  90.6 0.5 fusion.11
  91.2 1.7 copy.73
  92.9 5.7 %all-to-all-start.1 = ((bf16[4,8,128,128]{3,1,0,2:T(8,128)(2,1)}), bf16[4,8,128,128]{3,1,0,2:T(8,128)(2,1)S(1)}, u32[]{:S(2)}, u32[]{:S(2)}) async-start(bf16[4,8,128,128]{3,1,0,2:T(8,128)(2,1)} %copy.73), calls=%async_computation.1 | async-start | bytes 2097152 | tf_op jit(solution)/shard_map/all_to_all | solution.py:42
  99.7 13.2 %all-to-all-done.1 = bf16[4,8,128,128]{3,1,0,2:T(8,128)(2,1)S(1)} async-done(((bf16[4,8,128,128]{3,1,0,2:T(8,128)(2,1)}), bf16[4,8,128,128]{3,1,0,2:T(8,128)(2,1)S(1)}, u32[]{:S(2)}, u32[]{:S(2)}) %all-to-all-start.1) | async-done | bytes 1048608 | tf_op jit(solution)/shard_map/all_to_all | solution.py:42
  113.5 0.7 fusion.21
  114.1 0.7 fusion.17
  114.8 0.8 fusion.2
  115.6 0.8 fusion.3
  116.9 0.4 fusion.60
  117.3 0.4 add_convert_fusion
  117.8 0.4 subtract_convert_fusion
  118.4 2.7 %copy.81 = bf16[4,2,64,16,128]{4,3,1,0,2:T(8,128)(2,1)} copy(bf16[4,2,64,16,128]{4,2,3,1,0:T(8,128)(2,1)S(1)} %pad_maximum_fusion) | data formatting | bytes 4194304 | tf_op jit(solution)/shard_map/concatenate | solution.py:39
  121.1 4.2 %all-to-all-start.2 = ((bf16[4,2,64,16,128]{4,3,1,0,2:T(8,128)(2,1)}), bf16[4,2,64,16,128]{4,3,1,0,2:T(8,128)(2,1)S(1)}, u32[]{:S(2)}, u32[]{:S(2)}) async-start(bf16[4,2,64,16,128]{4,3,1,0,2:T(8,128)(2,1)} %copy.81), calls=%async_computation.2 | async-start | bytes 4194304 | tf_op jit(solution)/shard_map/all_to_all | solution.py:42
  126.0 0.7 compare_and_fusion.6
  126.9 1.0 sine_convert_fusion
  128.2 4.7 %gather_fusion.2 = bf16[2,64,64,64]{3,2,1,0:T(8,128)(2,1)} fusion(bf16[5,64,64,64]{3,2,1,0:T(8,128)(2,1)} %reshape_reshape.3, s32[1024]{0:T(1024)S(1)} %pad_clamp_fusion), kind=kCustom, calls=%fused_computation.8 | custom fusion | bytes 2097160 | tf_op jit(solution)/shard_map/gather | solution.py:120
  132.9 2.2 %gather_fusion.6 = bf16[16,64,64]{2,1,0:T(8,128)(2,1)S(1)} fusion(bf16[2,64,64,64]{3,2,1,0:T(8,128)(2,1)} %gather_fusion.2, s32[16]{0:T(128)S(1)} %reshape.669), kind=kCustom, calls=%fused_computation.3.clone | custom fusion | bytes 262272 | tf_op jit(solution)/shard_map/vmap(jit(_take))/gather | solution.py:62
  135.3 0.9 gather_fusion.7
  136.4 0.9 gather_fusion.8
  137.3 0.9 copy.89
  138.2 12.8 %all-to-all-done.2 = bf16[4,2,64,16,128]{4,3,1,0,2:T(8,128)(2,1)S(1)} async-done(((bf16[4,2,64,16,128]{4,3,1,0,2:T(8,128)(2,1)}), bf16[4,2,64,16,128]{4,3,1,0,2:T(8,128)(2,1)S(1)}, u32[]{:S(2)}, u32[]{:S(2)}) %all-to-all-start.2) | async-done | bytes 2097184 | tf_op jit(solution)/shard_map/all_to_all | solution.py:42
  151.4 0.5 fusion.179
  152.5 1.3 fusion.64
  154.1 2.2 %fusion.13 = f32[2,2,8,64,64]{4,3,2,1,0:T(8,128)} fusion(f32[2,2,8,128,64]{3,4,2,1,0:T(8,128)S(1)} %fusion.62, bf16[2,2,8,128,128]{4,3,2,1,0:T(8,128)(2,1)S(1)} %bitcast.254, bf16[2,1,64,128]{3,2,1,0:T(8,128)(2,1)S(1)} %stack_broadcast_in_dim.18, bf16[2,1,64,128]{3,2,1,0:T(8,128)(2,1)} %get-tuple-element.26, ...), kind=kOutput, calls=%fused_computation.32 | convolution fusion | flops 101351424 | bytes 2752512 | tf_op jit(solution)/shard_map/pmzk,pmryk->pmryz/dot_general | solution.py:73
  156.3 2.0 fusion.4
  158.4 0.5 fusion.15
  159.0 1.3 fusion.84
  160.3 1.3 fusion.82
  161.6 1.3 fusion.80
  162.9 1.3 fusion.78
  164.2 2.0 collective-permute-start.11
  166.2 1.9 collective-permute-start.10
  168.1 2.5 %collective-permute-start.9 = (f32[1,8,64,64]{3,2,1,0:T(8,128)S(1)}, f32[1,8,64,64]{3,2,1,0:T(8,128)S(1)}, u32[]{:S(2)}, u32[]{:S(2)}) collective-permute-start(f32[1,8,64,64]{3,2,1,0:T(8,128)S(1)} %bitcast.268), channel_id=1, source_target_pairs={{496,0},{504,8},{0,16},{8,24},{16,32},{24,40},{32,48},{40,56},{48,... | collective-permute-start | bytes 393224 | tf_op jit(solution)/shard_map/ppermute | solution.py:15
  170.6 1.9 collective-permute-start.8
  172.5 1.3 fusion.86
  173.8 14.8 %collective-permute-done.11 = f32[1,8,64,64]{3,2,1,0:T(8,128)S(1)} collective-permute-done((f32[1,8,64,64]{3,2,1,0:T(8,128)S(1)}, f32[1,8,64,64]{3,2,1,0:T(8,128)S(1)}, u32[]{:S(2)}, u32[]{:S(2)}) %collective-permute-start.11) | collective-permute-done | bytes 131104 | tf_op jit(solution)/shard_map/ppermute | solution.py:15
  188.6 9.1 %collective-permute-done.10 = f32[1,8,64,64]{3,2,1,0:T(8,128)S(1)} collective-permute-done((f32[1,8,64,64]{3,2,1,0:T(8,128)S(1)}, f32[1,8,64,64]{3,2,1,0:T(8,128)S(1)}, u32[]{:S(2)}, u32[]{:S(2)}) %collective-permute-start.10) | collective-permute-done | bytes 131104 | tf_op jit(solution)/shard_map/ppermute | solution.py:15
  197.7 14.1 %collective-permute-done.9 = f32[1,8,64,64]{3,2,1,0:T(8,128)S(1)} collective-permute-done((f32[1,8,64,64]{3,2,1,0:T(8,128)S(1)}, f32[1,8,64,64]{3,2,1,0:T(8,128)S(1)}, u32[]{:S(2)}, u32[]{:S(2)}) %collective-permute-start.9) | collective-permute-done | bytes 131104 | tf_op jit(solution)/shard_map/ppermute | solution.py:15
  212.0 0.8 reshape.558
  (84 shorter events, 7.7 us)
Async XLA Ops:
  0.0 26.3 %collective-permute-start.6 = (bf16[1,8,4096]{2,1,0:T(8,128)(2,1)}, bf16[1,8,4096]{2,1,0:T(8,128)(2,1)S(1)}, u32[]{:S(2)}, u32[]{:S(2)}) collective-permute-start(bf16[1,8,4096]{2,1,0:T(8,128)(2,1)} %param.10), channel_id=1, source_target_pairs={{24,0},{32,8},{40,16},{48,24},{56,32},{64,40},{72,48},{80,56},{88,... | collective-permute-start | bytes 196616 | tf_op jit(solution)/shard_map/ppermute | solution.py:15
  14.7 11.5 %collective-permute-start.5 = (bf16[1,8,4096]{2,1,0:T(8,128)(2,1)}, bf16[1,8,4096]{2,1,0:T(8,128)(2,1)S(1)}, u32[]{:S(2)}, u32[]{:S(2)}) collective-permute-start(bf16[1,8,4096]{2,1,0:T(8,128)(2,1)} %param.10), channel_id=1, source_target_pairs={{16,0},{24,8},{32,16},{40,24},{48,32},{56,40},{64,48},{72,56},{80,... | collective-permute-start | bytes 196616 | tf_op jit(solution)/shard_map/ppermute | solution.py:15
  17.9 8.4 %collective-permute-start.4 = (bf16[1,8,4096]{2,1,0:T(8,128)(2,1)}, bf16[1,8,4096]{2,1,0:T(8,128)(2,1)S(1)}, u32[]{:S(2)}, u32[]{:S(2)}) collective-permute-start(bf16[1,8,4096]{2,1,0:T(8,128)(2,1)} %param.10), channel_id=1, source_target_pairs={{8,0},{16,8},{24,16},{32,24},{40,32},{48,40},{56,48},{64,56},{72,6... | collective-permute-start | bytes 196616 | tf_op jit(solution)/shard_map/ppermute | solution.py:15
  20.4 11.7 %collective-permute-start.7 = (bf16[1,8,4096]{2,1,0:T(8,128)(2,1)}, bf16[1,8,4096]{2,1,0:T(8,128)(2,1)S(1)}, u32[]{:S(2)}, u32[]{:S(2)}) collective-permute-start(bf16[1,8,4096]{2,1,0:T(8,128)(2,1)} %param.10), channel_id=1, source_target_pairs={{32,0},{40,8},{48,16},{56,24},{64,32},{72,40},{80,48},{88,56},{96,... | collective-permute-start | bytes 196616 | tf_op jit(solution)/shard_map/ppermute | solution.py:15
  33.9 5.9 %copy-start.4 = (s32[1,3]{1,0:T(1,128)S(1)}, s32[1,3]{1,0:T(1,128)}, u32[]{:S(2)}) copy-start(s32[1,3]{1,0:T(1,128)} %param.12) | copy-start | bytes 40
  33.9 19.8 %copy-start.2 = (bf16[1,8,4096]{2,1,0:T(8,128)(2,1)S(1)}, bf16[1,8,4096]{2,1,0:T(8,128)(2,1)}, u32[]{:S(2)}) copy-start(bf16[1,8,4096]{2,1,0:T(8,128)(2,1)} %param.10) | copy-start | bytes 196612
  33.9 20.0 %copy-start.7 = (s32[1,2]{1,0:T(1,128)S(1)}, s32[1,2]{1,0:T(1,128)}, u32[]{:S(2)}) copy-start(s32[1,2]{1,0:T(1,128)} %param.11) | copy-start | bytes 28
  33.9 37.7 %all-to-all-start = ((bf16[8,5,8,4096]{3,2,1,0:T(8,128)(2,1)}), bf16[8,5,8,4096]{3,2,1,0:T(8,128)(2,1)S(1)}, u32[]{:S(2)}, u32[]{:S(2)}) async-start(bf16[8,5,8,4096]{3,2,1,0:T(8,128)(2,1)} %broadcast_in_dim.33), calls=%async_computation | async-start | bytes 5242880 | tf_op jit(solution)/shard_map/all_to_all | solution.py:20
  39.8 30.1 %collective-permute-start.3 = (s32[1,3]{1,0:T(1,128)S(1)}, s32[1,3]{1,0:T(1,128)S(1)}, u32[]{:S(2)}, u32[]{:S(2)}) collective-permute-start(s32[1,3]{1,0:T(1,128)S(1)} %copy-done.4), channel_id=1, source_target_pairs={{32,0},{40,8},{48,16},{56,24},{64,32},{72,40},{80,48},{88,56},{96,... | collective-permute-start | bytes 44 | tf_op jit(solution)/shard_map/ppermute | solution.py:15
  46.2 23.7 %collective-permute-start.2 = (s32[1,3]{1,0:T(1,128)S(1)}, s32[1,3]{1,0:T(1,128)S(1)}, u32[]{:S(2)}, u32[]{:S(2)}) collective-permute-start(s32[1,3]{1,0:T(1,128)S(1)} %copy-done.4), channel_id=1, source_target_pairs={{24,0},{32,8},{40,16},{48,24},{56,32},{64,40},{72,48},{80,56},{88,... | collective-permute-start | bytes 44 | tf_op jit(solution)/shard_map/ppermute | solution.py:15
  48.2 21.8 %collective-permute-start.1 = (s32[1,3]{1,0:T(1,128)S(1)}, s32[1,3]{1,0:T(1,128)S(1)}, u32[]{:S(2)}, u32[]{:S(2)}) collective-permute-start(s32[1,3]{1,0:T(1,128)S(1)} %copy-done.4), channel_id=1, source_target_pairs={{16,0},{24,8},{32,16},{40,24},{48,32},{56,40},{64,48},{72,56},{80,... | collective-permute-start | bytes 44 | tf_op jit(solution)/shard_map/ppermute | solution.py:15
  50.5 19.5 %collective-permute-start = (s32[1,3]{1,0:T(1,128)S(1)}, s32[1,3]{1,0:T(1,128)S(1)}, u32[]{:S(2)}, u32[]{:S(2)}) collective-permute-start(s32[1,3]{1,0:T(1,128)S(1)} %copy-done.4), channel_id=1, source_target_pairs={{8,0},{16,8},{24,16},{32,24},{40,32},{48,40},{56,48},{64,56},{72,6... | collective-permute-start | bytes 44 | tf_op jit(solution)/shard_map/ppermute | solution.py:15
  91.2 7.5 %copy-start = (f32[128,16,128]{2,1,0:T(8,128)S(1)}, f32[128,16,128]{2,1,0:T(8,128)}, u32[]{:S(2)}) copy-start(f32[128,16,128]{2,1,0:T(8,128)} %param.13) | copy-start | bytes 3145732
  92.9 19.9 %all-to-all-start.1 = ((bf16[4,8,128,128]{3,1,0,2:T(8,128)(2,1)}), bf16[4,8,128,128]{3,1,0,2:T(8,128)(2,1)S(1)}, u32[]{:S(2)}, u32[]{:S(2)}) async-start(bf16[4,8,128,128]{3,1,0,2:T(8,128)(2,1)} %copy.73), calls=%async_computation.1 | async-start | bytes 2097152 | tf_op jit(solution)/shard_map/all_to_all | solution.py:42
  121.1 29.9 %all-to-all-start.2 = ((bf16[4,2,64,16,128]{4,3,1,0,2:T(8,128)(2,1)}), bf16[4,2,64,16,128]{4,3,1,0,2:T(8,128)(2,1)S(1)}, u32[]{:S(2)}, u32[]{:S(2)}) async-start(bf16[4,2,64,16,128]{4,3,1,0,2:T(8,128)(2,1)} %copy.81), calls=%async_computation.2 | async-start | bytes 4194304 | tf_op jit(solution)/shard_map/all_to_all | solution.py:42
  154.1 2.2 %copy-start.3 = (bf16[2,1,64,128]{3,2,1,0:T(8,128)(2,1)S(1)}, bf16[2,1,64,128]{3,2,1,0:T(8,128)(2,1)}, u32[]{:S(2)}) copy-start(bf16[2,1,64,128]{3,2,1,0:T(8,128)(2,1)} %get-tuple-element.25) | copy-start | bytes 98308
  156.3 2.1 copy-start.1
  156.3 2.1 copy-start.5
  156.3 2.1 copy-start.6
  158.3 0.7 copy-start.8
  164.2 24.4 %collective-permute-start.11 = (f32[1,8,64,64]{3,2,1,0:T(8,128)S(1)}, f32[1,8,64,64]{3,2,1,0:T(8,128)S(1)}, u32[]{:S(2)}, u32[]{:S(2)}) collective-permute-start(f32[1,8,64,64]{3,2,1,0:T(8,128)S(1)} %bitcast.270), channel_id=1, source_target_pairs={{480,0},{488,8},{496,16},{504,24},{0,32},{8,40},{16,48},{24,56},{3... | collective-permute-start | bytes 393224 | tf_op jit(solution)/shard_map/ppermute | solution.py:15
  166.2 31.5 %collective-permute-start.10 = (f32[1,8,64,64]{3,2,1,0:T(8,128)S(1)}, f32[1,8,64,64]{3,2,1,0:T(8,128)S(1)}, u32[]{:S(2)}, u32[]{:S(2)}) collective-permute-start(f32[1,8,64,64]{3,2,1,0:T(8,128)S(1)} %bitcast.269), channel_id=1, source_target_pairs={{488,0},{496,8},{504,16},{0,24},{8,32},{16,40},{24,48},{32,56},{40... | collective-permute-start | bytes 393224 | tf_op jit(solution)/shard_map/ppermute | solution.py:15
  168.1 43.7 %collective-permute-start.9 = (f32[1,8,64,64]{3,2,1,0:T(8,128)S(1)}, f32[1,8,64,64]{3,2,1,0:T(8,128)S(1)}, u32[]{:S(2)}, u32[]{:S(2)}) collective-permute-start(f32[1,8,64,64]{3,2,1,0:T(8,128)S(1)} %bitcast.268), channel_id=1, source_target_pairs={{496,0},{504,8},{0,16},{8,24},{16,32},{24,40},{32,48},{40,56},{48,... | collective-permute-start | bytes 393224 | tf_op jit(solution)/shard_map/ppermute | solution.py:15
  170.6 41.3 %collective-permute-start.8 = (f32[1,8,64,64]{3,2,1,0:T(8,128)S(1)}, f32[1,8,64,64]{3,2,1,0:T(8,128)S(1)}, u32[]{:S(2)}, u32[]{:S(2)}) collective-permute-start(f32[1,8,64,64]{3,2,1,0:T(8,128)S(1)} %bitcast.267), channel_id=1, source_target_pairs={{504,0},{0,8},{8,16},{16,24},{24,32},{32,40},{40,48},{48,56},{56,6... | collective-permute-start | bytes 393224 | tf_op jit(solution)/shard_map/ppermute | solution.py:15
where the time goes:
time: 214 us; the launch traced here: 213 us
  waiting for transfers between devices  85.8 us (40%)
  starting transfers between devices  63.3 us (30%)
  local copies, waits for them, and re-layouts  37.9 us (18%)
  matrix products  19.8 us (9%)
  other arithmetic  5.34 us (2%)
    ppermute x12, waiting for transfers between devices, passed_along(): return lax.ppermute(block, axis, route)  59.9 us
    ppermute x12, starting transfers between devices, passed_along(): return lax.ppermute(block, axis, route)  47.5 us
    all_to_all x2, waiting for transfers between devices, in_one_piece(): lax.all_to_all(both, axis, split_axis=split_dim, concat_axis=concat_dim,...  25.9 us
    dot_general x18, matrix products, product(): jnp.einsum(form, left_side, right_side, preferred_element_type=jnp.float32)  13.4 us
    all_to_all x2, starting transfers between devices, in_one_piece(): lax.all_to_all(both, axis, split_axis=split_dim, concat_axis=concat_dim,...  9.9 us
    another operation x1, local copies, waits for them, and re-layouts, per_device(): candidates.reshape(candidates.shape[0], box_edge, box_edge, box_edge)  8.38 us
    dot_general x5, matrix products, per_device(): jnp.einsum('po,prst->orst', weights, far_term, precision=lax.Precision.HI...  6.47 us
    all_to_all x1, starting transfers between devices, from_everyone(): return lax.all_to_all(copies, axis, split_axis=0, concat_axis=0, tiled=True)  5.89 us
  transfers between devices with their start and end apart: 15, of which 8 were waited for; matrix products, arithmetic and copies ran while one was open for 8% of the time, Pallas kernels for 0%

commit v1 on v0

v1 whole, which is shorter than its diff:
```python
import math

import jax
import jax.numpy as jnp
import numpy as np
from jax import lax
from jax.experimental import pallas as pl
from jax.experimental.pallas import tpu as pltpu
from jax.sharding import PartitionSpec as P

EDGE = 64
GRID = 128
HALF = 32
SLABS = 8
ROWS = EDGE // SLABS
WAVES = GRID // SLABS
PAIRS = 2
LANES = 128
FLAT = EDGE * EDGE // LANES
PAD = 24
SPAN = PAD + FLAT + PAD
F32 = jnp.float32
BF16 = jnp.bfloat16


def full_tables():
    index = np.arange(GRID)
    angle = (index[:, None] * index[None, :] % GRID) * (2.0 * np.pi / GRID)
    rounded = lambda a: a.astype(np.float32).astype(BF16)
    return rounded(np.cos(angle)), rounded(np.sin(angle))


COS, SIN = full_tables()
BOX = slice(HALF, HALF + EDGE)
SPLIT_CELLS = np.concatenate([np.arange(0, EDGE, 2), np.arange(1, EDGE, 2)]) + HALF


def forward_first():
    return np.concatenate([COS[:, SPLIT_CELLS], -SIN[:, SPLIT_CELLS]], axis=1)


def forward_depth():
    c, s = COS[BOX], SIN[BOX]
    return np.block([[c, -s], [s, c]])


def forward_rows():
    c, s = COS[:, BOX], SIN[:, BOX]
    return np.block([[c, s], [-s, c]])


def dot(a, b):
    return jnp.dot(a, b, preferred_element_type=F32)


def swapped(x):
    return pltpu.roll(x, EDGE, axis=1)


def low_half(shape):
    return lax.broadcasted_iota(jnp.int32, shape, 1) < EDGE


def moved(ref, row, d0, d1, d2):
    source = row - d0
    inside = jnp.logical_and(source >= 0, source < EDGE)
    source = jnp.clip(source, 0, EDGE - 1)
    flat = d1 * EDGE + d2
    turn = flat & (LANES - 1)
    jump = (flat - turn) // LANES
    here = pltpu.roll(ref[source, pl.ds(PAD - jump, FLAT), :], turn, axis=1)
    before = pltpu.roll(ref[source, pl.ds(PAD - jump - 1, FLAT), :], turn, axis=1)
    lane = lax.broadcasted_iota(jnp.int32, (FLAT, LANES), 1)
    depth = (lane & (EDGE - 1)) - d2
    keep = (depth >= 0) & (depth < EDGE) & inside
    return jnp.where(keep, jnp.where(lane >= turn, here, before), 0.0)


def unfold(box_of, target):
    flat_target = target.reshape(EDGE * SPAN, LANES)
    for t in range(SLABS):
        for k in range(FLAT):
            piece = box_of(t, k).astype(F32)
            flat_target[pl.ds(t * ROWS * SPAN + PAD + k, ROWS, stride=SPAN), :] = piece


def clear_edges(ref):
    zeros = jnp.zeros((EDGE, PAD, LANES), F32)
    ref[:, :PAD, :] = zeros
    ref[:, PAD + FLAT :, :] = zeros


def pair_kernel(
    scal,
    own_in,
    far_in,
    kern,
    cos_f,
    sin_f,
    first_t,
    depth_t,
    rows_t,
    send,
    here_out,
    there_out,
    own_s,
    far_s,
    zr,
    zi,
    back_s,
    row_tab,
    dep_tab,
):
    slab = scal[0]
    clear_edges(own_s)
    clear_edges(far_s)
    unfold(lambda t, k: own_in[t, :, k * LANES : (k + 1) * LANES], own_s)
    first = first_t[pl.ds(pl.multiple_of(slab * WAVES, WAVES), WAVES), :]
    first = jnp.concatenate([first[:, :EDGE], first[:, EDGE:]], axis=0)
    depth_m = depth_t[...]
    rows_m = rows_t[...]
    low_d = low_half((FLAT, LANES))
    low_w = low_half((WAVES, LANES))
    kern_flat = kern.reshape(GRID * WAVES, LANES)
    back_flat = back_s.reshape(2 * EDGE * WAVES, LANES)

    def tables_for(slot, d0, d2):
        c = cos_f[pl.ds(HALF + d0, EDGE), :].astype(BF16)
        s = sin_f[pl.ds(HALF + d0, EDGE), :].astype(BF16)
        base = slot * 2 * EDGE
        row_tab[base : base + EDGE, :GRID] = c
        row_tab[base : base + EDGE, GRID:] = -s
        row_tab[base + EDGE : base + 2 * EDGE, :GRID] = s
        row_tab[base + EDGE : base + 2 * EDGE, GRID:] = c
        turn = (GRID - HALF - d2) & (LANES - 1)
        low = low_half((GRID, LANES))
        c = pltpu.roll(cos_f[...], turn, axis=1)
        s = pltpu.roll(sin_f[...], turn, axis=1)
        dep_tab[slot, :GRID, :] = jnp.where(low, c, swapped(s)).astype(BF16)
        dep_tab[slot, GRID:, :] = jnp.where(low, -s, swapped(c)).astype(BF16)

    tables_for(0, 0, 0)
    for n in range(PAIRS):
        d0, d1, d2 = scal[1 + 3 * n], scal[2 + 3 * n], scal[3 + 3 * n]
        unfold(lambda t, k: far_in[t, n, :, k * LANES : (k + 1) * LANES], far_s)
        tables_for(1, d0, d2)

        def forward(step, carry):
            waves = []
            for half in range(2):
                a = step * 4 + half * 2
                dens_a = own_s[a, PAD : PAD + FLAT, :] * moved(far_s, a, d0, d1, d2)
                dens_b = own_s[a + 1, PAD : PAD + FLAT, :] * moved(far_s, a + 1, d0, d1, d2)
                even = jnp.where(low_d, dens_a, swapped(dens_b)).astype(BF16)
                odd = jnp.where(low_d, swapped(dens_a), dens_b).astype(BF16)
                y = dot(first, jnp.concatenate([even, odd], axis=0))
                re, im = y[:WAVES], y[WAVES:]
                waves.append(jnp.where(low_w, re, swapped(im)))
                waves.append(jnp.where(low_w, swapped(re), im))
            z = dot(jnp.concatenate(waves, axis=0).astype(BF16), depth_m)
            for q in range(4):
                block = z[q * WAVES : (q + 1) * WAVES]
                zr[pl.ds(step * 4 + q, WAVES, stride=EDGE), :] = block[:, :LANES]
                zi[pl.ds(step * 4 + q, WAVES, stride=EDGE), :] = block[:, LANES:]
            return carry

        lax.fori_loop(0, EDGE // 4, forward, 0)

        def middle(step, carry):
            def plane(w):
                at = pl.ds(pl.multiple_of(w * EDGE, EDGE), EDGE)
                return jnp.concatenate([zr[at, :], zi[at, :]], axis=0).astype(BF16)

            w0, w1 = step * 2, step * 2 + 1
            x = dot(rows_m, jnp.concatenate([plane(w0), plane(w1)], axis=1))
            scale = jnp.concatenate(
                [kern_flat[pl.ds(w0, GRID, stride=WAVES), :], kern_flat[pl.ds(w1, GRID, stride=WAVES), :]], axis=1
            )
            w = jnp.concatenate([x[:GRID] * scale, x[GRID:] * scale], axis=0).astype(BF16)
            v = dot(row_tab[...], w).astype(BF16)
            for m in range(2):
                re = v[2 * m * EDGE : (2 * m + 1) * EDGE]
                im = v[(2 * m + 1) * EDGE : (2 * m + 2) * EDGE]
                left = jnp.concatenate(
                    [
                        jnp.concatenate([re[:, :LANES], im[:, :LANES]], axis=1),
                        jnp.concatenate([re[:, LANES:], im[:, LANES:]], axis=1),
                    ],
                    axis=0,
                )
                r = dot(left, dep_tab[m])
                back_flat[pl.ds(m * EDGE * WAVES + w0, EDGE, stride=WAVES), :] = r[:EDGE]
                back_flat[pl.ds(m * EDGE * WAVES + w1, EDGE, stride=WAVES), :] = r[EDGE:]
            return carry

        lax.fori_loop(0, WAVES // 2, middle, 0)
        for m in range(2):
            for t in range(SLABS):
                send[t, n, m] = back_s[m * EDGE + t * ROWS : m * EDGE + (t + 1) * ROWS].astype(BF16)
        for r in range(ROWS):
            here_out[n, r] = moved(far_s, slab * ROWS + r, d0, d1, d2).astype(BF16)
            there_out[n, r] = moved(own_s, slab * ROWS + r, -d0, -d1, -d2).astype(BF16)


def pair_call(scal, own_box, far_box, kernel, interpret=False):
    vmem = pl.BlockSpec(memory_space=pltpu.VMEM)
    return pl.pallas_call(
        pair_kernel,
        out_shape=(
            jax.ShapeDtypeStruct((SLABS, PAIRS, 2, ROWS, WAVES, LANES), BF16),
            jax.ShapeDtypeStruct((PAIRS, ROWS, FLAT, LANES), BF16),
            jax.ShapeDtypeStruct((PAIRS, ROWS, FLAT, LANES), BF16),
        ),
        in_specs=[pl.BlockSpec(memory_space=pltpu.SMEM)] + [vmem] * 8,
        out_specs=(vmem, vmem, vmem),
        scratch_shapes=[
            pltpu.VMEM((EDGE, SPAN, LANES), F32),
            pltpu.VMEM((EDGE, SPAN, LANES), F32),
            pltpu.VMEM((WAVES * EDGE, LANES), F32),
            pltpu.VMEM((WAVES * EDGE, LANES), F32),
            pltpu.VMEM((2 * EDGE, WAVES, LANES), F32),
            pltpu.VMEM((4 * EDGE, 2 * GRID), BF16),
            pltpu.VMEM((2, 2 * GRID, LANES), BF16),
        ],
        interpret=interpret,
        name="pair_waves",
    )(
        scal,
        own_box,
        far_box,
        kernel,
        jnp.asarray(COS.astype(np.float32)),
        jnp.asarray(SIN.astype(np.float32)),
        jnp.asarray(forward_first()),
        jnp.asarray(forward_depth()),
        jnp.asarray(forward_rows()),
    )


def term_kernel(scal, got, here, there, cos_f, sin_f, own_out, odd_out, even_out, far_s):
    low = low_half((FLAT, LANES))
    scale = 1.0 / GRID**3

    def table(shift):
        parts = [ref[pl.ds(HALF + shift + par, FLAT, stride=2), :] for ref in (cos_f, sin_f) for par in range(2)]
        return jnp.concatenate(parts, axis=0).astype(BF16)

    def fields(n, m, tab, row):
        def column(r):
            return jnp.concatenate([got[t, n, m, r] for t in range(SLABS)], axis=0)

        g = dot(tab, jnp.concatenate([column(row), column(row + 1)], axis=1))
        out = []
        for side in range(2):
            part = g[:, side * LANES : (side + 1) * LANES]
            c0, c1, s0, s1 = (part[q * FLAT : (q + 1) * FLAT] for q in range(4))
            out.append(jnp.where(low, c0 - swapped(s0), swapped(c1) - s1) * scale)
        return out

    own_tab = table(0)
    far_tabs = [table(scal[1 + n]) for n in range(PAIRS)]
    for row in range(0, ROWS, 2):
        total = [jnp.zeros((FLAT, LANES), F32)] * 2
        for n in range(PAIRS):
            pots = fields(n, 0, own_tab, row)
            total = [total[q] + pots[q] * here[n, row + q].astype(F32) for q in range(2)]
            pots = fields(n, 1, far_tabs[n], row)
            for q in range(2):
                far_s[n, row + q] = pots[q] * there[n, row + q].astype(F32)
        for q in range(2):
            own_out[row + q] = total[q]
    hops = [scal[3 + n] for n in range(PAIRS)]
    for e in range(1, 5):
        target = odd_out if e % 2 else even_out
        for row in range(ROWS):
            value = sum(jnp.where(hops[n] == e, far_s[n, row], 0.0) for n in range(PAIRS))
            target[(e - 1) // 2, row] = value.astype(BF16)


def term_call(scal, got, here, there, interpret=False):
    vmem = pl.BlockSpec(memory_space=pltpu.VMEM)
    return pl.pallas_call(
        term_kernel,
        out_shape=(
            jax.ShapeDtypeStruct((ROWS, FLAT, LANES), F32),
            jax.ShapeDtypeStruct((2, ROWS, FLAT, LANES), BF16),
            jax.ShapeDtypeStruct((2, ROWS, FLAT, LANES), BF16),
        ),
        in_specs=[pl.BlockSpec(memory_space=pltpu.SMEM)] + [vmem] * 5,
        out_specs=(vmem, vmem, vmem),
        scratch_shapes=[pltpu.VMEM((PAIRS, ROWS, FLAT, LANES), F32)],
        interpret=interpret,
        name="pair_terms",
    )(scal, got, here, there, jnp.asarray(COS.astype(np.float32)), jnp.asarray(SIN.astype(np.float32)))


def passed_along(block, distance):
    count = lax.axis_size("orb")
    return lax.ppermute(block, "orb", [((i - distance) % count, i) for i in range(count)])


def other_core(block):
    count = lax.axis_size("orb")
    return lax.ppermute(block, "orb", [(i ^ 1, i) for i in range(count)])


def to_everyone(shard):
    copies = jnp.broadcast_to(shard, (lax.axis_size("slab"), *shard.shape))
    return lax.all_to_all(copies, "slab", split_axis=0, concat_axis=0, tiled=True)


def per_device(orbitals, partners, offsets, kernel):
    orbit = lax.axis_index("orb")
    slab = lax.axis_index("slab")
    even_core = orbit % 2 == 0
    cells = EDGE * EDGE
    own = orbitals[0]
    corner = jnp.pad(offsets.astype(BF16), ((0, 0), (0, LANES - 3)))
    loaded = jnp.concatenate([own, jnp.broadcast_to(corner, (ROWS, LANES))], axis=1)
    four = passed_along(loaded, -4)
    two = passed_along(loaded, -2)
    own_box = to_everyone(own)
    given = jnp.stack([jnp.where(even_core, two, loaded), jnp.where(even_core, four, two)])
    odd = other_core(given)
    hops = (partners[0] - orbit) % lax.axis_size("orb")

    def chosen(hop):
        low = jnp.where(hop == 1, odd[0], two)
        high = jnp.where(hop == 3, odd[1], four)
        return jnp.where(hop <= 2, low, high)

    picked = jnp.stack([chosen(hops[n]) for n in range(PAIRS)])
    shifts = picked[:, 0, cells : cells + 3].astype(jnp.int32) - offsets
    far_box = to_everyone(picked[:, :, :cells])
    scal = jnp.concatenate([slab[None].astype(jnp.int32), shifts.reshape(-1)])
    send, here, there = pair_call(scal, own_box, far_box, kernel)
    got = lax.all_to_all(send, "slab", split_axis=0, concat_axis=0, tiled=True)
    scal = jnp.concatenate([jnp.zeros((1,), jnp.int32), shifts[:, 1], hops])
    mine, odd_out, even_out = term_call(scal, got, here, there)
    crossed = other_core(odd_out).astype(F32)
    by_two = even_out[0].astype(F32) + jnp.where(even_core, crossed[0], crossed[1])
    by_four = even_out[1].astype(F32) + jnp.where(even_core, crossed[1], 0.0)
    four_back = passed_along(by_four.astype(BF16), 4).astype(F32)
    two_back = passed_along(by_two.astype(BF16), 2).astype(F32)
    total = mine + jnp.where(even_core, 0.0, crossed[0]) + two_back + four_back
    return total.reshape(1, ROWS, cells)


def solution(mesh):
    return jax.shard_map(
        per_device,
        mesh=mesh,
        in_specs=(P("orb", "slab", None), P("orb", None), P("orb", None), P(None, "slab", None)),
        out_specs=P("orb", "slab", None),
        check_vma=False,
    )
```

time: 214 us -> 129 us (0.60)
  the two profiles are of different devices: /device:TPU:8 before, /device:TPU:16 now
where the time goes in v1:
time: 129 us
  waiting for transfers between devices  41.8 us (32%)
  starting transfers between devices  39.9 us (31%)
  Pallas kernels  32.3 us (25%)
  local copies, waits for them, and re-layouts  6.83 us (5%)
  between operations  4.05 us (3%)
  other arithmetic  3.81 us (3%)
    pallas_call x1, Pallas kernels, pair_call(): pl.pallas_call(pair_kernel, out_shape=(jax.ShapeDtypeStruct((SLABS, PAIRS...  29.7 us
    ppermute x4, starting transfers between devices, passed_along(): lax.ppermute(block, 'orb', [((i - distance) % count, i) for i in range(co...  24.3 us
    all_to_all x2, waiting for transfers between devices, to_everyone(): lax.all_to_all(copies, 'slab', split_axis=0, concat_axis=0, tiled=True)  14.9 us
    all_to_all x1, waiting for transfers between devices, per_device(): got = lax.all_to_all(send, 'slab', split_axis=0, concat_axis=0, tiled=True)  14.1 us
    ppermute x4, waiting for transfers between devices, passed_along(): lax.ppermute(block, 'orb', [((i - distance) % count, i) for i in range(co...  11.3 us
    all_to_all x2, starting transfers between devices, to_everyone(): lax.all_to_all(copies, 'slab', split_axis=0, concat_axis=0, tiled=True)  7.97 us
    ppermute x2, starting transfers between devices, other_core(): return lax.ppermute(block, 'orb', [(i ^ 1, i) for i in range(count)])  3.96 us
    all_to_all x1, starting transfers between devices, per_device(): got = lax.all_to_all(send, 'slab', split_axis=0, concat_axis=0, tiled=True)  3.64 us
  transfers between devices with their start and end apart: 9, of which 6 were waited for; matrix products, arithmetic and copies ran while one was open for 3% of the time, Pallas kernels for 0%

profile of v1, /device:TPU:16, one launch (start us, length us, event | category | flops | bytes accessed | tf_op | source)
XLA Modules:
  0.0 128.7 jit_solution(15637461054366488819)
XLA Ops:
  0.0 0.7 convert_element_type.46
  0.7 0.0 copy-start.3
  0.7 0.9 pad_maximum_fusion.2
  1.6 14.4 %collective-permute-start.1 = (bf16[8,4224]{1,0:T(8,128)(2,1)S(1)}, bf16[8,4224]{1,0:T(8,128)(2,1)S(1)}, u32[]{:S(2)}, u32[]{:S(2)}) collective-permute-start(bf16[8,4224]{1,0:T(8,128)(2,1)S(1)} %pad_maximum_fusion.2), channel_id=1, source_target_pairs={{32,0},{40,8},{48,16},{56,24},{64,32},{72,40},{80,48},{88,56},{96,... | collective-permute-start | bytes 202760 | tf_op jit(solution)/shard_map/ppermute | solution.py:299
  16.0 4.0 %collective-permute-start = (bf16[8,4224]{1,0:T(8,128)(2,1)S(1)}, bf16[8,4224]{1,0:T(8,128)(2,1)S(1)}, u32[]{:S(2)}, u32[]{:S(2)}) collective-permute-start(bf16[8,4224]{1,0:T(8,128)(2,1)S(1)} %pad_maximum_fusion.2), channel_id=1, source_target_pairs={{16,0},{24,8},{32,16},{40,24},{48,32},{56,40},{64,48},{72,56},{80,... | collective-permute-start | bytes 202760 | tf_op jit(solution)/shard_map/ppermute | solution.py:299
  20.1 0.0 copy-done.3
  20.1 0.8 broadcast_in_dim.25
  20.9 4.4 %all-to-all-start = ((bf16[8,8,4096]{2,1,0:T(8,128)(2,1)}), bf16[8,8,4096]{2,1,0:T(8,128)(2,1)S(1)}, u32[]{:S(2)}, u32[]{:S(2)}) async-start(bf16[8,8,4096]{2,1,0:T(8,128)(2,1)} %broadcast_in_dim.25), calls=%async_computation | async-start | bytes 1048576 | tf_op jit(solution)/shard_map/all_to_all | solution.py:309
  25.3 0.0 collective-permute-done.1
  25.4 0.0 collective-permute-done
  25.4 0.0 copy-start.7
  25.5 1.9 %collective-permute-start.2 = (bf16[2,8,4224]{2,1,0:T(8,128)(2,1)S(1)}, bf16[2,8,4224]{2,1,0:T(8,128)(2,1)S(1)}, u32[]{:S(2)}, u32[]{:S(2)}) collective-permute-start(bf16[2,8,4224]{2,1,0:T(8,128)(2,1)S(1)} %pad_maximum_fusion), channel_id=1, source_target_pairs={{8,0},{0,8},{24,16},{16,24},{40,32},{32,40},{56,48},{48,56},{72,64... | collective-permute-start | bytes 405512 | tf_op jit(solution)/shard_map/ppermute | solution.py:304
  27.4 0.0 copy-done.7
  27.4 0.6 fusion.6
  31.9 0.0 collective-permute-done.2
  31.9 2.5 %all-to-all-done.own_in = bf16[8,8,4096]{2,1,0:T(8,128)(2,1)S(1)} async-done(((bf16[8,8,4096]{2,1,0:T(8,128)(2,1)}), bf16[8,8,4096]{2,1,0:T(8,128)(2,1)S(1)}, u32[]{:S(2)}, u32[]{:S(2)}) %all-to-all-start) | async-done | bytes 524320 | tf_op jit(solution)/shard_map/all_to_all | solution.py:309
  34.5 0.0 copy-start.2
  34.5 1.2 broadcast_in_dim.26
  35.6 0.0 copy-done.2
  35.6 3.6 %all-to-all-start.1 = ((bf16[8,2,8,4096]{3,2,1,0:T(8,128)(2,1)}), bf16[8,2,8,4096]{3,2,1,0:T(8,128)(2,1)S(1)}, u32[]{:S(2)}, u32[]{:S(2)}) async-start(bf16[8,2,8,4096]{3,2,1,0:T(8,128)(2,1)} %broadcast_in_dim.26), calls=%async_computation.1 | async-start | bytes 2097152 | tf_op jit(solution)/shard_map/all_to_all | solution.py:309
  39.2 0.0 copy-start.6
  39.2 0.6 copy-done.6
  39.9 0.1 sub.30
  40.0 0.5 broadcast.27
  40.5 0.7 fusion.5
  41.1 0.1 reshape.40
  41.2 0.7 pad_add_fusion.1.scal
  41.9 12.4 %all-to-all-done.1.far_in = bf16[8,2,8,4096]{3,2,1,0:T(8,128)(2,1)S(1)} async-done(((bf16[8,2,8,4096]{3,2,1,0:T(8,128)(2,1)}), bf16[8,2,8,4096]{3,2,1,0:T(8,128)(2,1)S(1)}, u32[]{:S(2)}, u32[]{:S(2)}) %all-to-all-start.1) | async-done | bytes 1048608 | tf_op jit(solution)/shard_map/all_to_all | solution.py:309
  54.3 0.0 copy-start
  54.3 1.0 copy-done
  55.3 29.7 %pair_waves.1 = (bf16[8,2,2,8,16,128]{5,4,3,2,1,0:T(8,128)(2,1)}, bf16[2,8,32,128]{3,2,1,0:T(8,128)(2,1)}, bf16[2,8,32,128]{3,2,1,0:T(8,128)(2,1)}) custom-call(s32[7]{0:T(128)} %pad_add_fusion.1.scal, bf16[8,8,4096]{2,1,0:T(8,128)(2,1)} %copy-done.2, bf16[8,2,8,4096]{3,2,1,0:T(8,128)(2,1)} %copy-done, f32[128,16,128]{2,1,0:T(8,128)} %kern.1, ...), custom_call_target="tpu_custom_call" | custom-call | tf_op jit(solution)/shard_map/pair_waves/pallas_call | solution.py:207
  85.0 3.6 %all-to-all-start.2 = ((bf16[8,2,2,8,16,128]{5,4,3,2,1,0:T(8,128)(2,1)}), bf16[8,2,2,8,16,128]{5,4,3,2,1,0:T(8,128)(2,1)S(1)}, u32[]{:S(2)}, u32[]{:S(2)}) async-start(bf16[8,2,2,8,16,128]{5,4,3,2,1,0:T(8,128)(2,1)} %get-tuple-element.11), calls=%async_computation.2 | async-start | bytes 2097152 | tf_op jit(solution)/shard_map/all_to_all | solution.py:337
  88.6 0.2 slice_reduce_fusion
  88.8 0.7 pad_add_fusion.scal
  89.5 14.1 %all-to-all-done.2.got = bf16[8,2,2,8,16,128]{5,4,3,2,1,0:T(8,128)(2,1)S(1)} async-done(((bf16[8,2,2,8,16,128]{5,4,3,2,1,0:T(8,128)(2,1)}), bf16[8,2,2,8,16,128]{5,4,3,2,1,0:T(8,128)(2,1)S(1)}, u32[]{:S(2)}, u32[]{:S(2)}) %all-to-all-start.2) | async-done | bytes 1048608 | tf_op jit(solution)/shard_map/all_to_all | solution.py:337
  103.6 0.0 copy-start.1
  103.6 1.0 copy-done.1
  104.6 2.7 %pair_terms.1 = (f32[8,32,128]{2,1,0:T(8,128)}, bf16[2,8,32,128]{3,2,1,0:T(8,128)(2,1)}, bf16[2,8,32,128]{3,2,1,0:T(8,128)(2,1)}) custom-call(s32[5]{0:T(128)} %pad_add_fusion.scal, bf16[8,2,2,8,16,128]{5,4,3,2,1,0:T(8,128)(2,1)} %copy-done.1, bf16[2,8,32,128]{3,2,1,0:T(8,128)(2,1)} %get-tuple-element.12.here, ...), custom_call_target="tpu_custom_call" | custom-call | tf_op jit(solution)/shard_map/pair_terms/pallas_call | solution.py:282
  107.2 0.0 copy-start.5
  107.2 2.0 %collective-permute-start.3 = (bf16[2,8,32,128]{3,2,1,0:T(8,128)(2,1)}, bf16[2,8,32,128]{3,2,1,0:T(8,128)(2,1)S(1)}, u32[]{:S(2)}, u32[]{:S(2)}) collective-permute-start(bf16[2,8,32,128]{3,2,1,0:T(8,128)(2,1)} %get-tuple-element.15), channel_id=1, source_target_pairs={{8,0},{0,8},{24,16},{16,24},{40,32},{32,40},{56,48},{48,56},{72,64... | collective-permute-start | bytes 393224 | tf_op jit(solution)/shard_map/ppermute | solution.py:304
  109.3 1.5 %collective-permute-done.3 = bf16[2,8,32,128]{3,2,1,0:T(8,128)(2,1)S(1)} collective-permute-done((bf16[2,8,32,128]{3,2,1,0:T(8,128)(2,1)}, bf16[2,8,32,128]{3,2,1,0:T(8,128)(2,1)S(1)}, u32[]{:S(2)}, u32[]{:S(2)}) %collective-permute-start.3) | collective-permute-done | bytes 131104 | tf_op jit(solution)/shard_map/ppermute | solution.py:304
  110.8 0.0 copy-done.5
  110.8 0.0 copy-start.4
  110.9 3.9 %collective-permute-start.4 = (bf16[8,32,128]{2,1,0:T(8,128)(2,1)S(1)}, bf16[8,32,128]{2,1,0:T(8,128)(2,1)S(1)}, u32[]{:S(2)}, u32[]{:S(2)}) collective-permute-start(bf16[8,32,128]{2,1,0:T(8,128)(2,1)S(1)} %get-tuple-element.19), channel_id=1, source_target_pairs={{496,0},{504,8},{0,16},{8,24},{16,32},{24,40},{32,48},{40,56},{48,... | collective-permute-start | bytes 196616 | tf_op jit(solution)/shard_map/ppermute | solution.py:299
  114.8 1.9 %collective-permute-start.5 = (bf16[8,32,128]{2,1,0:T(8,128)(2,1)S(1)}, bf16[8,32,128]{2,1,0:T(8,128)(2,1)S(1)}, u32[]{:S(2)}, u32[]{:S(2)}) collective-permute-start(bf16[8,32,128]{2,1,0:T(8,128)(2,1)S(1)} %get-tuple-element.20), channel_id=1, source_target_pairs={{480,0},{488,8},{496,16},{504,24},{0,32},{8,40},{16,48},{24,56},{3... | collective-permute-start | bytes 196616 | tf_op jit(solution)/shard_map/ppermute | solution.py:299
  116.7 1.9 %collective-permute-done.4 = bf16[8,32,128]{2,1,0:T(8,128)(2,1)S(1)} collective-permute-done((bf16[8,32,128]{2,1,0:T(8,128)(2,1)S(1)}, bf16[8,32,128]{2,1,0:T(8,128)(2,1)S(1)}, u32[]{:S(2)}, u32[]{:S(2)}) %collective-permute-start.4) | collective-permute-done | bytes 65568 | tf_op jit(solution)/shard_map/ppermute | solution.py:299
  118.6 9.4 %collective-permute-done.5 = bf16[8,32,128]{2,1,0:T(8,128)(2,1)S(1)} collective-permute-done((bf16[8,32,128]{2,1,0:T(8,128)(2,1)S(1)}, bf16[8,32,128]{2,1,0:T(8,128)(2,1)S(1)}, u32[]{:S(2)}, u32[]{:S(2)}) %collective-permute-start.5) | collective-permute-done | bytes 65568 | tf_op jit(solution)/shard_map/ppermute | solution.py:299
  128.0 0.0 copy-done.4
  128.0 0.7 reshape.38
  (13 shorter events, 0.2 us)
Async XLA Ops:
  0.7 19.4 %copy-start.3 = (bf16[1,8,4096]{2,1,0:T(8,128)(2,1)S(1)}, bf16[1,8,4096]{2,1,0:T(8,128)(2,1)}, u32[]{:S(2)}) copy-start(bf16[1,8,4096]{2,1,0:T(8,128)(2,1)} %param.11) | copy-start | bytes 196612
  1.6 23.7 %collective-permute-start.1 = (bf16[8,4224]{1,0:T(8,128)(2,1)S(1)}, bf16[8,4224]{1,0:T(8,128)(2,1)S(1)}, u32[]{:S(2)}, u32[]{:S(2)}) collective-permute-start(bf16[8,4224]{1,0:T(8,128)(2,1)S(1)} %pad_maximum_fusion.2), channel_id=1, source_target_pairs={{32,0},{40,8},{48,16},{56,24},{64,32},{72,40},{80,48},{88,56},{96,... | collective-permute-start | bytes 202760 | tf_op jit(solution)/shard_map/ppermute | solution.py:299
  16.0 9.3 %collective-permute-start = (bf16[8,4224]{1,0:T(8,128)(2,1)S(1)}, bf16[8,4224]{1,0:T(8,128)(2,1)S(1)}, u32[]{:S(2)}, u32[]{:S(2)}) collective-permute-start(bf16[8,4224]{1,0:T(8,128)(2,1)S(1)} %pad_maximum_fusion.2), channel_id=1, source_target_pairs={{16,0},{24,8},{32,16},{40,24},{48,32},{56,40},{64,48},{72,56},{80,... | collective-permute-start | bytes 202760 | tf_op jit(solution)/shard_map/ppermute | solution.py:299
  20.9 13.5 %all-to-all-start = ((bf16[8,8,4096]{2,1,0:T(8,128)(2,1)}), bf16[8,8,4096]{2,1,0:T(8,128)(2,1)S(1)}, u32[]{:S(2)}, u32[]{:S(2)}) async-start(bf16[8,8,4096]{2,1,0:T(8,128)(2,1)} %broadcast_in_dim.25), calls=%async_computation | async-start | bytes 1048576 | tf_op jit(solution)/shard_map/all_to_all | solution.py:309
  25.4 2.0 %copy-start.7 = (s32[1,2]{1,0:T(1,128)S(1)}, s32[1,2]{1,0:T(1,128)}, u32[]{:S(2)}) copy-start(s32[1,2]{1,0:T(1,128)} %param.12) | copy-start | bytes 28
  25.5 6.4 %collective-permute-start.2 = (bf16[2,8,4224]{2,1,0:T(8,128)(2,1)S(1)}, bf16[2,8,4224]{2,1,0:T(8,128)(2,1)S(1)}, u32[]{:S(2)}, u32[]{:S(2)}) collective-permute-start(bf16[2,8,4224]{2,1,0:T(8,128)(2,1)S(1)} %pad_maximum_fusion), channel_id=1, source_target_pairs={{8,0},{0,8},{24,16},{16,24},{40,32},{32,40},{56,48},{48,56},{72,64... | collective-permute-start | bytes 405512 | tf_op jit(solution)/shard_map/ppermute | solution.py:304
  34.5 1.2 copy-start.2
  35.6 18.6 %all-to-all-start.1 = ((bf16[8,2,8,4096]{3,2,1,0:T(8,128)(2,1)}), bf16[8,2,8,4096]{3,2,1,0:T(8,128)(2,1)S(1)}, u32[]{:S(2)}, u32[]{:S(2)}) async-start(bf16[8,2,8,4096]{3,2,1,0:T(8,128)(2,1)} %broadcast_in_dim.26), calls=%async_computation.1 | async-start | bytes 2097152 | tf_op jit(solution)/shard_map/all_to_all | solution.py:309
  39.2 0.7 copy-start.6
  54.3 1.0 copy-start
  85.0 18.6 %all-to-all-start.2 = ((bf16[8,2,2,8,16,128]{5,4,3,2,1,0:T(8,128)(2,1)}), bf16[8,2,2,8,16,128]{5,4,3,2,1,0:T(8,128)(2,1)S(1)}, u32[]{:S(2)}, u32[]{:S(2)}) async-start(bf16[8,2,2,8,16,128]{5,4,3,2,1,0:T(8,128)(2,1)} %get-tuple-element.11), calls=%async_computation.2 | async-start | bytes 2097152 | tf_op jit(solution)/shard_map/all_to_all | solution.py:337
  103.6 1.0 copy-start.1
  107.2 3.6 %copy-start.5 = (bf16[2,8,32,128]{3,2,1,0:T(8,128)(2,1)S(1)}, bf16[2,8,32,128]{3,2,1,0:T(8,128)(2,1)}, u32[]{:S(2)}) copy-start(bf16[2,8,32,128]{3,2,1,0:T(8,128)(2,1)} %get-tuple-element.16) | copy-start | bytes 393220
  107.2 3.6 %collective-permute-start.3 = (bf16[2,8,32,128]{3,2,1,0:T(8,128)(2,1)}, bf16[2,8,32,128]{3,2,1,0:T(8,128)(2,1)S(1)}, u32[]{:S(2)}, u32[]{:S(2)}) collective-permute-start(bf16[2,8,32,128]{3,2,1,0:T(8,128)(2,1)} %get-tuple-element.15), channel_id=1, source_target_pairs={{8,0},{0,8},{24,16},{16,24},{40,32},{32,40},{56,48},{48,56},{72,64... | collective-permute-start | bytes 393224 | tf_op jit(solution)/shard_map/ppermute | solution.py:304
  110.8 17.2 %copy-start.4 = (f32[8,32,128]{2,1,0:T(8,128)S(1)}, f32[8,32,128]{2,1,0:T(8,128)}, u32[]{:S(2)}) copy-start(f32[8,32,128]{2,1,0:T(8,128)} %get-tuple-element.14) | copy-start | bytes 393220
  110.9 7.7 %collective-permute-start.4 = (bf16[8,32,128]{2,1,0:T(8,128)(2,1)S(1)}, bf16[8,32,128]{2,1,0:T(8,128)(2,1)S(1)}, u32[]{:S(2)}, u32[]{:S(2)}) collective-permute-start(bf16[8,32,128]{2,1,0:T(8,128)(2,1)S(1)} %get-tuple-element.19), channel_id=1, source_target_pairs={{496,0},{504,8},{0,16},{8,24},{16,32},{24,40},{32,48},{40,56},{48,... | collective-permute-start | bytes 196616 | tf_op jit(solution)/shard_map/ppermute | solution.py:299
  114.8 13.2 %collective-permute-start.5 = (bf16[8,32,128]{2,1,0:T(8,128)(2,1)S(1)}, bf16[8,32,128]{2,1,0:T(8,128)(2,1)S(1)}, u32[]{:S(2)}, u32[]{:S(2)}) collective-permute-start(bf16[8,32,128]{2,1,0:T(8,128)(2,1)S(1)} %get-tuple-element.20), channel_id=1, source_target_pairs={{480,0},{488,8},{496,16},{504,24},{0,32},{8,40},{16,48},{24,56},{3... | collective-permute-start | bytes 196616 | tf_op jit(solution)/shard_map/ppermute | solution.py:299

commit v2 on v1

v2 whole, which is shorter than its diff:
```python
import math

import jax
import jax.numpy as jnp
import numpy as np
from jax import lax
from jax.experimental import pallas as pl
from jax.experimental.pallas import tpu as pltpu
from jax.sharding import PartitionSpec as P

EDGE = 64
GRID = 128
HALF = 32
SLABS = 8
ROWS = EDGE // SLABS
WAVES = GRID // SLABS
PAIRS = 2
LANES = 128
FLAT = EDGE * EDGE // LANES
PAD = 24
SPAN = PAD + FLAT + PAD + 1
SLOTS = 8
ZSPAN = EDGE + 1
BSPAN = 2 * SLOTS + 1
ROOM = HALF + EDGE + HALF
F32 = jnp.float32
BF16 = jnp.bfloat16


def full_tables():
    index = np.arange(GRID)
    angle = (index[:, None] * index[None, :] % GRID) * (2.0 * np.pi / GRID)
    rounded = lambda a: a.astype(np.float32).astype(BF16).astype(np.float32)
    return rounded(np.cos(angle)), rounded(np.sin(angle))


COS, SIN = full_tables()
SIGN = COS[:, EDGE]
BOX = slice(HALF, HALF + EDGE)
SPLIT_CELLS = np.concatenate([np.arange(0, EDGE, 2), np.arange(1, EDGE, 2)]) + HALF
OWN_WAVES = np.array([[16 * (q // 2) + 2 * s + q % 2 for q in range(SLOTS)] for s in range(SLABS)])


def forward_first():
    re = COS[:, SPLIT_CELLS]
    im = -SIN[:, SPLIT_CELLS]
    im[0] = SIGN[SPLIT_CELLS]
    return np.concatenate([re[OWN_WAVES], im[OWN_WAVES]], axis=1).astype(BF16)


def backward_last():
    c, s = COS.copy(), SIN.copy()
    s[:, 0] = -SIGN
    out = []
    for m in range(2):
        for table in (c, s):
            wide = np.zeros((GRID, SLABS, 2, SLOTS), np.float32)
            wide[:, :, m] = table[:, OWN_WAVES]
            out.append(wide.reshape(GRID, GRID))
    return np.concatenate(out)


def forward_depth():
    c, s = COS[BOX], SIN[BOX]
    return np.block([[c, -s], [s, c]]).astype(BF16)


def forward_rows():
    c, s = COS[:, BOX], SIN[:, BOX]
    return np.block([[c, s], [-s, c]]).astype(BF16)


def reversal():
    flip = np.zeros((GRID, GRID), np.float32)
    flip[np.arange(GRID), -np.arange(GRID) % GRID] = 1.0
    return flip.astype(BF16)


def dot(a, b):
    return jnp.dot(a, b, preferred_element_type=F32)


def swapped(x):
    return pltpu.roll(x, EDGE, axis=1)


def lanes_of(shape):
    return lax.broadcasted_iota(jnp.int32, shape, 1)


def low_half(shape):
    return lanes_of(shape) < EDGE


def in_depth(lane, d2):
    depth = (lane & (EDGE - 1)) - d2
    return (depth >= 0) & (depth < EDGE)


def offer_kernel(slab_ref, own, kern, send):
    slab = slab_ref[0]
    kern_flat = kern.reshape(GRID * WAVES, LANES)
    mine = [jnp.concatenate([own[:, (k + h) * LANES : (k + h + 1) * LANES] for h in range(2)], axis=0) for k in range(0, FLAT, 2)]
    mine = jnp.concatenate(mine, axis=0)
    for t in range(SLABS):
        for j in range(2):
            high = (WAVES - 2 * t) % WAVES if j == 0 else WAVES - 1 - 2 * t
            at = jnp.where(slab < SLABS // 2, 2 * t + j, high)
            send[t, j * GRID : (j + 1) * GRID, :] = kern_flat[pl.ds(at, GRID, stride=WAVES), :].astype(BF16)
        send[t, 2 * GRID :, :] = mine


def moved(ref, row, d0, d1, d2):
    source = row - d0
    inside = jnp.logical_and(source >= 0, source < EDGE)
    base = jnp.clip(source, 0, EDGE - 1) * SPAN + PAD
    flat = d1 * EDGE + d2
    turn = flat & (LANES - 1)
    jump = (flat - turn) // LANES
    here = pltpu.roll(ref[pl.ds(base - jump, FLAT), :], turn, axis=1)
    before = pltpu.roll(ref[pl.ds(base - jump - 1, FLAT), :], turn, axis=1)
    lane = lanes_of((FLAT, LANES))
    return jnp.where(in_depth(lane, d2) & inside, jnp.where(lane >= turn, here, before), 0.0)


def prepare_kernel(scal, got, flip_t, cos_f, sin_f, own_out, scale_out, there_out, row_out, dep_out, own_s):
    slab = scal[0]
    zeros = jnp.zeros((PAD + 1, LANES), F32)
    for c in range(EDGE):
        own_s[c * SPAN : c * SPAN + PAD, :] = zeros[:PAD]
        own_s[c * SPAN + PAD + FLAT : (c + 1) * SPAN, :] = zeros
    for t in range(SLABS):
        for k in range(FLAT):
            at = 2 * GRID + k * ROWS
            own_s[pl.ds(t * ROWS * SPAN + PAD + k, ROWS, stride=SPAN), :] = got[t, at : at + ROWS, :].astype(F32)
    for c in range(EDGE):
        own_out[c * FLAT : (c + 1) * FLAT, :] = own_s[c * SPAN + PAD : c * SPAN + PAD + FLAT, :].astype(BF16)
    flip = flip_t[...]

    def reversed_plane(plane):
        return dot(dot(flip, plane).astype(BF16), flip)

    first = slab == 0
    for t in range(SLABS // 2):
        for j in range(2):
            here = got[t, j * GRID : (j + 1) * GRID, :]
            if j:
                there = got[SLABS - 1 - t, GRID : 2 * GRID, :]
            else:
                there = got[jnp.where(first, (SLABS - t) % SLABS, SLABS - 1 - t), :GRID, :]
            both = here.astype(F32) + reversed_plane(there)
            if t + j:
                scale_out[2 * t + j] = both
            else:
                top = got[SLABS // 2, :GRID, :]
                top = top.astype(F32) + reversed_plane(top)
                scale_out[0] = jnp.where(first, 0.25 * (both + top), both)
                scale_out[SLOTS] = jnp.where(first, 0.25 * (both - top), 0.0)
    for n in range(PAIRS):
        d0, d1, d2 = scal[1 + 3 * n], scal[2 + 3 * n], scal[3 + 3 * n]
        for r in range(ROWS):
            there_out[n, r] = moved(own_s, slab * ROWS + r, -d0, -d1, -d2).astype(BF16)
    for n in range(PAIRS):
        for m in range(2):
            d0 = scal[1 + 3 * n] * m
            d2 = scal[3 + 3 * n] * m
            c = cos_f[pl.ds(HALF + d0, EDGE), :].astype(BF16)
            s = sin_f[pl.ds(HALF + d0, EDGE), :].astype(BF16)
            base = m * 2 * EDGE
            row_out[n, base : base + EDGE, :GRID] = c
            row_out[n, base : base + EDGE, GRID:] = -s
            row_out[n, base + EDGE : base + 2 * EDGE, :GRID] = s
            row_out[n, base + EDGE : base + 2 * EDGE, GRID:] = c
            turn = (GRID - HALF - d2) & (LANES - 1)
            low = low_half((GRID, LANES))
            c = pltpu.roll(cos_f[...], turn, axis=1)
            s = pltpu.roll(sin_f[...], turn, axis=1)
            dep_out[n, m, :GRID, :] = jnp.where(low, c, swapped(s)).astype(BF16)
            dep_out[n, m, GRID:, :] = jnp.where(low, -s, swapped(c)).astype(BF16)


def pair_kernel(scal, own_s, far_in, scale_t, row_t, dep_t, first_t, depth_t, rows_t, flip_t, send, here_out, far_s, zr, zi, back_s):
    slab = scal[0]
    first = first_t[slab]
    depth_m = depth_t[...]
    rows_m = rows_t[...]
    flip = flip_t[...]
    low_d = low_half((FLAT, LANES))
    low_w = low_half((SLOTS, LANES))
    lane_d = lanes_of((FLAT, LANES))
    lane_r = lanes_of((ROWS, LANES))
    blank = jnp.zeros((FLAT + 8, LANES), F32)
    for n in range(PAIRS):
        d0, d1, d2 = scal[1 + 3 * n], scal[2 + 3 * n], scal[3 + 3 * n]
        flat = d1 * EDGE + d2
        turn = flat & (LANES - 1)
        jump = (flat - turn) // LANES

        def clear(c, carry):
            far_s[pl.ds((HALF + c) * SPAN + PAD - 8, FLAT + 8), :] = blank
            return carry

        lax.fori_loop(0, EDGE, clear, 0, unroll=8)
        keep = in_depth(lane_r, d2)
        for t in range(SLABS):
            start = (HALF + t * ROWS + d0) * SPAN + PAD + jump
            for k in range(FLAT):
                piece = far_in[t, n, :, k * LANES : (k + 1) * LANES].astype(F32)
                piece = jnp.where(keep, pltpu.roll(piece, turn, axis=1), 0.0)
                far_s[pl.ds(start + k, ROWS, stride=SPAN), :] = piece
        after = lane_d >= turn

        def aligned(c):
            base = (HALF + c) * SPAN + PAD
            return jnp.where(after, far_s[pl.ds(base, FLAT), :], far_s[pl.ds(base - 1, FLAT), :])

        def own_row(c):
            return own_s[pl.ds(pl.multiple_of(c * FLAT, FLAT), FLAT), :].astype(F32)

        def forward(step, carry):
            waves = []
            for quad in range(2):
                sides = []
                for half in range(2):
                    a = step * 8 + quad * 4 + half * 2
                    dens_a = own_row(a) * aligned(a)
                    dens_b = own_row(a + 1) * aligned(a + 1)
                    even = jnp.where(low_d, dens_a, swapped(dens_b)).astype(BF16)
                    odd = jnp.where(low_d, swapped(dens_a), dens_b).astype(BF16)
                    sides.append(jnp.concatenate([even, odd], axis=0))
                y = dot(first, jnp.concatenate(sides, axis=1))
                for half in range(2):
                    re = y[:SLOTS, half * LANES : (half + 1) * LANES]
                    im = y[SLOTS:, half * LANES : (half + 1) * LANES]
                    waves.append(jnp.where(low_w, re, swapped(im)))
                    waves.append(jnp.where(low_w, swapped(re), im))
            z = dot(jnp.concatenate(waves, axis=0).astype(BF16), depth_m)
            for q in range(8):
                block = z[q * SLOTS : (q + 1) * SLOTS]
                zr[pl.ds(step * 8 + q, SLOTS, stride=ZSPAN), :] = block[:, :LANES]
                zi[pl.ds(step * 8 + q, SLOTS, stride=ZSPAN), :] = block[:, LANES:]
            return carry

        lax.fori_loop(0, EDGE // 8, forward, 0, unroll=2)
        tab = row_t[n]

        def plane(w):
            at = slice(w * ZSPAN, w * ZSPAN + EDGE)
            return jnp.concatenate([zr[at, :], zi[at, :]], axis=0).astype(BF16)

        for w0 in range(0, SLOTS, 2):
            x = dot(rows_m, jnp.concatenate([plane(w0), plane(w0 + 1)], axis=1))
            weight = jnp.concatenate([scale_t[w0], scale_t[w0 + 1]], axis=1)
            re, im = x[:GRID] * weight, x[GRID:] * weight
            if w0 == 0:
                edge = x[:, :LANES].astype(BF16)
                back_re = dot(dot(flip, edge[:GRID]).astype(BF16), flip)
                back_im = dot(dot(flip, edge[GRID:]).astype(BF16), flip)
                extra = scale_t[SLOTS]
                re = jnp.concatenate([re[:, :LANES] + extra * back_re, re[:, LANES:]], axis=1)
                im = jnp.concatenate([im[:, :LANES] - extra * back_im, im[:, LANES:]], axis=1)
            w = jnp.concatenate([re, im], axis=0).astype(BF16)
            v = dot(tab, w).astype(BF16)
            for m in range(2):
                re = v[2 * m * EDGE : (2 * m + 1) * EDGE]
                im = v[(2 * m + 1) * EDGE : (2 * m + 2) * EDGE]
                left = jnp.concatenate(
                    [
                        jnp.concatenate([re[:, :LANES], im[:, :LANES]], axis=1),
                        jnp.concatenate([re[:, LANES:], im[:, LANES:]], axis=1),
                    ],
                    axis=0,
                )
                r = dot(left, dep_t[n, m])
                for h in range(2):
                    back_s[pl.ds(m * SLOTS + w0 + h, EDGE, stride=BSPAN), :] = r[h * EDGE : (h + 1) * EDGE]
        for t in range(SLABS):
            for r in range(ROWS):
                at = (t * ROWS + r) * BSPAN
                send[t, n, r] = back_s[at : at + 2 * SLOTS, :].astype(BF16)
        for r in range(ROWS):
            here_out[n, r] = aligned(slab * ROWS + r).astype(BF16)


def term_kernel(scal, got, here, there, last_t, own_out, odd_out, even_out, far_s):
    low = low_half((FLAT, LANES))
    scale = 1.0 / GRID**3

    def table(m, shift):
        parts = [last_t[pl.ds((2 * m + f) * GRID + HALF + shift + par, FLAT, stride=2), :] for f in range(2) for par in range(2)]
        return jnp.concatenate(parts, axis=0)

    own_tab = table(0, 0)
    for n in range(PAIRS):
        tab = jnp.concatenate([own_tab, table(1, scal[1 + n])], axis=0).astype(BF16)
        for row in range(0, ROWS, 2):
            data = [jnp.concatenate([got[t, n, row + q] for t in range(SLABS)], axis=0) for q in range(2)]
            g = dot(tab, jnp.concatenate(data, axis=1))
            for q in range(2):
                pots = []
                for m in range(2):
                    part = g[m * GRID : (m + 1) * GRID, q * LANES : (q + 1) * LANES]
                    c0, c1, s0, s1 = (part[f * FLAT : (f + 1) * FLAT] for f in range(4))
                    pots.append(jnp.where(low, c0 - swapped(s0), swapped(c1) - s1) * scale)
                term = pots[0] * here[n, row + q].astype(F32)
                own_out[row + q] = term if n == 0 else own_out[row + q] + term
                far_s[n, row + q] = pots[1] * there[n, row + q].astype(F32)
    hops = [scal[3 + n] for n in range(PAIRS)]
    for e in range(1, 5):
        target = odd_out if e % 2 else even_out
        for row in range(ROWS):
            value = sum(jnp.where(hops[n] == e, far_s[n, row], 0.0) for n in range(PAIRS))
            target[(e - 1) // 2, row] = value.astype(BF16)


VMEM = pl.BlockSpec(memory_space=pltpu.VMEM)
SMEM = pl.BlockSpec(memory_space=pltpu.SMEM)


def kept(shape, dtype):
    return pltpu.VMEM(shape, dtype)


def near(x):
    return pltpu.with_memory_space_constraint(x, pltpu.VMEM)


def offer_call(slab, own, kernel, interpret=False):
    return pl.pallas_call(
        offer_kernel,
        out_shape=jax.ShapeDtypeStruct((SLABS, 4 * GRID, LANES), BF16),
        in_specs=[SMEM, VMEM, VMEM],
        out_specs=VMEM,
        interpret=interpret,
        name="offer",
        compiler_params=pltpu.CompilerParams(vmem_limit_bytes=10 << 20),
    )(slab, own, kernel)


def prepare_call(scal, got, interpret=False):
    return pl.pallas_call(
        prepare_kernel,
        out_shape=(
            kept((EDGE * FLAT, LANES), BF16),
            kept((SLOTS + 1, GRID, LANES), F32),
            jax.ShapeDtypeStruct((PAIRS, ROWS, FLAT, LANES), BF16),
            jax.ShapeDtypeStruct((PAIRS, 4 * EDGE, 2 * GRID), BF16),
            jax.ShapeDtypeStruct((PAIRS, 2, 2 * GRID, LANES), BF16),
        ),
        in_specs=[SMEM] + [VMEM] * 4,
        out_specs=(VMEM,) * 5,
        scratch_shapes=[pltpu.VMEM((EDGE * SPAN, LANES), F32)],
        interpret=interpret,
        name="prepare",
        compiler_params=pltpu.CompilerParams(vmem_limit_bytes=12 << 20),
    )(scal, near(got), jnp.asarray(reversal()), jnp.asarray(COS), jnp.asarray(SIN))


def pair_call(scal, own_s, far_box, scale, rows, depths, interpret=False):
    return pl.pallas_call(
        pair_kernel,
        out_shape=(
            jax.ShapeDtypeStruct((SLABS, PAIRS, ROWS, 2 * SLOTS, LANES), BF16),
            kept((PAIRS, ROWS, FLAT, LANES), BF16),
        ),
        in_specs=[SMEM] + [VMEM] * 9,
        out_specs=(VMEM, VMEM),
        scratch_shapes=[
            pltpu.VMEM((ROOM * SPAN, LANES), F32),
            pltpu.VMEM((SLOTS * ZSPAN, LANES), F32),
            pltpu.VMEM((SLOTS * ZSPAN, LANES), F32),
            pltpu.VMEM((EDGE * BSPAN, LANES), F32),
        ],
        interpret=interpret,
        name="pair_waves",
        compiler_params=pltpu.CompilerParams(vmem_limit_bytes=20 << 20),
    )(
        scal,
        near(own_s),
        near(far_box),
        near(scale),
        rows,
        depths,
        jnp.asarray(forward_first()),
        jnp.asarray(forward_depth()),
        jnp.asarray(forward_rows()),
        jnp.asarray(reversal()),
    )


def term_call(scal, got, here, there, interpret=False):
    return pl.pallas_call(
        term_kernel,
        out_shape=(
            kept((ROWS, FLAT, LANES), F32),
            kept((2, ROWS, FLAT, LANES), BF16),
            kept((2, ROWS, FLAT, LANES), BF16),
        ),
        in_specs=[SMEM] + [VMEM] * 4,
        out_specs=(VMEM,) * 3,
        scratch_shapes=[pltpu.VMEM((PAIRS, ROWS, FLAT, LANES), F32)],
        interpret=interpret,
        name="pair_terms",
        compiler_params=pltpu.CompilerParams(vmem_limit_bytes=12 << 20),
    )(scal, near(got), near(here), there, jnp.asarray(backward_last()))


def passed_along(block, distance):
    count = lax.axis_size("orb")
    return lax.ppermute(block, "orb", [((i - distance) % count, i) for i in range(count)])


def other_core(block):
    count = lax.axis_size("orb")
    return lax.ppermute(block, "orb", [(i ^ 1, i) for i in range(count)])


def to_everyone(shard):
    copies = jnp.broadcast_to(shard, (lax.axis_size("slab"), *shard.shape))
    return lax.all_to_all(copies, "slab", split_axis=0, concat_axis=0, tiled=True)


def shared(block):
    return lax.all_to_all(block, "slab", split_axis=0, concat_axis=0, tiled=True)


def per_device(orbitals, partners, offsets, kernel):
    orbit = lax.axis_index("orb")
    slab = lax.axis_index("slab").astype(jnp.int32)
    even_core = orbit % 2 == 0
    cells = EDGE * EDGE
    own = orbitals[0]
    corner = jnp.pad(offsets.astype(BF16), ((0, 0), (0, LANES - 3)))
    loaded = jnp.concatenate([own, jnp.broadcast_to(corner, (ROWS, LANES))], axis=1)
    four = passed_along(loaded, -4)
    two = passed_along(loaded, -2)
    offered = shared(offer_call(slab[None], own, kernel))
    given = jnp.stack([jnp.where(even_core, two, loaded), jnp.where(even_core, four, two)])
    odd = other_core(given)
    hops = (partners[0] - orbit) % lax.axis_size("orb")

    def chosen(hop):
        low = jnp.where(hop == 1, odd[0], two)
        high = jnp.where(hop == 3, odd[1], four)
        return jnp.where(hop <= 2, low, high)

    picked = jnp.stack([chosen(hops[n]) for n in range(PAIRS)])
    shifts = picked[:, 0, cells : cells + 3].astype(jnp.int32) - offsets
    far_box = to_everyone(picked[:, :, :cells])
    scal = jnp.concatenate([slab[None], shifts.reshape(-1)])
    own_s, scale, there, rows, depths = prepare_call(scal, offered)
    send, here = pair_call(scal, own_s, far_box, scale, rows, depths)
    got = shared(send)
    scal = jnp.concatenate([jnp.zeros((1,), jnp.int32), shifts[:, 1], hops])
    mine, odd_out, even_out = term_call(scal, got, here, there)
    crossed = other_core(odd_out).astype(F32)
    by_two = even_out[0].astype(F32) + jnp.where(even_core, crossed[0], crossed[1])
    by_four = even_out[1].astype(F32) + jnp.where(even_core, crossed[1], 0.0)
    four_back = passed_along(by_four.astype(BF16), 4).astype(F32)
    two_back = passed_along(by_two.astype(BF16), 2).astype(F32)
    total = mine + jnp.where(even_core, 0.0, crossed[0]) + two_back + four_back
    return total.reshape(1, ROWS, cells)


def solution(mesh):
    return jax.shard_map(
        per_device,
        mesh=mesh,
        in_specs=(P("orb", "slab", None), P("orb", None), P("orb", None), P(None, "slab", None)),
        out_specs=P("orb", "slab", None),
        check_vma=False,
    )
```

time: 129 us -> 109 us (0.84)
  Pallas kernels: 32.3 us -> 13 us
  local copies, waits for them, and re-layouts: 6.83 us -> 10.8 us
  waiting for transfers between devices: 41.8 us -> 38.4 us
    pallas_call x1, Pallas kernels: 29.7 us -> 9.06 us  [pair_call(): pl.pallas_call(pair_kernel, out_shape=(jax.ShapeDtypeStruct((SLABS, PAIRS...]
    all_to_all x2 -> x1, waiting for transfers between devices: 14.9 us -> 8.54 us  [to_everyone(): lax.all_to_all(copies, 'slab', split_axis=0, concat_axis=0, tiled=True)]
    unnamed x16 -> x30, local copies, waits for them, and re-layouts: 2.63 us -> 7.55 us
    all_to_all x1 -> x2, starting transfers between devices: 3.64 us -> 8.18 us  [shared(): lax.all_to_all(block, 'slab', split_axis=0, concat_axis=0, tiled=True)]
    all_to_all x2 -> x1, starting transfers between devices: 7.97 us -> 3.63 us  [to_everyone(): lax.all_to_all(copies, 'slab', split_axis=0, concat_axis=0, tiled=True)]
    all_to_all x1 -> x2, waiting for transfers between devices: 14.1 us -> 17.3 us  [shared(): lax.all_to_all(block, 'slab', split_axis=0, concat_axis=0, tiled=True)]
    pallas_call x1 -> x3, Pallas kernels: 2.66 us -> 3.94 us  [the longest x1 1.57 us: offer_call(): pl.pallas_call(offer_kernel, out_shape=jax.ShapeDtypeStruct((SLABS, 4 * G...]
  transfers between devices with their start and end apart: 9 -> 9, of which waited for: 6 -> 6; matrix products, arithmetic and copies ran while one was open for 3% -> 2% of each run, Pallas kernels for 0% -> 3%
where the time goes in v2:
time: 109 us
  starting transfers between devices  39.9 us (37%)
  waiting for transfers between devices  38.4 us (35%)
  Pallas kernels  13 us (12%)
  local copies, waits for them, and re-layouts  10.8 us (10%)
  between operations  3.79 us (3%)
  other arithmetic  2.63 us (2%)
    ppermute x4, starting transfers between devices, passed_along(): lax.ppermute(block, 'orb', [((i - distance) % count, i) for i in range(co...  24.3 us
    all_to_all x2, waiting for transfers between devices, shared(): lax.all_to_all(block, 'slab', split_axis=0, concat_axis=0, tiled=True)  17.3 us
    ppermute x4, waiting for transfers between devices, passed_along(): lax.ppermute(block, 'orb', [((i - distance) % count, i) for i in range(co...  11.3 us
    pallas_call x1, Pallas kernels, pair_call(): pl.pallas_call(pair_kernel, out_shape=(jax.ShapeDtypeStruct((SLABS, PAIRS...  9.06 us
    all_to_all x1, waiting for transfers between devices, to_everyone(): lax.all_to_all(copies, 'slab', split_axis=0, concat_axis=0, tiled=True)  8.54 us
    all_to_all x2, starting transfers between devices, shared(): lax.all_to_all(block, 'slab', split_axis=0, concat_axis=0, tiled=True)  8.18 us
    unnamed x30, local copies, waits for them, and re-layouts  7.55 us
    ppermute x2, starting transfers between devices, other_core(): return lax.ppermute(block, 'orb', [(i ^ 1, i) for i in range(count)])  3.84 us
  transfers between devices with their start and end apart: 9, of which 6 were waited for; matrix products, arithmetic and copies ran while one was open for 2% of the time, Pallas kernels for 3%

profile of v2, /device:TPU:16, one launch (start us, length us, event | category | flops | bytes accessed | tf_op | source)
XLA Modules:
  0.0 108.5 jit_solution(3966201201654065158)
XLA Ops:
  0.0 0.7 convert_element_type.46
  0.7 0.0 copy-start.1
  0.7 0.9 pad_maximum_fusion.2
  1.6 14.4 %collective-permute-start.1 = (bf16[8,4224]{1,0:T(8,128)(2,1)S(1)}, bf16[8,4224]{1,0:T(8,128)(2,1)S(1)}, u32[]{:S(2)}, u32[]{:S(2)}) collective-permute-start(bf16[8,4224]{1,0:T(8,128)(2,1)S(1)} %pad_maximum_fusion.2), channel_id=1, source_target_pairs={{32,0},{40,8},{48,16},{56,24},{64,32},{72,40},{80,48},{88,56},{96,... | collective-permute-start | bytes 202760 | tf_op jit(solution)/shard_map/ppermute | solution.py:410
  16.0 4.0 %collective-permute-start = (bf16[8,4224]{1,0:T(8,128)(2,1)S(1)}, bf16[8,4224]{1,0:T(8,128)(2,1)S(1)}, u32[]{:S(2)}, u32[]{:S(2)}) collective-permute-start(bf16[8,4224]{1,0:T(8,128)(2,1)S(1)} %pad_maximum_fusion.2), channel_id=1, source_target_pairs={{16,0},{24,8},{32,16},{40,24},{48,32},{56,40},{64,48},{72,56},{80,... | collective-permute-start | bytes 202760 | tf_op jit(solution)/shard_map/ppermute | solution.py:410
  20.1 0.0 copy-done.1
  20.1 0.0 copy-start
  20.1 1.2 %copy-done = f32[128,16,128]{2,1,0:T(8,128)S(1)} copy-done((f32[128,16,128]{2,1,0:T(8,128)S(1)}, f32[128,16,128]{2,1,0:T(8,128)}, u32[]{:S(2)}) %copy-start) | copy-done | bytes 1048600
  21.3 1.6 %offer.1 = bf16[8,512,128]{2,1,0:T(8,128)(2,1)} custom-call(s32[1]{0:T(128)} %bitcast.17.slab_ref, bf16[8,4096]{1,0:T(8,128)(2,1)S(1)} %bitcast.45, f32[128,16,128]{2,1,0:T(8,128)S(1)} %copy-done), custom_call_target="tpu_custom_call" | custom-call | tf_op jit(solution)/shard_map/offer/pallas_call | solution.py:329
  22.9 4.4 %all-to-all-start = ((bf16[8,512,128]{2,1,0:T(8,128)(2,1)}), bf16[8,512,128]{2,1,0:T(8,128)(2,1)S(1)}, u32[]{:S(2)}, u32[]{:S(2)}) async-start(bf16[8,512,128]{2,1,0:T(8,128)(2,1)} %offer.1), calls=%async_computation | async-start | bytes 2097152 | tf_op jit(solution)/shard_map/all_to_all | solution.py:424
  27.3 0.0 collective-permute-done.1
  27.3 0.0 collective-permute-done
  27.4 0.0 copy-start.14
  27.4 1.9 %collective-permute-start.2 = (bf16[2,8,4224]{2,1,0:T(8,128)(2,1)S(1)}, bf16[2,8,4224]{2,1,0:T(8,128)(2,1)S(1)}, u32[]{:S(2)}, u32[]{:S(2)}) collective-permute-start(bf16[2,8,4224]{2,1,0:T(8,128)(2,1)S(1)} %pad_maximum_fusion), channel_id=1, source_target_pairs={{8,0},{0,8},{24,16},{16,24},{40,32},{32,40},{56,48},{48,56},{72,64... | collective-permute-start | bytes 405512 | tf_op jit(solution)/shard_map/ppermute | solution.py:415
  29.3 0.0 copy-done.14
  29.4 0.6 fusion.6
  33.5 0.0 collective-permute-done.2
  33.6 8.0 %all-to-all-done.got = bf16[8,512,128]{2,1,0:T(8,128)(2,1)S(1)} async-done(((bf16[8,512,128]{2,1,0:T(8,128)(2,1)}), bf16[8,512,128]{2,1,0:T(8,128)(2,1)S(1)}, u32[]{:S(2)}, u32[]{:S(2)}) %all-to-all-start) | async-done | bytes 1048608 | tf_op jit(solution)/shard_map/all_to_all | solution.py:424
  41.5 1.1 %broadcast_in_dim.23 = bf16[8,2,8,4096]{3,2,1,0:T(8,128)(2,1)} broadcast(bf16[2,8,4096]{2,1,0:T(8,128)(2,1)S(1)} %pad_maximum_fusion.1), dimensions={1,2,3} | broadcast | bytes 1179648 | tf_op jit(solution)/shard_map/broadcast_in_dim | solution.py:419
  42.6 3.6 %all-to-all-start.1 = ((bf16[8,2,8,4096]{3,2,1,0:T(8,128)(2,1)}), bf16[8,2,8,4096]{3,2,1,0:T(8,128)(2,1)S(1)}, u32[]{:S(2)}, u32[]{:S(2)}) async-start(bf16[8,2,8,4096]{3,2,1,0:T(8,128)(2,1)} %broadcast_in_dim.23), calls=%async_computation.1 | async-start | bytes 2097152 | tf_op jit(solution)/shard_map/all_to_all | solution.py:420
  46.3 0.0 copy-start.13
  46.3 0.7 copy-done.13
  46.9 0.1 sub.30
  47.0 0.5 broadcast.27
  47.5 0.0 copy-start.5
  47.5 0.7 fusion.5
  48.2 0.1 reshape.40
  48.3 0.1 pad_add_fusion.1.scal
  48.4 0.0 copy-done.5
  48.4 0.0 copy-start.10
  48.4 0.8 copy-done.10
  49.2 0.0 copy-start.11
  49.2 0.8 copy-done.11
  50.1 0.0 copy-start.12
  50.1 1.3 %prepare.1 = (bf16[2048,128]{1,0:T(8,128)(2,1)S(1)}, f32[9,128,128]{2,1,0:T(8,128)S(1)}, bf16[2,8,32,128]{3,2,1,0:T(8,128)(2,1)S(1)}, bf16[2,256,256]{2,1,0:T(8,128)(2,1)S(1)}, bf16[2,2,256,128]{3,2,1,0:T(8,128)(2,1)S(1)}) custom-call(s32[7]{0:T(128)S(1)} %pad_add_fusion.1.scal, bf16[8,512,128]{2,1,0:T(8,128)(2,1)S(1)} %all-to-all-done.got, ...), custom_call_target="tpu_custom_call" | custom-call | tf_op jit(solution)/shard_map/prepare/pallas_call | solution.py:341
  51.4 0.0 copy-start.2
  51.4 0.7 copy-done.2
  52.1 0.0 copy-start.6
  52.1 0.7 copy-done.6
  52.7 8.5 %all-to-all-done.1.far_in = bf16[8,2,8,4096]{3,2,1,0:T(8,128)(2,1)S(1)} async-done(((bf16[8,2,8,4096]{3,2,1,0:T(8,128)(2,1)}), bf16[8,2,8,4096]{3,2,1,0:T(8,128)(2,1)S(1)}, u32[]{:S(2)}, u32[]{:S(2)}) %all-to-all-start.1) | async-done | bytes 1048608 | tf_op jit(solution)/shard_map/all_to_all | solution.py:420
  61.3 0.0 copy-done.12
  61.3 0.0 copy-start.3
  61.3 0.9 copy-done.3
  62.2 0.0 copy-start.8
  62.2 0.8 copy-done.8
  63.0 0.0 copy-start.9
  63.0 0.8 copy-done.9
  63.9 9.1 %pair_waves.1 = (bf16[8,2,8,16,128]{4,3,2,1,0:T(8,128)(2,1)}, bf16[2,8,32,128]{3,2,1,0:T(8,128)(2,1)S(1)}) custom-call(s32[7]{0:T(128)S(1)} %pad_add_fusion.1.scal, bf16[2048,128]{1,0:T(8,128)(2,1)S(1)} %get-tuple-element.15.own_s, bf16[8,2,8,4096]{3,2,1,0:T(8,128)(2,1)S(1)} %all-to-all-done.1.far_in, f32[9,128,128]{2,1,0:T(8,128)S(1)} %get-tuple-element.16.scale_t, ...), custom_call_target="tpu_custom_call" | custom-call | tf_op jit(solution)/shard_map/pair_waves/pallas_call | solution.py:360
  72.9 0.0 copy-start.4
  72.9 0.0 copy-start.7
  73.0 3.8 %all-to-all-start.2 = ((bf16[8,2,8,16,128]{4,3,2,1,0:T(8,128)(2,1)}), bf16[8,2,8,16,128]{4,3,2,1,0:T(8,128)(2,1)S(1)}, u32[]{:S(2)}, u32[]{:S(2)}) async-start(bf16[8,2,8,16,128]{4,3,2,1,0:T(8,128)(2,1)} %get-tuple-element.19), calls=%async_computation.2 | async-start | bytes 1048576 | tf_op jit(solution)/shard_map/all_to_all | solution.py:424
  76.7 0.2 slice_reduce_fusion
  76.9 0.1 pad_add_fusion.scal
  77.0 9.3 %all-to-all-done.2.got = bf16[8,2,8,16,128]{4,3,2,1,0:T(8,128)(2,1)S(1)} async-done(((bf16[8,2,8,16,128]{4,3,2,1,0:T(8,128)(2,1)}), bf16[8,2,8,16,128]{4,3,2,1,0:T(8,128)(2,1)S(1)}, u32[]{:S(2)}, u32[]{:S(2)}) %all-to-all-start.2) | async-done | bytes 524320 | tf_op jit(solution)/shard_map/all_to_all | solution.py:424
  86.3 0.0 copy-done.4
  86.3 0.0 copy-done.7
  86.3 1.1 pair_terms.1
  87.4 1.9 %collective-permute-start.3 = (bf16[2,8,32,128]{3,2,1,0:T(8,128)(2,1)S(1)}, bf16[2,8,32,128]{3,2,1,0:T(8,128)(2,1)S(1)}, u32[]{:S(2)}, u32[]{:S(2)}) collective-permute-start(bf16[2,8,32,128]{3,2,1,0:T(8,128)(2,1)S(1)} %get-tuple-element.23), channel_id=1, source_target_pairs={{8,0},{0,8},{24,16},{16,24},{40,32},{32,40},{56,48},{48,56},{72,64... | collective-permute-start | bytes 393224 | tf_op jit(solution)/shard_map/ppermute | solution.py:415
  89.3 1.3 %collective-permute-done.3 = bf16[2,8,32,128]{3,2,1,0:T(8,128)(2,1)S(1)} collective-permute-done((bf16[2,8,32,128]{3,2,1,0:T(8,128)(2,1)S(1)}, bf16[2,8,32,128]{3,2,1,0:T(8,128)(2,1)S(1)}, u32[]{:S(2)}, u32[]{:S(2)}) %collective-permute-start.3) | collective-permute-done | bytes 131104 | tf_op jit(solution)/shard_map/ppermute | solution.py:415
  90.7 3.9 %collective-permute-start.4 = (bf16[8,32,128]{2,1,0:T(8,128)(2,1)S(1)}, bf16[8,32,128]{2,1,0:T(8,128)(2,1)S(1)}, u32[]{:S(2)}, u32[]{:S(2)}) collective-permute-start(bf16[8,32,128]{2,1,0:T(8,128)(2,1)S(1)} %get-tuple-element.27), channel_id=1, source_target_pairs={{496,0},{504,8},{0,16},{8,24},{16,32},{24,40},{32,48},{40,56},{48,... | collective-permute-start | bytes 196616 | tf_op jit(solution)/shard_map/ppermute | solution.py:410
  94.7 1.9 %collective-permute-start.5 = (bf16[8,32,128]{2,1,0:T(8,128)(2,1)S(1)}, bf16[8,32,128]{2,1,0:T(8,128)(2,1)S(1)}, u32[]{:S(2)}, u32[]{:S(2)}) collective-permute-start(bf16[8,32,128]{2,1,0:T(8,128)(2,1)S(1)} %get-tuple-element.28), channel_id=1, source_target_pairs={{480,0},{488,8},{496,16},{504,24},{0,32},{8,40},{16,48},{24,56},{3... | collective-permute-start | bytes 196616 | tf_op jit(solution)/shard_map/ppermute | solution.py:410
  96.6 1.9 %collective-permute-done.4 = bf16[8,32,128]{2,1,0:T(8,128)(2,1)S(1)} collective-permute-done((bf16[8,32,128]{2,1,0:T(8,128)(2,1)S(1)}, bf16[8,32,128]{2,1,0:T(8,128)(2,1)S(1)}, u32[]{:S(2)}, u32[]{:S(2)}) %collective-permute-start.4) | collective-permute-done | bytes 65568 | tf_op jit(solution)/shard_map/ppermute | solution.py:410
  98.5 9.4 %collective-permute-done.5 = bf16[8,32,128]{2,1,0:T(8,128)(2,1)S(1)} collective-permute-done((bf16[8,32,128]{2,1,0:T(8,128)(2,1)S(1)}, bf16[8,32,128]{2,1,0:T(8,128)(2,1)S(1)}, u32[]{:S(2)}, u32[]{:S(2)}) %collective-permute-start.5) | collective-permute-done | bytes 65568 | tf_op jit(solution)/shard_map/ppermute | solution.py:410
  107.9 0.7 reshape.38
  (13 shorter events, 0.2 us)
Async XLA Ops:
  0.7 19.4 %copy-start.1 = (bf16[1,8,4096]{2,1,0:T(8,128)(2,1)S(1)}, bf16[1,8,4096]{2,1,0:T(8,128)(2,1)}, u32[]{:S(2)}) copy-start(bf16[1,8,4096]{2,1,0:T(8,128)(2,1)} %param.12) | copy-start | bytes 196612
  1.6 25.7 %collective-permute-start.1 = (bf16[8,4224]{1,0:T(8,128)(2,1)S(1)}, bf16[8,4224]{1,0:T(8,128)(2,1)S(1)}, u32[]{:S(2)}, u32[]{:S(2)}) collective-permute-start(bf16[8,4224]{1,0:T(8,128)(2,1)S(1)} %pad_maximum_fusion.2), channel_id=1, source_target_pairs={{32,0},{40,8},{48,16},{56,24},{64,32},{72,40},{80,48},{88,56},{96,... | collective-permute-start | bytes 202760 | tf_op jit(solution)/shard_map/ppermute | solution.py:410
  16.0 11.3 %collective-permute-start = (bf16[8,4224]{1,0:T(8,128)(2,1)S(1)}, bf16[8,4224]{1,0:T(8,128)(2,1)S(1)}, u32[]{:S(2)}, u32[]{:S(2)}) collective-permute-start(bf16[8,4224]{1,0:T(8,128)(2,1)S(1)} %pad_maximum_fusion.2), channel_id=1, source_target_pairs={{16,0},{24,8},{32,16},{40,24},{48,32},{56,40},{64,48},{72,56},{80,... | collective-permute-start | bytes 202760 | tf_op jit(solution)/shard_map/ppermute | solution.py:410
  20.1 1.2 %copy-start = (f32[128,16,128]{2,1,0:T(8,128)S(1)}, f32[128,16,128]{2,1,0:T(8,128)}, u32[]{:S(2)}) copy-start(f32[128,16,128]{2,1,0:T(8,128)} %kern.1) | copy-start | bytes 3145732
  22.9 18.7 %all-to-all-start = ((bf16[8,512,128]{2,1,0:T(8,128)(2,1)}), bf16[8,512,128]{2,1,0:T(8,128)(2,1)S(1)}, u32[]{:S(2)}, u32[]{:S(2)}) async-start(bf16[8,512,128]{2,1,0:T(8,128)(2,1)} %offer.1), calls=%async_computation | async-start | bytes 2097152 | tf_op jit(solution)/shard_map/all_to_all | solution.py:424
  27.4 2.0 %copy-start.14 = (s32[1,2]{1,0:T(1,128)S(1)}, s32[1,2]{1,0:T(1,128)}, u32[]{:S(2)}) copy-start(s32[1,2]{1,0:T(1,128)} %param.13) | copy-start | bytes 28
  27.4 6.1 %collective-permute-start.2 = (bf16[2,8,4224]{2,1,0:T(8,128)(2,1)S(1)}, bf16[2,8,4224]{2,1,0:T(8,128)(2,1)S(1)}, u32[]{:S(2)}, u32[]{:S(2)}) collective-permute-start(bf16[2,8,4224]{2,1,0:T(8,128)(2,1)S(1)} %pad_maximum_fusion), channel_id=1, source_target_pairs={{8,0},{0,8},{24,16},{16,24},{40,32},{32,40},{56,48},{48,56},{72,64... | collective-permute-start | bytes 405512 | tf_op jit(solution)/shard_map/ppermute | solution.py:415
  42.6 18.6 %all-to-all-start.1 = ((bf16[8,2,8,4096]{3,2,1,0:T(8,128)(2,1)}), bf16[8,2,8,4096]{3,2,1,0:T(8,128)(2,1)S(1)}, u32[]{:S(2)}, u32[]{:S(2)}) async-start(bf16[8,2,8,4096]{3,2,1,0:T(8,128)(2,1)} %broadcast_in_dim.23), calls=%async_computation.1 | async-start | bytes 2097152 | tf_op jit(solution)/shard_map/all_to_all | solution.py:420
  46.3 0.7 copy-start.13
  47.5 0.8 copy-start.5
  48.4 0.8 copy-start.10
  49.2 0.8 copy-start.11
  50.1 11.2 %copy-start.12 = (bf16[8,16,64]{2,1,0:T(8,128)(2,1)S(1)}, bf16[8,16,64]{2,1,0:T(8,128)(2,1)}, u32[]{:S(2)}) copy-start(bf16[8,16,64]{2,1,0:T(8,128)(2,1)} %constant.71.clone.first_t) | copy-start | bytes 49156
  51.4 0.7 copy-start.2
  52.1 0.7 copy-start.6
  61.3 1.0 copy-start.3
  62.2 0.8 copy-start.8
  63.0 0.8 copy-start.9
  72.9 13.4 %copy-start.4 = (f32[512,128]{1,0:T(8,128)S(1)}, f32[512,128]{1,0:T(8,128)}, u32[]{:S(2)}) copy-start(f32[512,128]{1,0:T(8,128)} %constant.74.clone.last_t) | copy-start | bytes 786436
  72.9 13.4 %copy-start.7 = (bf16[2,8,32,128]{3,2,1,0:T(8,128)(2,1)S(1)}, bf16[2,8,32,128]{3,2,1,0:T(8,128)(2,1)}, u32[]{:S(2)}) copy-start(bf16[2,8,32,128]{3,2,1,0:T(8,128)(2,1)} %copy-done.6) | copy-start | bytes 393220
  73.0 13.4 %all-to-all-start.2 = ((bf16[8,2,8,16,128]{4,3,2,1,0:T(8,128)(2,1)}), bf16[8,2,8,16,128]{4,3,2,1,0:T(8,128)(2,1)S(1)}, u32[]{:S(2)}, u32[]{:S(2)}) async-start(bf16[8,2,8,16,128]{4,3,2,1,0:T(8,128)(2,1)} %get-tuple-element.19), calls=%async_computation.2 | async-start | bytes 1048576 | tf_op jit(solution)/shard_map/all_to_all | solution.py:424
  87.4 3.2 %collective-permute-start.3 = (bf16[2,8,32,128]{3,2,1,0:T(8,128)(2,1)S(1)}, bf16[2,8,32,128]{3,2,1,0:T(8,128)(2,1)S(1)}, u32[]{:S(2)}, u32[]{:S(2)}) collective-permute-start(bf16[2,8,32,128]{3,2,1,0:T(8,128)(2,1)S(1)} %get-tuple-element.23), channel_id=1, source_target_pairs={{8,0},{0,8},{24,16},{16,24},{40,32},{32,40},{56,48},{48,56},{72,64... | collective-permute-start | bytes 393224 | tf_op jit(solution)/shard_map/ppermute | solution.py:415
  90.7 7.7 %collective-permute-start.4 = (bf16[8,32,128]{2,1,0:T(8,128)(2,1)S(1)}, bf16[8,32,128]{2,1,0:T(8,128)(2,1)S(1)}, u32[]{:S(2)}, u32[]{:S(2)}) collective-permute-start(bf16[8,32,128]{2,1,0:T(8,128)(2,1)S(1)} %get-tuple-element.27), channel_id=1, source_target_pairs={{496,0},{504,8},{0,16},{8,24},{16,32},{24,40},{32,48},{40,56},{48,... | collective-permute-start | bytes 196616 | tf_op jit(solution)/shard_map/ppermute | solution.py:410
  94.7 13.2 %collective-permute-start.5 = (bf16[8,32,128]{2,1,0:T(8,128)(2,1)S(1)}, bf16[8,32,128]{2,1,0:T(8,128)(2,1)S(1)}, u32[]{:S(2)}, u32[]{:S(2)}) collective-permute-start(bf16[8,32,128]{2,1,0:T(8,128)(2,1)S(1)} %get-tuple-element.28), channel_id=1, source_target_pairs={{480,0},{488,8},{496,16},{504,24},{0,32},{8,40},{16,48},{24,56},{3... | collective-permute-start | bytes 196616 | tf_op jit(solution)/shard_map/ppermute | solution.py:410

commit v3 on v2

--- a/solution.py
+++ b/solution.py
@@ -1,5 +1,3 @@
-import math
-
 import jax
 import jax.numpy as jnp
 import numpy as np
@@ -7,6 +5,7 @@
 from jax.experimental import pallas as pl
 from jax.experimental.pallas import tpu as pltpu
 from jax.sharding import PartitionSpec as P
+
 
 EDGE = 64
 GRID = 128
@@ -38,7 +37,7 @@
 SIGN = COS[:, EDGE]
 BOX = slice(HALF, HALF + EDGE)
 SPLIT_CELLS = np.concatenate([np.arange(0, EDGE, 2), np.arange(1, EDGE, 2)]) + HALF
-OWN_WAVES = np.array([[16 * (q // 2) + 2 * s + q % 2 for q in range(SLOTS)] for s in range(SLABS)])
+OWN_WAVES = np.array([[WAVES * s + (s >= SLABS // 2) + q for q in range(SLOTS)] for s in range(SLABS)])
 
 
 def forward_first():
@@ -97,17 +96,42 @@
     return (depth >= 0) & (depth < EDGE)
 
 
-def offer_kernel(slab_ref, own, kern, send):
-    slab = slab_ref[0]
+def load_kernel(corner, own, loaded, copies):
+    cells = own[...]
+    loaded[:, : EDGE * EDGE] = cells
+    lane = lanes_of((ROWS, LANES))
+    mark = jnp.zeros((ROWS, LANES), F32)
+    for k in range(3):
+        mark = jnp.where(lane == k, corner[0, k].astype(F32), mark)
+    loaded[:, EDGE * EDGE :] = mark.astype(BF16)
+    for t in range(SLABS):
+        copies[t] = cells
+
+
+def mirror_kernel(kern, upper, lowest):
     kern_flat = kern.reshape(GRID * WAVES, LANES)
-    mine = [jnp.concatenate([own[:, (k + h) * LANES : (k + h + 1) * LANES] for h in range(2)], axis=0) for k in range(0, FLAT, 2)]
-    mine = jnp.concatenate(mine, axis=0)
-    for t in range(SLABS):
-        for j in range(2):
-            high = (WAVES - 2 * t) % WAVES if j == 0 else WAVES - 1 - 2 * t
-            at = jnp.where(slab < SLABS // 2, 2 * t + j, high)
-            send[t, j * GRID : (j + 1) * GRID, :] = kern_flat[pl.ds(at, GRID, stride=WAVES), :].astype(BF16)
-        send[t, 2 * GRID :, :] = mine
+    for q in range(SLOTS):
+        upper[q] = kern_flat[pl.ds(SLOTS + q, GRID, stride=WAVES), :].astype(BF16)
+    lowest[...] = kern_flat[pl.ds(0, GRID, stride=WAVES), :].astype(BF16)
+
+
+def pick_kernel(hops, two, four, odd, copies, marks, block, sems):
+    for n in range(PAIRS):
+        hop = hops[n]
+        for k in range(0, EDGE * EDGE + LANES, LANES):
+            at = slice(k, k + LANES)
+            low = jnp.where(hop == 1, odd[0, :, at].astype(F32), two[:, at].astype(F32))
+            high = jnp.where(hop == 3, odd[1, :, at].astype(F32), four[:, at].astype(F32))
+            value = jnp.where(hop <= 2, low, high).astype(BF16)
+            if k == EDGE * EDGE:
+                marks[n] = value
+            else:
+                block[n, :, at] = value
+    sends = [pltpu.make_async_copy(block, copies.at[t], sems.at[t]) for t in range(SLABS)]
+    for one in sends:
+        one.start()
+    for one in sends:
+        one.wait()
 
 
 def moved(ref, row, d0, d1, d2):
@@ -123,7 +147,7 @@
     return jnp.where(in_depth(lane, d2) & inside, jnp.where(lane >= turn, here, before), 0.0)
 
 
-def prepare_kernel(scal, got, flip_t, cos_f, sin_f, own_out, scale_out, there_out, row_out, dep_out, own_s):
+def prepare_kernel(scal, got, kern, upper, lowest, flip_t, cos_f, sin_f, own_out, scale_out, there_out, row_out, dep_out, own_s):
     slab = scal[0]
     zeros = jnp.zeros((PAD + 1, LANES), F32)
     for c in range(EDGE):
@@ -131,8 +155,8 @@
         own_s[c * SPAN + PAD + FLAT : (c + 1) * SPAN, :] = zeros
     for t in range(SLABS):
         for k in range(FLAT):
-            at = 2 * GRID + k * ROWS
-            own_s[pl.ds(t * ROWS * SPAN + PAD + k, ROWS, stride=SPAN), :] = got[t, at : at + ROWS, :].astype(F32)
+            piece = got[t, :, k * LANES : (k + 1) * LANES].astype(F32)
+            own_s[pl.ds(t * ROWS * SPAN + PAD + k, ROWS, stride=SPAN), :] = piece
     for c in range(EDGE):
         own_out[c * FLAT : (c + 1) * FLAT, :] = own_s[c * SPAN + PAD : c * SPAN + PAD + FLAT, :].astype(BF16)
     flip = flip_t[...]
@@ -140,22 +164,22 @@
     def reversed_plane(plane):
         return dot(dot(flip, plane).astype(BF16), flip)
 
+    kern_flat = kern.reshape(GRID * WAVES, LANES)
     first = slab == 0
-    for t in range(SLABS // 2):
-        for j in range(2):
-            here = got[t, j * GRID : (j + 1) * GRID, :]
-            if j:
-                there = got[SLABS - 1 - t, GRID : 2 * GRID, :]
-            else:
-                there = got[jnp.where(first, (SLABS - t) % SLABS, SLABS - 1 - t), :GRID, :]
-            both = here.astype(F32) + reversed_plane(there)
-            if t + j:
-                scale_out[2 * t + j] = both
-            else:
-                top = got[SLABS // 2, :GRID, :]
-                top = top.astype(F32) + reversed_plane(top)
-                scale_out[0] = jnp.where(first, 0.25 * (both + top), both)
-                scale_out[SLOTS] = jnp.where(first, 0.25 * (both - top), 0.0)
+    lower = slab < SLABS // 2
+    for q in range(SLOTS):
+        here = kern_flat[pl.ds(jnp.where(lower, q, q + 1), GRID, stride=WAVES), :]
+        if q:
+            there = upper[jnp.where(lower, SLOTS - q, SLOTS - 1 - q)]
+            scale_out[q] = here + reversed_plane(there)
+        else:
+            here = here.astype(BF16).astype(F32)
+            low = lowest[...].astype(F32)
+            there = jnp.where(lower, low, upper[SLOTS - 1].astype(F32))
+            both = here + reversed_plane(jnp.where(first, here, there).astype(BF16))
+            top = low + reversed_plane(lowest[...])
+            scale_out[0] = jnp.where(first, 0.25 * (both + top), both)
+            scale_out[SLOTS] = jnp.where(first, 0.25 * (both - top), 0.0)
     for n in range(PAIRS):
         d0, d1, d2 = scal[1 + 3 * n], scal[2 + 3 * n], scal[3 + 3 * n]
         for r in range(ROWS):
@@ -179,12 +203,38 @@
             dep_out[n, m, GRID:, :] = jnp.where(low, -s, swapped(c)).astype(BF16)
 
 
-def pair_kernel(scal, own_s, far_in, scale_t, row_t, dep_t, first_t, depth_t, rows_t, flip_t, send, here_out, far_s, zr, zi, back_s):
+def pair_kernel(
+    scal,
+    own_h,
+    far_in,
+    scale_t,
+    row_h,
+    dep_h,
+    first_h,
+    depth_h,
+    rows_h,
+    flip_h,
+    send,
+    here_out,
+    far_s,
+    zr,
+    zi,
+    back_s,
+    own_s,
+    row_t,
+    dep_t,
+    first_t,
+    depth_t,
+    rows_t,
+    flip_t,
+    sems,
+):
     slab = scal[0]
-    first = first_t[slab]
-    depth_m = depth_t[...]
-    rows_m = rows_t[...]
-    flip = flip_t[...]
+    held = (own_h, row_h, dep_h, first_h, depth_h, rows_h, flip_h)
+    local = (own_s, row_t, dep_t, first_t, depth_t, rows_t, flip_t)
+    loads = [pltpu.make_async_copy(a, b, sems.at[i]) for i, (a, b) in enumerate(zip(held, local))]
+    for load in loads:
+        load.start()
     low_d = low_half((FLAT, LANES))
     low_w = low_half((SLOTS, LANES))
     lane_d = lanes_of((FLAT, LANES))
@@ -209,6 +259,13 @@
                 piece = jnp.where(keep, pltpu.roll(piece, turn, axis=1), 0.0)
                 far_s[pl.ds(start + k, ROWS, stride=SPAN), :] = piece
         after = lane_d >= turn
+        if n == 0:
+            for load in loads:
+                load.wait()
+            first = first_t[slab]
+        depth_m = depth_t[...]
+        rows_m = rows_t[...]
+        flip = flip_t[...]
 
         def aligned(c):
             base = (HALF + c) * SPAN + PAD
@@ -315,45 +372,88 @@
 
 VMEM = pl.BlockSpec(memory_space=pltpu.VMEM)
 SMEM = pl.BlockSpec(memory_space=pltpu.SMEM)
+HBM = pl.BlockSpec(memory_space=pltpu.HBM)
 
 
 def kept(shape, dtype):
     return pltpu.VMEM(shape, dtype)
 
 
+def far(shape, dtype):
+    return pltpu.HBM(shape, dtype)
+
+
+def away(x):
+    return pltpu.with_memory_space_constraint(x, pltpu.HBM)
+
+
 def near(x):
     return pltpu.with_memory_space_constraint(x, pltpu.VMEM)
 
 
-def offer_call(slab, own, kernel, interpret=False):
+def load_call(offsets, own, interpret=False):
     return pl.pallas_call(
-        offer_kernel,
-        out_shape=jax.ShapeDtypeStruct((SLABS, 4 * GRID, LANES), BF16),
-        in_specs=[SMEM, VMEM, VMEM],
-        out_specs=VMEM,
+        load_kernel,
+        out_shape=(
+            kept((ROWS, EDGE * EDGE + LANES), BF16),
+            kept((SLABS, ROWS, EDGE * EDGE), BF16),
+        ),
+        in_specs=[SMEM, VMEM],
+        out_specs=(VMEM,) * 2,
         interpret=interpret,
-        name="offer",
-        compiler_params=pltpu.CompilerParams(vmem_limit_bytes=10 << 20),
-    )(slab, own, kernel)
-
-
-def prepare_call(scal, got, interpret=False):
+        name="load",
+        compiler_params=pltpu.CompilerParams(vmem_limit_bytes=8 << 20),
+    )(offsets, own)
+
+
+def mirror_call(kernel, interpret=False):
+    return pl.pallas_call(
+        mirror_kernel,
+        out_shape=(
+            kept((SLOTS, GRID, LANES), BF16),
+            kept((GRID, LANES), BF16),
+        ),
+        in_specs=[VMEM],
+        out_specs=(VMEM,) * 2,
+        interpret=interpret,
+        name="mirror",
+        compiler_params=pltpu.CompilerParams(vmem_limit_bytes=8 << 20),
+    )(kernel)
+
+
+def pick_call(hops, two, four, odd, interpret=False):
+    return pl.pallas_call(
+        pick_kernel,
+        out_shape=(
+            far((SLABS, PAIRS, ROWS, EDGE * EDGE), BF16),
+            kept((PAIRS, ROWS, LANES), BF16),
+        ),
+        in_specs=[SMEM] + [VMEM] * 3,
+        out_specs=(HBM, VMEM),
+        scratch_shapes=[pltpu.VMEM((PAIRS, ROWS, EDGE * EDGE), BF16), pltpu.SemaphoreType.DMA((SLABS,))],
+        interpret=interpret,
+        name="pick",
+        compiler_params=pltpu.CompilerParams(vmem_limit_bytes=8 << 20),
+    )(hops, near(two), near(four), near(odd))
+
+
+def prepare_call(scal, got, kernel, upper, lowest, interpret=False):
     return pl.pallas_call(
         prepare_kernel,
         out_shape=(
-            kept((EDGE * FLAT, LANES), BF16),
+            far((EDGE * FLAT, LANES), BF16),
             kept((SLOTS + 1, GRID, LANES), F32),
-            jax.ShapeDtypeStruct((PAIRS, ROWS, FLAT, LANES), BF16),
-            jax.ShapeDtypeStruct((PAIRS, 4 * EDGE, 2 * GRID), BF16),
-            jax.ShapeDtypeStruct((PAIRS, 2, 2 * GRID, LANES), BF16),
+            far((PAIRS, ROWS, FLAT, LANES), BF16),
+            far((PAIRS, 4 * EDGE, 2 * GRID), BF16),
+            far((PAIRS, 2, 2 * GRID, LANES), BF16),
         ),
-        in_specs=[SMEM] + [VMEM] * 4,
+        in_specs=[SMEM] + [VMEM] * 7,
         out_specs=(VMEM,) * 5,
         scratch_shapes=[pltpu.VMEM((EDGE * SPAN, LANES), F32)],
         interpret=interpret,
         name="prepare",
         compiler_params=pltpu.CompilerParams(vmem_limit_bytes=12 << 20),
-    )(scal, near(got), jnp.asarray(reversal()), jnp.asarray(COS), jnp.asarray(SIN))
+    )(scal, near(got), kernel, near(upper), near(lowest), jnp.asarray(reversal()), jnp.asarray(COS), jnp.asarray(SIN))
 
 
 def pair_call(scal, own_s, far_box, scale, rows, depths, interpret=False):
@@ -363,28 +463,36 @@
             jax.ShapeDtypeStruct((SLABS, PAIRS, ROWS, 2 * SLOTS, LANES), BF16),
             kept((PAIRS, ROWS, FLAT, LANES), BF16),
         ),
-        in_specs=[SMEM] + [VMEM] * 9,
+        in_specs=[SMEM, HBM, VMEM, VMEM] + [HBM] * 6,
         out_specs=(VMEM, VMEM),
         scratch_shapes=[
             pltpu.VMEM((ROOM * SPAN, LANES), F32),
             pltpu.VMEM((SLOTS * ZSPAN, LANES), F32),
             pltpu.VMEM((SLOTS * ZSPAN, LANES), F32),
             pltpu.VMEM((EDGE * BSPAN, LANES), F32),
+            pltpu.VMEM((EDGE * FLAT, LANES), BF16),
+            pltpu.VMEM((PAIRS, 4 * EDGE, 2 * GRID), BF16),
+            pltpu.VMEM((PAIRS, 2, 2 * GRID, LANES), BF16),
+            pltpu.VMEM((SLABS, 2 * SLOTS, EDGE), BF16),
+            pltpu.VMEM((GRID, 2 * GRID), BF16),
+            pltpu.VMEM((2 * GRID, GRID), BF16),
+            pltpu.VMEM((GRID, GRID), BF16),
+            pltpu.SemaphoreType.DMA((7,)),
         ],
         interpret=interpret,
         name="pair_waves",
         compiler_params=pltpu.CompilerParams(vmem_limit_bytes=20 << 20),
     )(
         scal,
-        near(own_s),
+        away(own_s),
         near(far_box),
         near(scale),
-        rows,
-        depths,
-        jnp.asarray(forward_first()),
-        jnp.asarray(forward_depth()),
-        jnp.asarray(forward_rows()),
-        jnp.asarray(reversal()),
+        away(rows),
+        away(depths),
+        away(jnp.asarray(forward_first())),
+        away(jnp.asarray(forward_depth())),
+        away(jnp.asarray(forward_rows())),
+        away(jnp.asarray(reversal())),
     )
 
 
@@ -415,11 +523,6 @@
     return lax.ppermute(block, "orb", [(i ^ 1, i) for i in range(count)])
 
 
-def to_everyone(shard):
-    copies = jnp.broadcast_to(shard, (lax.axis_size("slab"), *shard.shape))
-    return lax.all_to_all(copies, "slab", split_axis=0, concat_axis=0, tiled=True)
-
-
 def shared(block):
     return lax.all_to_all(block, "slab", split_axis=0, concat_axis=0, tiled=True)
 
@@ -428,27 +531,21 @@
     orbit = lax.axis_index("orb")
     slab = lax.axis_index("slab").astype(jnp.int32)
     even_core = orbit % 2 == 0
-    cells = EDGE * EDGE
-    own = orbitals[0]
-    corner = jnp.pad(offsets.astype(BF16), ((0, 0), (0, LANES - 3)))
-    loaded = jnp.concatenate([own, jnp.broadcast_to(corner, (ROWS, LANES))], axis=1)
+    loaded, copies = load_call(offsets, orbitals[0])
     four = passed_along(loaded, -4)
     two = passed_along(loaded, -2)
-    offered = shared(offer_call(slab[None], own, kernel))
+    own_box = shared(copies)
+    upper, lowest = mirror_call(kernel)
     given = jnp.stack([jnp.where(even_core, two, loaded), jnp.where(even_core, four, two)])
     odd = other_core(given)
     hops = (partners[0] - orbit) % lax.axis_size("orb")
-
-    def chosen(hop):
-        low = jnp.where(hop == 1, odd[0], two)
-        high = jnp.where(hop == 3, odd[1], four)
-        return jnp.where(hop <= 2, low, high)
-
-    picked = jnp.stack([chosen(hops[n]) for n in range(PAIRS)])
-    shifts = picked[:, 0, cells : cells + 3].astype(jnp.int32) - offsets
-    far_box = to_everyone(picked[:, :, :cells])
+    copies, marks = pick_call(hops, two, four, odd)
+    far_box = shared(copies)
+    upper = lax.ppermute(upper, "slab", [(s, SLABS - 1 - s) for s in range(SLABS)])
+    lowest = lax.ppermute(lowest, "slab", [(4, 0), (7, 1), (6, 2), (5, 3)])
+    shifts = marks[:, 0, :3].astype(jnp.int32) - offsets
     scal = jnp.concatenate([slab[None], shifts.reshape(-1)])
-    own_s, scale, there, rows, depths = prepare_call(scal, offered)
+    own_s, scale, there, rows, depths = prepare_call(scal, own_box, kernel, upper, lowest)
     send, here = pair_call(scal, own_s, far_box, scale, rows, depths)
     got = shared(send)
     scal = jnp.concatenate([jnp.zeros((1,), jnp.int32), shifts[:, 1], hops])
@@ -459,7 +556,7 @@
     four_back = passed_along(by_four.astype(BF16), 4).astype(F32)
     two_back = passed_along(by_two.astype(BF16), 2).astype(F32)
     total = mine + jnp.where(even_core, 0.0, crossed[0]) + two_back + four_back
-    return total.reshape(1, ROWS, cells)
+    return total.reshape(1, ROWS, EDGE * EDGE)
 
 
 def solution(mesh):

time: 109 us -> 108 us (level)
  starting transfers between devices: 39.9 us -> 47.1 us
  local copies, waits for them, and re-layouts: 10.8 us -> 4.24 us
  Pallas kernels: 13 us -> 16.7 us
  between operations: 3.79 us -> 0.23 us
  other arithmetic: 2.63 us -> 0.33 us
    ppermute x0 -> x2, waiting for transfers between devices: none -> 13.2 us  [the longest x1 11.7 us: per_device(): lowest = lax.ppermute(lowest, 'slab', [(4, 0), (7, 1), (6, 2), (5, 3)])]
    all_to_all x1 -> x0, waiting for transfers between devices: 8.54 us -> none  [to_everyone(): lax.all_to_all(copies, 'slab', split_axis=0, concat_axis=0, tiled=True)]
    ppermute x0 -> x2, starting transfers between devices: none -> 7.25 us  [the longest x1 5.96 us: per_device(): lax.ppermute(upper, 'slab', [(s, SLABS - 1 - s) for s in range(SLABS)])]
    all_to_all x2 -> x3, waiting for transfers between devices: 17.3 us -> 11.5 us  [shared(): lax.all_to_all(block, 'slab', split_axis=0, concat_axis=0, tiled=True)]
    unnamed x30 -> x18, local copies, waits for them, and re-layouts: 7.55 us -> 3.2 us
    all_to_all x1 -> x0, starting transfers between devices: 3.63 us -> none  [to_everyone(): lax.all_to_all(copies, 'slab', split_axis=0, concat_axis=0, tiled=True)]
    all_to_all x2 -> x3, starting transfers between devices: 8.18 us -> 11.7 us  [shared(): lax.all_to_all(block, 'slab', split_axis=0, concat_axis=0, tiled=True)]
    pallas_call x2 -> x4, Pallas kernels: 2.86 us -> 5.65 us  [the longest x1 2.39 us: prepare_call(): pl.pallas_call(prepare_kernel, out_shape=(far((EDGE * FLAT, LANES), BF16)...]
  transfers between devices with their start and end apart: 9 -> 11, of which waited for: 6 -> 9; matrix products, arithmetic and copies ran while one was open for 2% -> 1% of each run, Pallas kernels for 3% -> 4%
where the time goes in v3:
time: 108 us
  starting transfers between devices  47.1 us (44%)
  waiting for transfers between devices  39.1 us (36%)
  Pallas kernels  16.7 us (15%)
  local copies, waits for them, and re-layouts  4.24 us (4%)
    ppermute x4, starting transfers between devices, passed_along(): lax.ppermute(block, 'orb', [((i - distance) % count, i) for i in range(co...  24.3 us
    ppermute x4, waiting for transfers between devices, passed_along(): lax.ppermute(block, 'orb', [((i - distance) % count, i) for i in range(co...  11.8 us
    all_to_all x3, starting transfers between devices, shared(): lax.all_to_all(block, 'slab', split_axis=0, concat_axis=0, tiled=True)  11.7 us
    ppermute x1, waiting for transfers between devices, per_device(): lowest = lax.ppermute(lowest, 'slab', [(4, 0), (7, 1), (6, 2), (5, 3)])  11.7 us
    all_to_all x3, waiting for transfers between devices, shared(): lax.all_to_all(block, 'slab', split_axis=0, concat_axis=0, tiled=True)  11.5 us
    pallas_call x1, Pallas kernels, pair_call(): pl.pallas_call(pair_kernel, out_shape=(jax.ShapeDtypeStruct((SLABS, PAIRS...  9.98 us
    ppermute x1, starting transfers between devices, per_device(): lax.ppermute(upper, 'slab', [(s, SLABS - 1 - s) for s in range(SLABS)])  5.96 us
    ppermute x2, starting transfers between devices, other_core(): return lax.ppermute(block, 'orb', [(i ^ 1, i) for i in range(count)])  3.84 us
  transfers between devices with their start and end apart: 11, of which 9 were waited for; matrix products, arithmetic and copies ran while one was open for 1% of the time, Pallas kernels for 4%

profile of v3, /device:TPU:16, one launch (start us, length us, event | category | flops | bytes accessed | tf_op | source)
XLA Modules:
  0.0 107.7 jit_solution(9811320495076256351)
XLA Ops:
  0.0 0.0 copy-start.7
  0.0 0.7 copy-done.7
  0.7 0.0 copy-start.6
  0.7 0.8 copy-done.6
  1.5 1.4 %load.1 = (bf16[8,4224]{1,0:T(8,128)(2,1)S(1)}, bf16[8,8,4096]{2,1,0:T(8,128)(2,1)}) custom-call(s32[1,3]{1,0:T(1,128)S(1)} %copy-done.7, bf16[8,4096]{1,0:T(8,128)(2,1)S(1)} %bitcast.20), custom_call_target="tpu_custom_call" | custom-call | tf_op jit(solution)/shard_map/load/pallas_call | solution.py:395
  2.9 14.4 %collective-permute-start.1 = (bf16[8,4224]{1,0:T(8,128)(2,1)S(1)}, bf16[8,4224]{1,0:T(8,128)(2,1)S(1)}, u32[]{:S(2)}, u32[]{:S(2)}) collective-permute-start(bf16[8,4224]{1,0:T(8,128)(2,1)S(1)} %get-tuple-element.21), channel_id=1, source_target_pairs={{32,0},{40,8},{48,16},{56,24},{64,32},{72,40},{80,48},{88,56},{96,... | collective-permute-start | bytes 202760 | tf_op jit(solution)/shard_map/ppermute | solution.py:518
  17.3 4.0 %collective-permute-start = (bf16[8,4224]{1,0:T(8,128)(2,1)S(1)}, bf16[8,4224]{1,0:T(8,128)(2,1)S(1)}, u32[]{:S(2)}, u32[]{:S(2)}) collective-permute-start(bf16[8,4224]{1,0:T(8,128)(2,1)S(1)} %get-tuple-element.21), channel_id=1, source_target_pairs={{16,0},{24,8},{32,16},{40,24},{48,32},{56,40},{64,48},{72,56},{80,... | collective-permute-start | bytes 202760 | tf_op jit(solution)/shard_map/ppermute | solution.py:518
  21.3 4.4 %all-to-all-start = ((bf16[8,8,4096]{2,1,0:T(8,128)(2,1)}), bf16[8,8,4096]{2,1,0:T(8,128)(2,1)S(1)}, u32[]{:S(2)}, u32[]{:S(2)}) async-start(bf16[8,8,4096]{2,1,0:T(8,128)(2,1)} %get-tuple-element.23), calls=%async_computation | async-start | bytes 1048576 | tf_op jit(solution)/shard_map/all_to_all | solution.py:527
  25.8 0.0 collective-permute-done.1.four
  25.8 0.6 collective-permute-done.two
  26.4 0.0 copy-start.8
  26.4 1.9 %collective-permute-start.2 = (bf16[2,8,4224]{2,1,0:T(8,128)(2,1)S(1)}, bf16[2,8,4224]{2,1,0:T(8,128)(2,1)S(1)}, u32[]{:S(2)}, u32[]{:S(2)}) collective-permute-start(bf16[2,8,4224]{2,1,0:T(8,128)(2,1)S(1)} %pad_maximum_fusion), channel_id=1, source_target_pairs={{8,0},{0,8},{24,16},{16,24},{40,32},{32,40},{56,48},{48,56},{72,64... | collective-permute-start | bytes 405512 | tf_op jit(solution)/shard_map/ppermute | solution.py:523
  28.3 0.0 copy-done.8
  28.3 1.3 %collective-permute-done.2.odd = bf16[2,8,4224]{2,1,0:T(8,128)(2,1)S(1)} collective-permute-done((bf16[2,8,4224]{2,1,0:T(8,128)(2,1)S(1)}, bf16[2,8,4224]{2,1,0:T(8,128)(2,1)S(1)}, u32[]{:S(2)}, u32[]{:S(2)}) %collective-permute-start.2) | collective-permute-done | bytes 135200 | tf_op jit(solution)/shard_map/ppermute | solution.py:523
  29.6 1.7 %pick.1 = (bf16[8,2,8,4096]{3,2,1,0:T(8,128)(2,1)}, bf16[2,8,128]{2,1,0:T(8,128)(2,1)S(1)}) custom-call(s32[2]{0:T(128)S(1)} %and_select_fusion.hops, bf16[8,4224]{1,0:T(8,128)(2,1)S(1)} %collective-permute-done.two, bf16[8,4224]{1,0:T(8,128)(2,1)S(1)} %collective-permute-done.1.four, bf16[2,8,4224]{2,1,0:T(8,128)(2,1)S(1)} %collective-permute-done.2.odd), custom_call_target="tpu_custom_call" | custom-call | tf_op jit(solution)/shard_map/pick/pallas_call | solution.py:425
  31.3 3.5 %all-to-all-done.got = bf16[8,8,4096]{2,1,0:T(8,128)(2,1)S(1)} async-done(((bf16[8,8,4096]{2,1,0:T(8,128)(2,1)}), bf16[8,8,4096]{2,1,0:T(8,128)(2,1)S(1)}, u32[]{:S(2)}, u32[]{:S(2)}) %all-to-all-start) | async-done | bytes 524320 | tf_op jit(solution)/shard_map/all_to_all | solution.py:527
  34.9 0.0 copy-start
  34.9 3.7 %all-to-all-start.1 = ((bf16[8,2,8,4096]{3,2,1,0:T(8,128)(2,1)}), bf16[8,2,8,4096]{3,2,1,0:T(8,128)(2,1)S(1)}, u32[]{:S(2)}, u32[]{:S(2)}) async-start(bf16[8,2,8,4096]{3,2,1,0:T(8,128)(2,1)} %get-tuple-element.27), calls=%async_computation.1 | async-start | bytes 2097152 | tf_op jit(solution)/shard_map/all_to_all | solution.py:527
  38.6 0.0 copy-done
  38.6 0.0 copy-start.2
  38.6 0.2 mirror.1
  38.8 6.0 %collective-permute-start.3 = (bf16[8,128,128]{2,1,0:T(8,128)(2,1)S(1)}, bf16[8,128,128]{2,1,0:T(8,128)(2,1)S(1)}, u32[]{:S(2)}, u32[]{:S(2)}) collective-permute-start(bf16[8,128,128]{2,1,0:T(8,128)(2,1)S(1)} %get-tuple-element.24), channel_id=1, source_target_pairs={{0,7},{1,6},{2,5},{3,4},{4,3},{5,2},{6,1},{7,0},{8,15},{9,14},{10,... | collective-permute-start | bytes 786440 | tf_op jit(solution)/shard_map/ppermute | solution.py:544
  44.8 1.3 %collective-permute-start.4 = (bf16[128,128]{1,0:T(8,128)(2,1)S(1)}, bf16[128,128]{1,0:T(8,128)(2,1)S(1)}, u32[]{:S(2)}, u32[]{:S(2)}) collective-permute-start(bf16[128,128]{1,0:T(8,128)(2,1)S(1)} %get-tuple-element.25), channel_id=1, source_target_pairs={{4,0},{7,1},{6,2},{5,3},{12,8},{15,9},{14,10},{13,11},{20,16},{23,... | collective-permute-start | bytes 98312 | tf_op jit(solution)/shard_map/ppermute | solution.py:545
  46.1 0.1 sub.30
  46.2 0.1 reshape.28
  46.3 0.1 pad_add_fusion.1.scal
  46.3 11.7 %collective-permute-done.4.lowest = bf16[128,128]{1,0:T(8,128)(2,1)S(1)} collective-permute-done((bf16[128,128]{1,0:T(8,128)(2,1)S(1)}, bf16[128,128]{1,0:T(8,128)(2,1)S(1)}, u32[]{:S(2)}, u32[]{:S(2)}) %collective-permute-start.4) | collective-permute-done | bytes 32800 | tf_op jit(solution)/shard_map/ppermute | solution.py:545
  58.0 1.6 %collective-permute-done.3.upper = bf16[8,128,128]{2,1,0:T(8,128)(2,1)S(1)} collective-permute-done((bf16[8,128,128]{2,1,0:T(8,128)(2,1)S(1)}, bf16[8,128,128]{2,1,0:T(8,128)(2,1)S(1)}, u32[]{:S(2)}, u32[]{:S(2)}) %collective-permute-start.3) | collective-permute-done | bytes 262176 | tf_op jit(solution)/shard_map/ppermute | solution.py:544
  59.6 0.0 copy-done.2
  59.6 0.0 copy-start.4
  59.6 0.8 copy-done.4
  60.4 0.0 copy-start.5
  60.4 0.8 copy-done.5
  61.3 2.4 %prepare.1 = (bf16[2048,128]{1,0:T(8,128)(2,1)}, f32[9,128,128]{2,1,0:T(8,128)S(1)}, bf16[2,8,32,128]{3,2,1,0:T(8,128)(2,1)}, bf16[2,256,256]{2,1,0:T(8,128)(2,1)}, bf16[2,2,256,128]{3,2,1,0:T(8,128)(2,1)}) custom-call(s32[7]{0:T(128)S(1)} %pad_add_fusion.1.scal, bf16[8,8,4096]{2,1,0:T(8,128)(2,1)S(1)} %all-to-all-done.got, f32[128,16,128]{2,1,0:T(8,128)S(1)} %copy-done, ...), custom_call_target="tpu_custom_call" | custom-call | tf_op jit(solution)/shard_map/prepare/pallas_call | solution.py:441
  63.6 0.0 all-to-all-done.1.far_in
  63.6 10.0 %pair_waves.1 = (bf16[8,2,8,16,128]{4,3,2,1,0:T(8,128)(2,1)}, bf16[2,8,32,128]{3,2,1,0:T(8,128)(2,1)S(1)}) custom-call(s32[7]{0:T(128)S(1)} %pad_add_fusion.1.scal, bf16[2048,128]{1,0:T(8,128)(2,1)} %get-tuple-element.26.own_h, bf16[8,2,8,4096]{3,2,1,0:T(8,128)(2,1)S(1)} %all-to-all-done.1.far_in, f32[9,128,128]{2,1,0:T(8,128)S(1)} %get-tuple-element.28.scale_t, ...), custom_call_target="tpu_custom_call" | custom-call | tf_op jit(solution)/shard_map/pair_waves/pallas_call | solution.py:460
  73.6 0.0 copy-start.1
  73.6 0.0 copy-start.3
  73.7 3.6 %all-to-all-start.2 = ((bf16[8,2,8,16,128]{4,3,2,1,0:T(8,128)(2,1)}), bf16[8,2,8,16,128]{4,3,2,1,0:T(8,128)(2,1)S(1)}, u32[]{:S(2)}, u32[]{:S(2)}) async-start(bf16[8,2,8,16,128]{4,3,2,1,0:T(8,128)(2,1)} %get-tuple-element.31), calls=%async_computation.2 | async-start | bytes 1048576 | tf_op jit(solution)/shard_map/all_to_all | solution.py:527
  77.3 0.2 slice_reduce_fusion
  77.5 0.1 pad_add_fusion.scal
  77.6 7.9 %all-to-all-done.2.got = bf16[8,2,8,16,128]{4,3,2,1,0:T(8,128)(2,1)S(1)} async-done(((bf16[8,2,8,16,128]{4,3,2,1,0:T(8,128)(2,1)}), bf16[8,2,8,16,128]{4,3,2,1,0:T(8,128)(2,1)S(1)}, u32[]{:S(2)}, u32[]{:S(2)}) %all-to-all-start.2) | async-done | bytes 524320 | tf_op jit(solution)/shard_map/all_to_all | solution.py:527
  85.5 0.0 copy-done.1
  85.5 0.0 copy-done.3
  85.5 1.1 %pair_terms.1 = (f32[8,32,128]{2,1,0:T(8,128)S(1)}, bf16[2,8,32,128]{3,2,1,0:T(8,128)(2,1)S(1)}, bf16[2,8,32,128]{3,2,1,0:T(8,128)(2,1)S(1)}) custom-call(s32[5]{0:T(128)S(1)} %pad_add_fusion.scal, bf16[8,2,8,16,128]{4,3,2,1,0:T(8,128)(2,1)S(1)} %all-to-all-done.2.got, bf16[2,8,32,128]{3,2,1,0:T(8,128)(2,1)S(1)} %get-tuple-element.32.here, ...), custom_call_target="tpu_custom_call" | custom-call | tf_op jit(solution)/shard_map/pair_terms/pallas_call | solution.py:500
  86.6 1.9 %collective-permute-start.5 = (bf16[2,8,32,128]{3,2,1,0:T(8,128)(2,1)S(1)}, bf16[2,8,32,128]{3,2,1,0:T(8,128)(2,1)S(1)}, u32[]{:S(2)}, u32[]{:S(2)}) collective-permute-start(bf16[2,8,32,128]{3,2,1,0:T(8,128)(2,1)S(1)} %get-tuple-element.35), channel_id=1, source_target_pairs={{8,0},{0,8},{24,16},{16,24},{40,32},{32,40},{56,48},{48,56},{72,64... | collective-permute-start | bytes 393224 | tf_op jit(solution)/shard_map/ppermute | solution.py:523
  88.5 1.3 %collective-permute-done.5 = bf16[2,8,32,128]{3,2,1,0:T(8,128)(2,1)S(1)} collective-permute-done((bf16[2,8,32,128]{3,2,1,0:T(8,128)(2,1)S(1)}, bf16[2,8,32,128]{3,2,1,0:T(8,128)(2,1)S(1)}, u32[]{:S(2)}, u32[]{:S(2)}) %collective-permute-start.5) | collective-permute-done | bytes 131104 | tf_op jit(solution)/shard_map/ppermute | solution.py:523
  89.9 3.9 %collective-permute-start.6 = (bf16[8,32,128]{2,1,0:T(8,128)(2,1)S(1)}, bf16[8,32,128]{2,1,0:T(8,128)(2,1)S(1)}, u32[]{:S(2)}, u32[]{:S(2)}) collective-permute-start(bf16[8,32,128]{2,1,0:T(8,128)(2,1)S(1)} %get-tuple-element.37), channel_id=1, source_target_pairs={{496,0},{504,8},{0,16},{8,24},{16,32},{24,40},{32,48},{40,56},{48,... | collective-permute-start | bytes 196616 | tf_op jit(solution)/shard_map/ppermute | solution.py:518
  93.8 1.9 %collective-permute-start.7 = (bf16[8,32,128]{2,1,0:T(8,128)(2,1)S(1)}, bf16[8,32,128]{2,1,0:T(8,128)(2,1)S(1)}, u32[]{:S(2)}, u32[]{:S(2)}) collective-permute-start(bf16[8,32,128]{2,1,0:T(8,128)(2,1)S(1)} %get-tuple-element.38), channel_id=1, source_target_pairs={{480,0},{488,8},{496,16},{504,24},{0,32},{8,40},{16,48},{24,56},{3... | collective-permute-start | bytes 196616 | tf_op jit(solution)/shard_map/ppermute | solution.py:518
  95.8 1.8 %collective-permute-done.6 = bf16[8,32,128]{2,1,0:T(8,128)(2,1)S(1)} collective-permute-done((bf16[8,32,128]{2,1,0:T(8,128)(2,1)S(1)}, bf16[8,32,128]{2,1,0:T(8,128)(2,1)S(1)}, u32[]{:S(2)}, u32[]{:S(2)}) %collective-permute-start.6) | collective-permute-done | bytes 65568 | tf_op jit(solution)/shard_map/ppermute | solution.py:518
  97.6 9.4 %collective-permute-done.7 = bf16[8,32,128]{2,1,0:T(8,128)(2,1)S(1)} collective-permute-done((bf16[8,32,128]{2,1,0:T(8,128)(2,1)S(1)}, bf16[8,32,128]{2,1,0:T(8,128)(2,1)S(1)}, u32[]{:S(2)}, u32[]{:S(2)}) %collective-permute-start.7) | collective-permute-done | bytes 65568 | tf_op jit(solution)/shard_map/ppermute | solution.py:518
  107.0 0.7 reshape.26
  (11 shorter events, 0.2 us)
Async XLA Ops:
  0.0 0.7 copy-start.7
  0.7 0.8 copy-start.6
  2.9 22.9 %collective-permute-start.1 = (bf16[8,4224]{1,0:T(8,128)(2,1)S(1)}, bf16[8,4224]{1,0:T(8,128)(2,1)S(1)}, u32[]{:S(2)}, u32[]{:S(2)}) collective-permute-start(bf16[8,4224]{1,0:T(8,128)(2,1)S(1)} %get-tuple-element.21), channel_id=1, source_target_pairs={{32,0},{40,8},{48,16},{56,24},{64,32},{72,40},{80,48},{88,56},{96,... | collective-permute-start | bytes 202760 | tf_op jit(solution)/shard_map/ppermute | solution.py:518
  17.3 9.0 %collective-permute-start = (bf16[8,4224]{1,0:T(8,128)(2,1)S(1)}, bf16[8,4224]{1,0:T(8,128)(2,1)S(1)}, u32[]{:S(2)}, u32[]{:S(2)}) collective-permute-start(bf16[8,4224]{1,0:T(8,128)(2,1)S(1)} %get-tuple-element.21), channel_id=1, source_target_pairs={{16,0},{24,8},{32,16},{40,24},{48,32},{56,40},{64,48},{72,56},{80,... | collective-permute-start | bytes 202760 | tf_op jit(solution)/shard_map/ppermute | solution.py:518
  21.3 13.5 %all-to-all-start = ((bf16[8,8,4096]{2,1,0:T(8,128)(2,1)}), bf16[8,8,4096]{2,1,0:T(8,128)(2,1)S(1)}, u32[]{:S(2)}, u32[]{:S(2)}) async-start(bf16[8,8,4096]{2,1,0:T(8,128)(2,1)} %get-tuple-element.23), calls=%async_computation | async-start | bytes 1048576 | tf_op jit(solution)/shard_map/all_to_all | solution.py:527
  26.4 2.0 %copy-start.8 = (s32[1,2]{1,0:T(1,128)S(1)}, s32[1,2]{1,0:T(1,128)}, u32[]{:S(2)}) copy-start(s32[1,2]{1,0:T(1,128)} %param.13) | copy-start | bytes 28
  26.4 3.2 %collective-permute-start.2 = (bf16[2,8,4224]{2,1,0:T(8,128)(2,1)S(1)}, bf16[2,8,4224]{2,1,0:T(8,128)(2,1)S(1)}, u32[]{:S(2)}, u32[]{:S(2)}) collective-permute-start(bf16[2,8,4224]{2,1,0:T(8,128)(2,1)S(1)} %pad_maximum_fusion), channel_id=1, source_target_pairs={{8,0},{0,8},{24,16},{16,24},{40,32},{32,40},{56,48},{48,56},{72,64... | collective-permute-start | bytes 405512 | tf_op jit(solution)/shard_map/ppermute | solution.py:523
  34.9 3.7 %copy-start = (f32[128,16,128]{2,1,0:T(8,128)S(1)}, f32[128,16,128]{2,1,0:T(8,128)}, u32[]{:S(2)}) copy-start(f32[128,16,128]{2,1,0:T(8,128)} %kern.3) | copy-start | bytes 3145732
  34.9 28.8 %all-to-all-start.1 = ((bf16[8,2,8,4096]{3,2,1,0:T(8,128)(2,1)}), bf16[8,2,8,4096]{3,2,1,0:T(8,128)(2,1)S(1)}, u32[]{:S(2)}, u32[]{:S(2)}) async-start(bf16[8,2,8,4096]{3,2,1,0:T(8,128)(2,1)} %get-tuple-element.27), calls=%async_computation.1 | async-start | bytes 2097152 | tf_op jit(solution)/shard_map/all_to_all | solution.py:527
  38.6 21.0 %copy-start.2 = (bf16[128,128]{1,0:T(8,128)(2,1)S(1)}, bf16[128,128]{1,0:T(8,128)(2,1)}, u32[]{:S(2)}) copy-start(bf16[128,128]{1,0:T(8,128)(2,1)} %constant.55.clone.flip_t.flip_h) | copy-start | bytes 98308
  38.8 20.8 %collective-permute-start.3 = (bf16[8,128,128]{2,1,0:T(8,128)(2,1)S(1)}, bf16[8,128,128]{2,1,0:T(8,128)(2,1)S(1)}, u32[]{:S(2)}, u32[]{:S(2)}) collective-permute-start(bf16[8,128,128]{2,1,0:T(8,128)(2,1)S(1)} %get-tuple-element.24), channel_id=1, source_target_pairs={{0,7},{1,6},{2,5},{3,4},{4,3},{5,2},{6,1},{7,0},{8,15},{9,14},{10,... | collective-permute-start | bytes 786440 | tf_op jit(solution)/shard_map/ppermute | solution.py:544
  44.8 13.2 %collective-permute-start.4 = (bf16[128,128]{1,0:T(8,128)(2,1)S(1)}, bf16[128,128]{1,0:T(8,128)(2,1)S(1)}, u32[]{:S(2)}, u32[]{:S(2)}) collective-permute-start(bf16[128,128]{1,0:T(8,128)(2,1)S(1)} %get-tuple-element.25), channel_id=1, source_target_pairs={{4,0},{7,1},{6,2},{5,3},{12,8},{15,9},{14,10},{13,11},{20,16},{23,... | collective-permute-start | bytes 98312 | tf_op jit(solution)/shard_map/ppermute | solution.py:545
  59.6 0.8 copy-start.4
  60.4 0.8 copy-start.5
  73.6 11.9 %copy-start.1 = (f32[512,128]{1,0:T(8,128)S(1)}, f32[512,128]{1,0:T(8,128)}, u32[]{:S(2)}) copy-start(f32[512,128]{1,0:T(8,128)} %constant.61.clone.last_t) | copy-start | bytes 786436
  73.6 11.9 %copy-start.3 = (bf16[2,8,32,128]{3,2,1,0:T(8,128)(2,1)S(1)}, bf16[2,8,32,128]{3,2,1,0:T(8,128)(2,1)}, u32[]{:S(2)}) copy-start(bf16[2,8,32,128]{3,2,1,0:T(8,128)(2,1)} %get-tuple-element.33.there) | copy-start | bytes 393220
  73.7 11.9 %all-to-all-start.2 = ((bf16[8,2,8,16,128]{4,3,2,1,0:T(8,128)(2,1)}), bf16[8,2,8,16,128]{4,3,2,1,0:T(8,128)(2,1)S(1)}, u32[]{:S(2)}, u32[]{:S(2)}) async-start(bf16[8,2,8,16,128]{4,3,2,1,0:T(8,128)(2,1)} %get-tuple-element.31), calls=%async_computation.2 | async-start | bytes 1048576 | tf_op jit(solution)/shard_map/all_to_all | solution.py:527
  86.6 3.2 %collective-permute-start.5 = (bf16[2,8,32,128]{3,2,1,0:T(8,128)(2,1)S(1)}, bf16[2,8,32,128]{3,2,1,0:T(8,128)(2,1)S(1)}, u32[]{:S(2)}, u32[]{:S(2)}) collective-permute-start(bf16[2,8,32,128]{3,2,1,0:T(8,128)(2,1)S(1)} %get-tuple-element.35), channel_id=1, source_target_pairs={{8,0},{0,8},{24,16},{16,24},{40,32},{32,40},{56,48},{48,56},{72,64... | collective-permute-start | bytes 393224 | tf_op jit(solution)/shard_map/ppermute | solution.py:523
  89.9 7.6 %collective-permute-start.6 = (bf16[8,32,128]{2,1,0:T(8,128)(2,1)S(1)}, bf16[8,32,128]{2,1,0:T(8,128)(2,1)S(1)}, u32[]{:S(2)}, u32[]{:S(2)}) collective-permute-start(bf16[8,32,128]{2,1,0:T(8,128)(2,1)S(1)} %get-tuple-element.37), channel_id=1, source_target_pairs={{496,0},{504,8},{0,16},{8,24},{16,32},{24,40},{32,48},{40,56},{48,... | collective-permute-start | bytes 196616 | tf_op jit(solution)/shard_map/ppermute | solution.py:518
  93.8 13.2 %collective-permute-start.7 = (bf16[8,32,128]{2,1,0:T(8,128)(2,1)S(1)}, bf16[8,32,128]{2,1,0:T(8,128)(2,1)S(1)}, u32[]{:S(2)}, u32[]{:S(2)}) collective-permute-start(bf16[8,32,128]{2,1,0:T(8,128)(2,1)S(1)} %get-tuple-element.38), channel_id=1, source_target_pairs={{480,0},{488,8},{496,16},{504,24},{0,32},{8,40},{16,48},{24,56},{3... | collective-permute-start | bytes 196616 | tf_op jit(solution)/shard_map/ppermute | solution.py:518

commit v4 on v0

v4 whole, which is shorter than its diff:
```python
import jax
import jax.numpy as jnp
import numpy as np
from jax import lax
from jax.experimental import pallas as pl
from jax.experimental.pallas import tpu as pltpu
from jax.sharding import PartitionSpec as P


EDGE = 64
GRID = 128
HALF = 32
SLABS = 8
ROWS = EDGE // SLABS
WAVES = GRID // SLABS
PAIRS = 2
LANES = 128
CELLS = EDGE * EDGE
FLAT = CELLS // LANES
PAD = 24
SPAN = PAD + FLAT + PAD + 1
SLOTS = 8
TWIN = 2 * SLOTS
ZSPAN = EDGE + 1
BSPAN = SLOTS + 1
RSPAN = FLAT + 1
F32 = jnp.float32
BF16 = jnp.bfloat16


def full_tables():
    index = np.arange(GRID)
    angle = (index[:, None] * index[None, :] % GRID) * (2.0 * np.pi / GRID)
    rounded = lambda a: a.astype(np.float32).astype(BF16).astype(np.float32)
    return rounded(np.cos(angle)), rounded(np.sin(angle))


COS, SIN = full_tables()
SIGN = COS[:, EDGE]
OWN_WAVES = np.array([[WAVES * s + (s >= SLABS // 2) + q for q in range(SLOTS)] for s in range(SLABS)])


def forward_first():
    waves = OWN_WAVES.reshape(-1)
    im = -SIN[:, waves]
    im[:, 0] = SIGN
    return np.concatenate([COS[:, waves], im], axis=1)


def backward_last():
    c, s = COS.copy(), SIN.copy()
    s[:, 0] = -SIGN
    out = []
    for par in range(2):
        for table in (c, s):
            wide = np.zeros((GRID, SLABS, 2, SLOTS), np.float32)
            wide[:, :, par] = table[:, OWN_WAVES]
            out.append(wide.reshape(GRID, GRID))
    return np.concatenate(out)


def reversal():
    flip = np.zeros((GRID, GRID), np.float32)
    flip[np.arange(GRID), -np.arange(GRID) % GRID] = 1.0
    return flip.astype(BF16)


def dot(a, b):
    return jnp.dot(a, b, preferred_element_type=F32)


def swapped(x):
    return pltpu.roll(x, EDGE, axis=1)


def lanes_of(shape):
    return lax.broadcasted_iota(jnp.int32, shape, 1)


def low_half(shape):
    return lanes_of(shape) < EDGE


def shifted(ref, base, d1, d2):
    flat = d1 * EDGE + d2
    turn = flat & (LANES - 1)
    jump = (flat - turn) // LANES
    here = pltpu.roll(ref[pl.ds(base - jump, FLAT), :], turn, axis=1)
    before = pltpu.roll(ref[pl.ds(base - jump - 1, FLAT), :], turn, axis=1)
    lane = lanes_of((FLAT, LANES))
    depth = (lane & (EDGE - 1)) - d2
    return jnp.where((depth >= 0) & (depth < EDGE), jnp.where(lane >= turn, here, before), 0.0)


def clear_edges(ref, rows):
    zeros = jnp.zeros((PAD + 1, LANES), F32)
    for c in range(rows):
        ref[c * SPAN : c * SPAN + PAD, :] = zeros[:PAD]
        ref[c * SPAN + PAD + FLAT : (c + 1) * SPAN, :] = zeros


def load_kernel(corner, own, loaded, copies):
    cells = own[...]
    loaded[:, :CELLS] = cells
    lane = lanes_of((ROWS, LANES))
    mark = jnp.zeros((ROWS, LANES), F32)
    for k in range(3):
        mark = jnp.where(lane == k, corner[0, k].astype(F32), mark)
    loaded[:, CELLS:] = mark.astype(BF16)
    for t in range(SLABS):
        copies[t] = cells


def mirror_kernel(kern, upper, lowest):
    kern_flat = kern.reshape(GRID * WAVES, LANES)
    for q in range(SLOTS):
        upper[q] = kern_flat[pl.ds(SLOTS + q, GRID, stride=WAVES), :].astype(BF16)
    lowest[...] = kern_flat[pl.ds(0, GRID, stride=WAVES), :].astype(BF16)


def start_kernel(info, partners, corner, two, four, odd, own_in, first_t, send, there_out, with_out, scal, own_s, part_s):
    slab, orbit = info[0], info[1]
    clear_edges(own_s, EDGE)
    for t in range(SLABS):
        for k in range(FLAT):
            piece = own_in[t, :, k * LANES : (k + 1) * LANES].astype(F32)
            own_s[pl.ds(t * ROWS * SPAN + PAD + k, ROWS, stride=SPAN), :] = piece
    scal[0] = slab
    low_d = low_half((FLAT, LANES))
    low_w = low_half((EDGE, LANES))
    lane = lanes_of((ROWS, LANES))
    weight = jnp.where(lane == 0, 1.0, jnp.where(lane == 1, 64.0, jnp.where(lane == 2, 4096.0, 0.0)))
    for n in range(PAIRS):
        hop = (partners[0, n] - orbit) & (EDGE - 1)
        for k in range(FLAT + 1):
            at = slice(k * LANES, (k + 1) * LANES)
            low = jnp.where(hop == 1, odd[0, :, at].astype(F32), two[:, at].astype(F32))
            high = jnp.where(hop == 3, odd[1, :, at].astype(F32), four[:, at].astype(F32))
            value = jnp.where(hop <= 2, low, high)
            if k < FLAT:
                part_s[pl.ds(k, ROWS, stride=RSPAN), :] = value
            else:
                code = jnp.sum(value[:1] * weight[:1]).astype(jnp.int32)
        d0 = (code & 63) - corner[0, 0]
        d1 = ((code >> 6) & 63) - corner[0, 1]
        d2 = (code >> 12) - corner[0, 2]
        scal[1 + 3 * n] = d0
        scal[2 + 3 * n] = d1
        scal[3 + 3 * n] = d2
        scal[7 + n] = hop
        halves = [first_t[pl.ds(HALF + d1 + par, FLAT, stride=2), :] for par in range(2)]
        first = jnp.concatenate(halves, axis=0).T.astype(BF16)
        sides = []
        for r in range(ROWS):
            source = slab * ROWS + r + d0
            inside = jnp.logical_and(source >= 0, source < EDGE)
            base = jnp.clip(source, 0, EDGE - 1) * SPAN + PAD
            there = jnp.where(inside, shifted(own_s, base, -d1, -d2), 0.0)
            part = part_s[r * RSPAN : r * RSPAN + FLAT, :]
            there_out[n, r] = there.astype(BF16)
            with_out[n, r] = part.astype(BF16)
            sides.append(there * part)
        for quad in range(ROWS // 4):
            columns = []
            for half in range(2):
                a, b = sides[quad * 4 + half * 2], sides[quad * 4 + half * 2 + 1]
                even = jnp.where(low_d, a, swapped(b)).astype(BF16)
                odd_part = jnp.where(low_d, swapped(a), b).astype(BF16)
                columns.append(jnp.concatenate([even, odd_part], axis=0))
            y = dot(first, jnp.concatenate(columns, axis=1))
            for half in range(2):
                re = y[:EDGE, half * LANES : (half + 1) * LANES]
                im = y[EDGE:, half * LANES : (half + 1) * LANES]
                wave_a = jnp.where(low_w, re, swapped(im))
                wave_b = jnp.where(low_w, swapped(re), im)
                for s in range(SLABS):
                    at = slice(s * SLOTS, (s + 1) * SLOTS)
                    both = jnp.concatenate([wave_a[at], wave_b[at]], axis=0)
                    send[s, n, quad * 2 + half] = both.astype(BF16)


def prepare_kernel(scal, kern, upper, lowest, flip_t, cos_f, sin_f, scale_out, rowf_out, depf_out, rowb_out, depb_out):
    slab = scal[0]
    flip = flip_t[...]

    def reversed_plane(plane):
        return dot(dot(flip, plane).astype(BF16), flip)

    kern_flat = kern.reshape(GRID * WAVES, LANES)
    first = slab == 0
    lower = slab < SLABS // 2
    for q in range(SLOTS):
        here = kern_flat[pl.ds(jnp.where(lower, q, q + 1), GRID, stride=WAVES), :]
        if q:
            there = upper[jnp.where(lower, SLOTS - q, SLOTS - 1 - q)]
            scale_out[q] = here + reversed_plane(there)
        else:
            here = here.astype(BF16).astype(F32)
            low = lowest[...].astype(F32)
            there = jnp.where(lower, low, upper[SLOTS - 1].astype(F32))
            both = here + reversed_plane(jnp.where(first, here, there).astype(BF16))
            top = low + reversed_plane(lowest[...])
            scale_out[0] = jnp.where(first, 0.25 * (both + top), both)
            scale_out[SLOTS] = jnp.where(first, 0.25 * (both - top), 0.0)
    half = low_half((GRID, LANES))

    def by_wave(shift):
        turn = (GRID - HALF - shift) & (LANES - 1)
        c = pltpu.roll(cos_f[...], turn, axis=1)
        s = pltpu.roll(sin_f[...], turn, axis=1)
        return jnp.where(half, c, swapped(s)).astype(BF16), jnp.where(half, -s, swapped(c)).astype(BF16)

    for n in range(PAIRS):
        d0, d2 = scal[1 + 3 * n], scal[3 + 3 * n]
        rowf_out[n, :GRID, :], rowf_out[n, GRID:, :] = by_wave(d0)
        depb_out[n, :GRID, :], depb_out[n, GRID:, :] = by_wave(d2)
        c, s = (ref[pl.ds(HALF + d0, EDGE), :].astype(BF16) for ref in (cos_f, sin_f))
        rowb_out[n] = jnp.concatenate(
            [jnp.concatenate([c, -s], axis=1), jnp.concatenate([s, c], axis=1)], axis=0
        )
        c, s = (ref[pl.ds(HALF + d2, EDGE), :].astype(BF16) for ref in (cos_f, sin_f))
        depf_out[n] = jnp.concatenate(
            [jnp.concatenate([c, -s], axis=1), jnp.concatenate([s, c], axis=1)], axis=0
        )


def wave_kernel(got, scale_t, rowf_h, depf_h, rowb_h, depb_h, flip_h, send, zr, zi, back_s, rowf_t, depf_t, rowb_t, depb_t, flip_t, sems):
    held = (depf_h, rowf_h, rowb_h, depb_h, flip_h)
    local = (depf_t, rowf_t, rowb_t, depb_t, flip_t)
    loads = [pltpu.make_async_copy(a, b, sems.at[i]) for i, (a, b) in enumerate(zip(held, local))]
    for load in loads:
        load.start()
    for load in loads:
        load.wait()
    flip = flip_t[...]
    for n in range(PAIRS):
        at_z = n * SLOTS * ZSPAN
        at_b = n * EDGE * BSPAN
        depth_m = depf_t[n]
        rows_m = rowf_t[n]
        for t in range(SLABS):
            block = jnp.concatenate([got[t, n, p] for p in range(ROWS // 2)], axis=0)
            z = dot(block, depth_m)
            for r in range(ROWS):
                part = z[r * SLOTS : (r + 1) * SLOTS]
                zr[pl.ds(at_z + t * ROWS + r, SLOTS, stride=ZSPAN), :] = part[:, :LANES]
                zi[pl.ds(at_z + t * ROWS + r, SLOTS, stride=ZSPAN), :] = part[:, LANES:]

        def plane(w):
            at = slice(at_z + w * ZSPAN, at_z + w * ZSPAN + EDGE)
            return jnp.concatenate([zr[at, :], zi[at, :]], axis=0).astype(BF16)

        for w0 in range(0, SLOTS, 2):
            x = dot(rows_m, jnp.concatenate([plane(w0), plane(w0 + 1)], axis=1))
            weight = jnp.concatenate([scale_t[w0], scale_t[w0 + 1]], axis=1)
            re, im = x[:GRID] * weight, x[GRID:] * weight
            if w0 == 0:
                edge = x[:, :LANES].astype(BF16)
                back_re = dot(dot(flip, edge[:GRID]).astype(BF16), flip)
                back_im = dot(dot(flip, edge[GRID:]).astype(BF16), flip)
                extra = scale_t[SLOTS]
                re = jnp.concatenate([re[:, :LANES] + extra * back_re, re[:, LANES:]], axis=1)
                im = jnp.concatenate([im[:, :LANES] - extra * back_im, im[:, LANES:]], axis=1)
            v = dot(rowb_t[n], jnp.concatenate([re, im], axis=0).astype(BF16)).astype(BF16)
            re, im = v[:EDGE], v[EDGE:]
            left = jnp.concatenate(
                [
                    jnp.concatenate([re[:, :LANES], im[:, :LANES]], axis=1),
                    jnp.concatenate([re[:, LANES:], im[:, LANES:]], axis=1),
                ],
                axis=0,
            )
            r = dot(left, depb_t[n])
            for h in range(2):
                back_s[pl.ds(at_b + w0 + h, EDGE, stride=BSPAN), :] = r[h * EDGE : (h + 1) * EDGE]
        for t in range(SLABS):
            for p in range(ROWS // 2):
                at = at_b + (t * ROWS + 2 * p) * BSPAN
                both = jnp.concatenate([back_s[at : at + SLOTS, :], back_s[at + BSPAN : at + BSPAN + SLOTS, :]], axis=0)
                send[t, n, p] = both.astype(BF16)


def term_kernel(scal, got, there, withs, last_t, move_out, odd_out, even_out, far_s, own_s, sum_s):
    slab = scal[0]
    low = low_half((FLAT, LANES))
    scale = 1.0 / GRID**3
    clear_edges(own_s, PAIRS * ROWS)
    blank = jnp.zeros((FLAT, LANES), F32)
    for c in range(EDGE):
        sum_s[HALF + c] = blank
    for n in range(PAIRS):
        d0, d1, d2 = scal[1 + 3 * n], scal[2 + 3 * n], scal[3 + 3 * n]
        parts = [
            last_t[pl.ds((2 * row + f) * GRID + HALF + d1 + par, FLAT, stride=2), :]
            for row in range(2)
            for f in range(2)
            for par in range(2)
        ]
        tab = jnp.concatenate(parts, axis=0).astype(BF16)
        for quad in range(ROWS // 4):
            data = [jnp.concatenate([got[t, n, quad * 2 + h] for t in range(SLABS)], axis=0) for h in range(2)]
            g = dot(tab, jnp.concatenate(data, axis=1))
            for h in range(2):
                for par in range(2):
                    r = quad * 4 + h * 2 + par
                    part = g[par * GRID : (par + 1) * GRID, h * LANES : (h + 1) * LANES]
                    c0, c1, s0, s1 = (part[f * FLAT : (f + 1) * FLAT] for f in range(4))
                    pot = jnp.where(low, c0 - swapped(s0), swapped(c1) - s1) * scale
                    far_s[n, r] = pot * there[n, r].astype(F32)
                    base = (n * ROWS + r) * SPAN + PAD
                    own_s[base : base + FLAT, :] = pot * withs[n, r].astype(F32)
        for r in range(ROWS):
            base = (n * ROWS + r) * SPAN + PAD
            at = HALF + slab * ROWS + r + d0
            sum_s[at] = sum_s[at] + shifted(own_s, base, d1, d2)
    for t in range(SLABS):
        for r in range(ROWS):
            move_out[t, r] = sum_s[HALF + t * ROWS + r].astype(BF16)
    hops = [scal[7 + n] for n in range(PAIRS)]
    for e in range(1, 5):
        target = odd_out if e % 2 else even_out
        for row in range(ROWS):
            value = sum(jnp.where(hops[n] == e, far_s[n, row], 0.0) for n in range(PAIRS))
            target[(e - 1) // 2, row] = value.astype(BF16)


def final_kernel(odd_core, moved, crossed, two, four, out, total_s):
    keep = odd_core[0] == 1
    for r in range(ROWS):
        total = two[r].astype(F32) + four[r].astype(F32) + jnp.where(keep, crossed[0, r].astype(F32), 0.0)
        for t in range(SLABS):
            total = total + moved[t, r].astype(F32)
        total_s[r * RSPAN : r * RSPAN + FLAT, :] = total
    for k in range(FLAT):
        out[:, k * LANES : (k + 1) * LANES] = total_s[pl.ds(k, ROWS, stride=RSPAN), :]


VMEM = pl.BlockSpec(memory_space=pltpu.VMEM)
SMEM = pl.BlockSpec(memory_space=pltpu.SMEM)
HBM = pl.BlockSpec(memory_space=pltpu.HBM)


def kept(shape, dtype):
    return pltpu.VMEM(shape, dtype)


def far(shape, dtype):
    return pltpu.HBM(shape, dtype)


def away(x):
    return pltpu.with_memory_space_constraint(x, pltpu.HBM)


def near(x):
    return pltpu.with_memory_space_constraint(x, pltpu.VMEM)


def call(kernel, mib, in_specs, out_shape, out_specs, scratch, args):
    return pl.pallas_call(
        kernel,
        out_shape=out_shape,
        in_specs=in_specs,
        out_specs=out_specs,
        scratch_shapes=scratch,
        interpret=INTERPRET,
        compiler_params=pltpu.CompilerParams(vmem_limit_bytes=mib << 20),
    )(*args)


INTERPRET = False
ROWBOX = (PAIRS, ROWS, FLAT, LANES)
PACKET = (SLABS, PAIRS, ROWS // 2, TWIN, LANES)


def load_call(offsets, own):
    shapes = (kept((ROWS, CELLS + LANES), BF16), kept((SLABS, ROWS, CELLS), BF16))
    return call(load_kernel, 8, [SMEM, VMEM], shapes, (VMEM,) * 2, (), (offsets, own))


def mirror_call(kernel):
    shapes = (kept((SLOTS, GRID, LANES), BF16), kept((GRID, LANES), BF16))
    return call(mirror_kernel, 8, [VMEM], shapes, (VMEM,) * 2, (), (kernel,))


def start_call(info, partners, offsets, two, four, odd, own_box):
    shapes = (far(PACKET, BF16), far(ROWBOX, BF16), far(ROWBOX, BF16), jax.ShapeDtypeStruct((9,), jnp.int32))
    scratch = (pltpu.VMEM((EDGE * SPAN, LANES), F32), pltpu.VMEM((ROWS * RSPAN, LANES), F32))
    args = (info, partners, offsets, near(two), near(four), near(odd), near(own_box), jnp.asarray(forward_first()))
    return call(start_kernel, 12, [SMEM] * 3 + [VMEM] * 5, shapes, (VMEM,) * 3 + (SMEM,), scratch, args)


def prepare_call(scal, kernel, upper, lowest):
    shapes = (
        kept((SLOTS + 1, GRID, LANES), F32),
        far((PAIRS, 2 * GRID, LANES), BF16),
        far((PAIRS, GRID, 2 * LANES), BF16),
        far((PAIRS, GRID, 2 * LANES), BF16),
        far((PAIRS, 2 * GRID, LANES), BF16),
    )
    args = (scal, kernel, near(upper), near(lowest), jnp.asarray(reversal()), jnp.asarray(COS), jnp.asarray(SIN))
    return call(prepare_kernel, 12, [SMEM] + [VMEM] * 6, shapes, (VMEM,) * 5, (), args)


def wave_call(got, scale, tables):
    scratch = (
        pltpu.VMEM((PAIRS * SLOTS * ZSPAN, LANES), F32),
        pltpu.VMEM((PAIRS * SLOTS * ZSPAN, LANES), F32),
        pltpu.VMEM((PAIRS * EDGE * BSPAN, LANES), F32),
        pltpu.VMEM((PAIRS, 2 * GRID, LANES), BF16),
        pltpu.VMEM((PAIRS, GRID, 2 * LANES), BF16),
        pltpu.VMEM((PAIRS, GRID, 2 * LANES), BF16),
        pltpu.VMEM((PAIRS, 2 * GRID, LANES), BF16),
        pltpu.VMEM((GRID, GRID), BF16),
        pltpu.SemaphoreType.DMA((5,)),
    )
    args = (near(got), near(scale), *(away(t) for t in tables), away(jnp.asarray(reversal())))
    return call(wave_kernel, 16, [VMEM] * 2 + [HBM] * 5, far(PACKET, BF16), VMEM, scratch, args)


def term_call(scal, got, there, withs):
    half = (2, ROWS, FLAT, LANES)
    shapes = (far((SLABS, ROWS, FLAT, LANES), BF16), kept(half, BF16), kept(half, BF16))
    scratch = (
        pltpu.VMEM(ROWBOX, F32),
        pltpu.VMEM((PAIRS * ROWS * SPAN, LANES), F32),
        pltpu.VMEM((HALF + EDGE + HALF, FLAT, LANES), F32),
    )
    args = (scal, near(got), there, withs, jnp.asarray(backward_last()))
    return call(term_kernel, 16, [SMEM] + [VMEM] * 4, shapes, (VMEM,) * 3, scratch, args)


def final_call(odd_core, moved, crossed, two, four):
    scratch = (pltpu.VMEM((ROWS * RSPAN, LANES), F32),)
    shape = jax.ShapeDtypeStruct((ROWS, CELLS), F32)
    args = (odd_core, near(moved), near(crossed), near(two), near(four))
    return call(final_kernel, 8, [SMEM] + [VMEM] * 4, shape, VMEM, scratch, args)


def passed_along(block, distance):
    count = lax.axis_size("orb")
    return lax.ppermute(block, "orb", [((i - distance) % count, i) for i in range(count)])


def other_core(block):
    count = lax.axis_size("orb")
    return lax.ppermute(block, "orb", [(i ^ 1, i) for i in range(count)])


def shared(block):
    return lax.all_to_all(block, "slab", split_axis=0, concat_axis=0, tiled=True)


def per_device(orbitals, partners, offsets, kernel):
    orbit = lax.axis_index("orb").astype(jnp.int32)
    slab = lax.axis_index("slab").astype(jnp.int32)
    even_core = orbit % 2 == 0
    info = jnp.stack([slab, orbit])
    odd_core = (orbit % 2)[None]
    loaded, copies = load_call(offsets, orbitals[0])
    four = passed_along(loaded, -4)
    two = passed_along(loaded, -2)
    own_box = shared(copies)
    upper, lowest = mirror_call(kernel)
    given = jnp.stack([jnp.where(even_core, two, loaded), jnp.where(even_core, four, two)])
    odd = other_core(given)
    upper = lax.ppermute(upper, "slab", [(s, SLABS - 1 - s) for s in range(SLABS)])
    send, there, withs, scal = start_call(info, partners, offsets, two, four, odd, own_box)
    got = shared(send)
    lowest = lax.ppermute(lowest, "slab", [(4, 0), (7, 1), (6, 2), (5, 3)])
    scale, *tables = prepare_call(scal, kernel, upper, lowest)
    send = wave_call(got, scale, tables)
    got = shared(send)
    move, odd_out, even_out = term_call(scal, got, there, withs)
    crossed = other_core(odd_out)
    move = shared(move)
    by_two = even_out[0].astype(F32) + jnp.where(even_core, crossed[0], crossed[1]).astype(F32)
    by_four = even_out[1].astype(F32) + jnp.where(even_core, crossed[1], 0.0).astype(F32)
    four_back = passed_along(by_four.astype(BF16), 4)
    two_back = passed_along(by_two.astype(BF16), 2)
    return final_call(odd_core, move, crossed, two_back, four_back)[None]


def solution(mesh):
    return jax.shard_map(
        per_device,
        mesh=mesh,
        in_specs=(P("orb", "slab", None), P("orb", None), P("orb", None), P(None, "slab", None)),
        out_specs=P("orb", "slab", None),
        check_vma=False,
    )
```

time: 214 us -> 99.5 us (0.46)
  the two profiles are of different devices: /device:TPU:8 before, /device:TPU:10 now
where the time goes in v4:
time: 99.5 us; the launch traced here: 98.7 us
  starting transfers between devices  53 us (53%)
  waiting for transfers between devices  19 us (19%)
  Pallas kernels  13.4 us (13%)
  blocking collectives  11.4 us (11%)
  local copies, waits for them, and re-layouts  1.54 us (2%)
    ppermute x4, starting transfers between devices, passed_along(): lax.ppermute(block, 'orb', [((i - distance) % count, i) for i in range(co...  25.4 us
    all_to_all x3, starting transfers between devices, shared(): lax.all_to_all(block, 'slab', split_axis=0, concat_axis=0, tiled=True)  16.3 us
    pallas_call x7, Pallas kernels, call(): pl.pallas_call(kernel, out_shape=out_shape, in_specs=in_specs, out_specs=...  13.4 us
    all_to_all x1, blocking collectives, shared(): lax.all_to_all(block, 'slab', split_axis=0, concat_axis=0, tiled=True)  11.4 us
    ppermute x4, waiting for transfers between devices, passed_along(): lax.ppermute(block, 'orb', [((i - distance) % count, i) for i in range(co...  9.43 us
    all_to_all x3, waiting for transfers between devices, shared(): lax.all_to_all(block, 'slab', split_axis=0, concat_axis=0, tiled=True)  4.01 us
    ppermute x1, starting transfers between devices, per_device(): lowest = lax.ppermute(lowest, 'slab', [(4, 0), (7, 1), (6, 2), (5, 3)])  3.99 us
    ppermute x2, starting transfers between devices, other_core(): return lax.ppermute(block, 'orb', [(i ^ 1, i) for i in range(count)])  3.96 us
  transfers between devices with their start and end apart: 11, of which 7 were waited for; matrix products, arithmetic and copies ran while one was open for 0% of the time, Pallas kernels for 2%

profile of v4, /device:TPU:10, one launch (start us, length us, event | category | flops | bytes accessed | tf_op | source)
XLA Modules:
  0.0 98.7 jit_solution(14377915937122312933)
XLA Ops:
  0.0 0.0 copy-start.9
  0.0 0.7 copy-done.9
  0.7 0.0 copy-start.8
  0.7 0.8 copy-done.8
  1.5 1.4 %shard_map.100 = (bf16[8,4224]{1,0:T(8,128)(2,1)S(1)}, bf16[8,8,4096]{2,1,0:T(8,128)(2,1)}) custom-call(s32[1,3]{1,0:T(1,128)S(1)} %copy-done.9, bf16[8,4096]{1,0:T(8,128)(2,1)S(1)} %bitcast.13), custom_call_target="tpu_custom_call" | custom-call | tf_op jit(solution)/shard_map/pallas_call | solution.py:360
  2.9 15.3 %collective-permute-start.1 = (bf16[8,4224]{1,0:T(8,128)(2,1)S(1)}, bf16[8,4224]{1,0:T(8,128)(2,1)S(1)}, u32[]{:S(2)}, u32[]{:S(2)}) collective-permute-start(bf16[8,4224]{1,0:T(8,128)(2,1)S(1)} %get-tuple-element.21), channel_id=1, source_target_pairs={{32,0},{40,8},{48,16},{56,24},{64,32},{72,40},{80,48},{88,56},{96,... | collective-permute-start | bytes 202760 | tf_op jit(solution)/shard_map/ppermute | solution.py:442
  18.2 3.1 %collective-permute-start = (bf16[8,4224]{1,0:T(8,128)(2,1)S(1)}, bf16[8,4224]{1,0:T(8,128)(2,1)S(1)}, u32[]{:S(2)}, u32[]{:S(2)}) collective-permute-start(bf16[8,4224]{1,0:T(8,128)(2,1)S(1)} %get-tuple-element.21), channel_id=1, source_target_pairs={{16,0},{24,8},{32,16},{40,24},{48,32},{56,40},{64,48},{72,56},{80,... | collective-permute-start | bytes 202760 | tf_op jit(solution)/shard_map/ppermute | solution.py:442
  21.3 0.0 copy-start.7
  21.4 0.0 copy-start.10
  21.4 5.9 %all-to-all-start = ((bf16[8,8,4096]{2,1,0:T(8,128)(2,1)}), bf16[8,8,4096]{2,1,0:T(8,128)(2,1)S(1)}, u32[]{:S(2)}, u32[]{:S(2)}) async-start(bf16[8,8,4096]{2,1,0:T(8,128)(2,1)} %get-tuple-element.22), calls=%async_computation | async-start | bytes 1048576 | tf_op jit(solution)/shard_map/all_to_all | solution.py:451
  27.2 0.0 copy-start
  27.3 0.0 collective-permute-done.1.four
  27.3 0.0 collective-permute-done.two
  27.3 2.1 %collective-permute-start.2 = (bf16[2,8,4224]{2,1,0:T(8,128)(2,1)S(1)}, bf16[2,8,4224]{2,1,0:T(8,128)(2,1)S(1)}, u32[]{:S(2)}, u32[]{:S(2)}) collective-permute-start(bf16[2,8,4224]{2,1,0:T(8,128)(2,1)S(1)} %pad_maximum_fusion), channel_id=1, source_target_pairs={{8,0},{0,8},{24,16},{16,24},{40,32},{32,40},{56,48},{48,56},{72,64... | collective-permute-start | bytes 405512 | tf_op jit(solution)/shard_map/ppermute | solution.py:447
  29.4 0.1 pad_add_fusion.info
  29.5 1.2 %collective-permute-done.2.odd = bf16[2,8,4224]{2,1,0:T(8,128)(2,1)S(1)} collective-permute-done((bf16[2,8,4224]{2,1,0:T(8,128)(2,1)S(1)}, bf16[2,8,4224]{2,1,0:T(8,128)(2,1)S(1)}, u32[]{:S(2)}, u32[]{:S(2)}) %collective-permute-start.2) | collective-permute-done | bytes 135200 | tf_op jit(solution)/shard_map/ppermute | solution.py:447
  30.7 4.0 %all-to-all-done.own_in = bf16[8,8,4096]{2,1,0:T(8,128)(2,1)S(1)} async-done(((bf16[8,8,4096]{2,1,0:T(8,128)(2,1)}), bf16[8,8,4096]{2,1,0:T(8,128)(2,1)S(1)}, u32[]{:S(2)}, u32[]{:S(2)}) %all-to-all-start) | async-done | bytes 524320 | tf_op jit(solution)/shard_map/all_to_all | solution.py:451
  34.7 0.0 copy-done.7
  34.7 0.0 copy-done.10
  34.7 2.2 %shard_map.101 = (bf16[8,2,4,16,128]{4,3,2,1,0:T(8,128)(2,1)}, bf16[2,8,32,128]{3,2,1,0:T(8,128)(2,1)}, bf16[2,8,32,128]{3,2,1,0:T(8,128)(2,1)}, s32[9]{0:T(128)S(1)}) custom-call(s32[2]{0:T(128)S(1)} %pad_add_fusion.info, s32[1,2]{1,0:T(1,128)S(1)} %copy-done.10, s32[1,3]{1,0:T(1,128)S(1)} %copy-done.9, bf16[8,4224]{1,0:T(8,128)(2,1)S(1)} %collective-permute-done.two, ...), custom_call_target="tpu_custom_call" | custom-call | tf_op jit(solution)/shard_map/pallas_call | solution.py:360
  36.9 5.0 %all-to-all-start.1 = ((bf16[8,2,4,16,128]{4,3,2,1,0:T(8,128)(2,1)}), bf16[8,2,4,16,128]{4,3,2,1,0:T(8,128)(2,1)S(1)}, u32[]{:S(2)}, u32[]{:S(2)}) async-start(bf16[8,2,4,16,128]{4,3,2,1,0:T(8,128)(2,1)} %get-tuple-element.24), calls=%async_computation.1 | async-start | bytes 524288 | tf_op jit(solution)/shard_map/all_to_all | solution.py:451
  42.0 0.0 copy-done
  42.0 0.0 copy-start.2
  42.0 0.0 copy-start.5
  42.0 0.0 copy-start.6
  42.0 0.2 shard_map.102
  42.2 3.4 %collective-permute-start.3 = (bf16[8,128,128]{2,1,0:T(8,128)(2,1)S(1)}, bf16[8,128,128]{2,1,0:T(8,128)(2,1)S(1)}, u32[]{:S(2)}, u32[]{:S(2)}) collective-permute-start(bf16[8,128,128]{2,1,0:T(8,128)(2,1)S(1)} %get-tuple-element.25), channel_id=1, source_target_pairs={{0,7},{1,6},{2,5},{3,4},{4,3},{5,2},{6,1},{7,0},{8,15},{9,14},{10,... | collective-permute-start | bytes 786440 | tf_op jit(solution)/shard_map/ppermute | solution.py:467
  45.5 4.0 %collective-permute-start.4 = (bf16[128,128]{1,0:T(8,128)(2,1)S(1)}, bf16[128,128]{1,0:T(8,128)(2,1)S(1)}, u32[]{:S(2)}, u32[]{:S(2)}) collective-permute-start(bf16[128,128]{1,0:T(8,128)(2,1)S(1)} %get-tuple-element.26), channel_id=1, source_target_pairs={{4,0},{7,1},{6,2},{5,3},{12,8},{15,9},{14,10},{13,11},{20,16},{23,... | collective-permute-start | bytes 98312 | tf_op jit(solution)/shard_map/ppermute | solution.py:470
  49.5 1.6 %collective-permute-done.4.lowest = bf16[128,128]{1,0:T(8,128)(2,1)S(1)} collective-permute-done((bf16[128,128]{1,0:T(8,128)(2,1)S(1)}, bf16[128,128]{1,0:T(8,128)(2,1)S(1)}, u32[]{:S(2)}, u32[]{:S(2)}) %collective-permute-start.4) | collective-permute-done | bytes 32800 | tf_op jit(solution)/shard_map/ppermute | solution.py:470
  51.1 1.4 %collective-permute-done.3.upper = bf16[8,128,128]{2,1,0:T(8,128)(2,1)S(1)} collective-permute-done((bf16[8,128,128]{2,1,0:T(8,128)(2,1)S(1)}, bf16[8,128,128]{2,1,0:T(8,128)(2,1)S(1)}, u32[]{:S(2)}, u32[]{:S(2)}) %collective-permute-start.3) | collective-permute-done | bytes 262176 | tf_op jit(solution)/shard_map/ppermute | solution.py:467
  52.5 0.0 copy-done.2
  52.5 0.0 copy-done.5
  52.5 0.0 copy-done.6
  52.5 1.8 %shard_map.103 = (f32[9,128,128]{2,1,0:T(8,128)S(1)}, bf16[2,256,128]{2,1,0:T(8,128)(2,1)}, bf16[2,128,256]{2,1,0:T(8,128)(2,1)}, bf16[2,128,256]{2,1,0:T(8,128)(2,1)}, bf16[2,256,128]{2,1,0:T(8,128)(2,1)}) custom-call(s32[9]{0:T(128)S(1)} %get-tuple-element.23.scal, f32[128,16,128]{2,1,0:T(8,128)S(1)} %copy-done, ...), custom_call_target="tpu_custom_call" | custom-call | tf_op jit(solution)/shard_map/pallas_call | solution.py:360
  54.4 0.0 all-to-all-done.1.got
  54.4 4.9 %shard_map.104 = bf16[8,2,4,16,128]{4,3,2,1,0:T(8,128)(2,1)} custom-call(bf16[8,2,4,16,128]{4,3,2,1,0:T(8,128)(2,1)S(1)} %all-to-all-done.1.got, f32[9,128,128]{2,1,0:T(8,128)S(1)} %get-tuple-element.27.scale_t, bf16[2,256,128]{2,1,0:T(8,128)(2,1)} %get-tuple-element.28.rowf_h, bf16[2,128,256]{2,1,0:T(8,128)(2,1)} %get-tuple-element.29.depf_h, ...), custom_call_target="tpu_custom_call" | custom-call | tf_op jit(solution)/shard_map/pallas_call | solution.py:360
  59.3 0.0 copy-start.1
  59.3 0.0 copy-start.3
  59.3 0.0 copy-start.4
  59.4 11.4 %all_to_all.20.got = bf16[8,2,4,16,128]{4,3,2,1,0:T(8,128)(2,1)S(1)} all-to-all(bf16[8,2,4,16,128]{4,3,2,1,0:T(8,128)(2,1)} %shard_map.104), channel_id=1, replica_groups=mesh['orb'=64,'slab'=8] {'slab'}, dimensions={0} | all-to-all | bytes 524288 | tf_op jit(solution)/shard_map/all_to_all | solution.py:451
  70.8 0.0 copy-done.1
  70.8 0.0 copy-done.3
  70.8 0.0 copy-done.4
  70.8 2.1 %shard_map.105 = (bf16[8,8,32,128]{3,2,1,0:T(8,128)(2,1)}, bf16[2,8,32,128]{3,2,1,0:T(8,128)(2,1)S(1)}, bf16[2,8,32,128]{3,2,1,0:T(8,128)(2,1)S(1)}) custom-call(s32[9]{0:T(128)S(1)} %get-tuple-element.23.scal, bf16[8,2,4,16,128]{4,3,2,1,0:T(8,128)(2,1)S(1)} %all_to_all.20.got, bf16[2,8,32,128]{3,2,1,0:T(8,128)(2,1)S(1)} %copy-done.3, ...), custom_call_target="tpu_custom_call" | custom-call | tf_op jit(solution)/shard_map/pallas_call | solution.py:360
  72.8 5.4 %all-to-all-start.3 = ((bf16[8,8,32,128]{3,2,1,0:T(8,128)(2,1)}), bf16[8,8,32,128]{3,2,1,0:T(8,128)(2,1)S(1)}, u32[]{:S(2)}, u32[]{:S(2)}) async-start(bf16[8,8,32,128]{3,2,1,0:T(8,128)(2,1)} %get-tuple-element.34), calls=%async_computation.3 | async-start | bytes 1048576 | tf_op jit(solution)/shard_map/all_to_all | solution.py:451
  78.3 1.9 %collective-permute-start.5 = (bf16[2,8,32,128]{3,2,1,0:T(8,128)(2,1)S(1)}, bf16[2,8,32,128]{3,2,1,0:T(8,128)(2,1)S(1)}, u32[]{:S(2)}, u32[]{:S(2)}) collective-permute-start(bf16[2,8,32,128]{3,2,1,0:T(8,128)(2,1)S(1)} %get-tuple-element.35), channel_id=1, source_target_pairs={{8,0},{0,8},{24,16},{16,24},{40,32},{32,40},{56,48},{48,56},{72,64... | collective-permute-start | bytes 393224 | tf_op jit(solution)/shard_map/ppermute | solution.py:447
  80.2 1.3 %collective-permute-done.5.crossed = bf16[2,8,32,128]{3,2,1,0:T(8,128)(2,1)S(1)} collective-permute-done((bf16[2,8,32,128]{3,2,1,0:T(8,128)(2,1)S(1)}, bf16[2,8,32,128]{3,2,1,0:T(8,128)(2,1)S(1)}, u32[]{:S(2)}, u32[]{:S(2)}) %collective-permute-start.5) | collective-permute-done | bytes 131104 | tf_op jit(solution)/shard_map/ppermute | solution.py:447
  81.6 5.0 %collective-permute-start.7 = (bf16[8,32,128]{2,1,0:T(8,128)(2,1)S(1)}, bf16[8,32,128]{2,1,0:T(8,128)(2,1)S(1)}, u32[]{:S(2)}, u32[]{:S(2)}) collective-permute-start(bf16[8,32,128]{2,1,0:T(8,128)(2,1)S(1)} %get-tuple-element.37), channel_id=1, source_target_pairs={{480,0},{488,8},{496,16},{504,24},{0,32},{8,40},{16,48},{24,56},{3... | collective-permute-start | bytes 196616 | tf_op jit(solution)/shard_map/ppermute | solution.py:442
  86.6 1.9 %collective-permute-start.6 = (bf16[8,32,128]{2,1,0:T(8,128)(2,1)S(1)}, bf16[8,32,128]{2,1,0:T(8,128)(2,1)S(1)}, u32[]{:S(2)}, u32[]{:S(2)}) collective-permute-start(bf16[8,32,128]{2,1,0:T(8,128)(2,1)S(1)} %get-tuple-element.38), channel_id=1, source_target_pairs={{496,0},{504,8},{0,16},{8,24},{16,32},{24,40},{32,48},{40,56},{48,... | collective-permute-start | bytes 196616 | tf_op jit(solution)/shard_map/ppermute | solution.py:442
  88.5 5.6 %collective-permute-done.7.four = bf16[8,32,128]{2,1,0:T(8,128)(2,1)S(1)} collective-permute-done((bf16[8,32,128]{2,1,0:T(8,128)(2,1)S(1)}, bf16[8,32,128]{2,1,0:T(8,128)(2,1)S(1)}, u32[]{:S(2)}, u32[]{:S(2)}) %collective-permute-start.7) | collective-permute-done | bytes 65568 | tf_op jit(solution)/shard_map/ppermute | solution.py:442
  94.1 3.8 %collective-permute-done.6.two = bf16[8,32,128]{2,1,0:T(8,128)(2,1)S(1)} collective-permute-done((bf16[8,32,128]{2,1,0:T(8,128)(2,1)S(1)}, bf16[8,32,128]{2,1,0:T(8,128)(2,1)S(1)}, u32[]{:S(2)}, u32[]{:S(2)}) %collective-permute-start.6) | collective-permute-done | bytes 65568 | tf_op jit(solution)/shard_map/ppermute | solution.py:442
  98.0 0.0 all-to-all-done.3.moved
  98.0 0.8 shard_map.106
  (3 shorter events, 0.1 us)
Async XLA Ops:
  0.0 0.7 copy-start.9
  0.7 0.8 copy-start.8
  2.9 24.4 %collective-permute-start.1 = (bf16[8,4224]{1,0:T(8,128)(2,1)S(1)}, bf16[8,4224]{1,0:T(8,128)(2,1)S(1)}, u32[]{:S(2)}, u32[]{:S(2)}) collective-permute-start(bf16[8,4224]{1,0:T(8,128)(2,1)S(1)} %get-tuple-element.21), channel_id=1, source_target_pairs={{32,0},{40,8},{48,16},{56,24},{64,32},{72,40},{80,48},{88,56},{96,... | collective-permute-start | bytes 202760 | tf_op jit(solution)/shard_map/ppermute | solution.py:442
  18.2 9.1 %collective-permute-start = (bf16[8,4224]{1,0:T(8,128)(2,1)S(1)}, bf16[8,4224]{1,0:T(8,128)(2,1)S(1)}, u32[]{:S(2)}, u32[]{:S(2)}) collective-permute-start(bf16[8,4224]{1,0:T(8,128)(2,1)S(1)} %get-tuple-element.21), channel_id=1, source_target_pairs={{16,0},{24,8},{32,16},{40,24},{48,32},{56,40},{64,48},{72,56},{80,... | collective-permute-start | bytes 202760 | tf_op jit(solution)/shard_map/ppermute | solution.py:442
  21.3 13.4 %copy-start.7 = (f32[128,128]{1,0:T(8,128)S(1)}, f32[128,128]{1,0:T(8,128)}, u32[]{:S(2)}) copy-start(f32[128,128]{1,0:T(8,128)} %constant.38.clone.first_t) | copy-start | bytes 196612
  21.4 13.3 %copy-start.10 = (s32[1,2]{1,0:T(1,128)S(1)}, s32[1,2]{1,0:T(1,128)}, u32[]{:S(2)}) copy-start(s32[1,2]{1,0:T(1,128)} %partners.1) | copy-start | bytes 28
  21.4 13.3 %all-to-all-start = ((bf16[8,8,4096]{2,1,0:T(8,128)(2,1)}), bf16[8,8,4096]{2,1,0:T(8,128)(2,1)S(1)}, u32[]{:S(2)}, u32[]{:S(2)}) async-start(bf16[8,8,4096]{2,1,0:T(8,128)(2,1)} %get-tuple-element.22), calls=%async_computation | async-start | bytes 1048576 | tf_op jit(solution)/shard_map/all_to_all | solution.py:451
  27.2 14.7 %copy-start = (f32[128,16,128]{2,1,0:T(8,128)S(1)}, f32[128,16,128]{2,1,0:T(8,128)}, u32[]{:S(2)}) copy-start(f32[128,16,128]{2,1,0:T(8,128)} %kern.3) | copy-start | bytes 3145732
  27.3 3.4 %collective-permute-start.2 = (bf16[2,8,4224]{2,1,0:T(8,128)(2,1)S(1)}, bf16[2,8,4224]{2,1,0:T(8,128)(2,1)S(1)}, u32[]{:S(2)}, u32[]{:S(2)}) collective-permute-start(bf16[2,8,4224]{2,1,0:T(8,128)(2,1)S(1)} %pad_maximum_fusion), channel_id=1, source_target_pairs={{8,0},{0,8},{24,16},{16,24},{40,32},{32,40},{56,48},{48,56},{72,64... | collective-permute-start | bytes 405512 | tf_op jit(solution)/shard_map/ppermute | solution.py:447
  36.9 17.4 %all-to-all-start.1 = ((bf16[8,2,4,16,128]{4,3,2,1,0:T(8,128)(2,1)}), bf16[8,2,4,16,128]{4,3,2,1,0:T(8,128)(2,1)S(1)}, u32[]{:S(2)}, u32[]{:S(2)}) async-start(bf16[8,2,4,16,128]{4,3,2,1,0:T(8,128)(2,1)} %get-tuple-element.24), calls=%async_computation.1 | async-start | bytes 524288 | tf_op jit(solution)/shard_map/all_to_all | solution.py:451
  42.0 10.6 %copy-start.2 = (bf16[128,128]{1,0:T(8,128)(2,1)S(1)}, bf16[128,128]{1,0:T(8,128)(2,1)}, u32[]{:S(2)}) copy-start(bf16[128,128]{1,0:T(8,128)(2,1)} %constant.39.clone.flip_t.flip_h) | copy-start | bytes 98308
  42.0 10.6 %copy-start.5 = (f32[128,128]{1,0:T(8,128)S(1)}, f32[128,128]{1,0:T(8,128)}, u32[]{:S(2)}) copy-start(f32[128,128]{1,0:T(8,128)} %constant.41.clone.sin_f) | copy-start | bytes 196612
  42.0 10.6 %copy-start.6 = (f32[128,128]{1,0:T(8,128)S(1)}, f32[128,128]{1,0:T(8,128)}, u32[]{:S(2)}) copy-start(f32[128,128]{1,0:T(8,128)} %constant.40.clone.cos_f) | copy-start | bytes 196612
  42.2 10.3 %collective-permute-start.3 = (bf16[8,128,128]{2,1,0:T(8,128)(2,1)S(1)}, bf16[8,128,128]{2,1,0:T(8,128)(2,1)S(1)}, u32[]{:S(2)}, u32[]{:S(2)}) collective-permute-start(bf16[8,128,128]{2,1,0:T(8,128)(2,1)S(1)} %get-tuple-element.25), channel_id=1, source_target_pairs={{0,7},{1,6},{2,5},{3,4},{4,3},{5,2},{6,1},{7,0},{8,15},{9,14},{10,... | collective-permute-start | bytes 786440 | tf_op jit(solution)/shard_map/ppermute | solution.py:467
  45.5 5.6 %collective-permute-start.4 = (bf16[128,128]{1,0:T(8,128)(2,1)S(1)}, bf16[128,128]{1,0:T(8,128)(2,1)S(1)}, u32[]{:S(2)}, u32[]{:S(2)}) collective-permute-start(bf16[128,128]{1,0:T(8,128)(2,1)S(1)} %get-tuple-element.26), channel_id=1, source_target_pairs={{4,0},{7,1},{6,2},{5,3},{12,8},{15,9},{14,10},{13,11},{20,16},{23,... | collective-permute-start | bytes 98312 | tf_op jit(solution)/shard_map/ppermute | solution.py:470
  59.3 11.5 %copy-start.1 = (f32[512,128]{1,0:T(8,128)S(1)}, f32[512,128]{1,0:T(8,128)}, u32[]{:S(2)}) copy-start(f32[512,128]{1,0:T(8,128)} %constant.42.clone.last_t) | copy-start | bytes 786436
  59.3 11.5 %copy-start.3 = (bf16[2,8,32,128]{3,2,1,0:T(8,128)(2,1)S(1)}, bf16[2,8,32,128]{3,2,1,0:T(8,128)(2,1)}, u32[]{:S(2)}) copy-start(bf16[2,8,32,128]{3,2,1,0:T(8,128)(2,1)} %get-tuple-element.32.there) | copy-start | bytes 393220
  59.3 11.4 %copy-start.4 = (bf16[2,8,32,128]{3,2,1,0:T(8,128)(2,1)S(1)}, bf16[2,8,32,128]{3,2,1,0:T(8,128)(2,1)}, u32[]{:S(2)}) copy-start(bf16[2,8,32,128]{3,2,1,0:T(8,128)(2,1)} %get-tuple-element.33.withs) | copy-start | bytes 393220
  72.8 25.1 %all-to-all-start.3 = ((bf16[8,8,32,128]{3,2,1,0:T(8,128)(2,1)}), bf16[8,8,32,128]{3,2,1,0:T(8,128)(2,1)S(1)}, u32[]{:S(2)}, u32[]{:S(2)}) async-start(bf16[8,8,32,128]{3,2,1,0:T(8,128)(2,1)} %get-tuple-element.34), calls=%async_computation.3 | async-start | bytes 1048576 | tf_op jit(solution)/shard_map/all_to_all | solution.py:451
  78.3 3.2 %collective-permute-start.5 = (bf16[2,8,32,128]{3,2,1,0:T(8,128)(2,1)S(1)}, bf16[2,8,32,128]{3,2,1,0:T(8,128)(2,1)S(1)}, u32[]{:S(2)}, u32[]{:S(2)}) collective-permute-start(bf16[2,8,32,128]{3,2,1,0:T(8,128)(2,1)S(1)} %get-tuple-element.35), channel_id=1, source_target_pairs={{8,0},{0,8},{24,16},{16,24},{40,32},{32,40},{56,48},{48,56},{72,64... | collective-permute-start | bytes 393224 | tf_op jit(solution)/shard_map/ppermute | solution.py:447
  81.6 12.5 %collective-permute-start.7 = (bf16[8,32,128]{2,1,0:T(8,128)(2,1)S(1)}, bf16[8,32,128]{2,1,0:T(8,128)(2,1)S(1)}, u32[]{:S(2)}, u32[]{:S(2)}) collective-permute-start(bf16[8,32,128]{2,1,0:T(8,128)(2,1)S(1)} %get-tuple-element.37), channel_id=1, source_target_pairs={{480,0},{488,8},{496,16},{504,24},{0,32},{8,40},{16,48},{24,56},{3... | collective-permute-start | bytes 196616 | tf_op jit(solution)/shard_map/ppermute | solution.py:442
  86.6 11.4 %collective-permute-start.6 = (bf16[8,32,128]{2,1,0:T(8,128)(2,1)S(1)}, bf16[8,32,128]{2,1,0:T(8,128)(2,1)S(1)}, u32[]{:S(2)}, u32[]{:S(2)}) collective-permute-start(bf16[8,32,128]{2,1,0:T(8,128)(2,1)S(1)} %get-tuple-element.38), channel_id=1, source_target_pairs={{496,0},{504,8},{0,16},{8,24},{16,32},{24,40},{32,48},{40,56},{48,... | collective-permute-start | bytes 196616 | tf_op jit(solution)/shard_map/ppermute | solution.py:442

commit v5 on v4

--- a/solution.py
+++ b/solution.py
@@ -92,6 +92,10 @@
     return jnp.where((depth >= 0) & (depth < EDGE), jnp.where(lane >= turn, here, before), 0.0)
 
 
+def reversed_plane(flip, plane):
+    return dot(dot(flip, plane).astype(BF16), flip)
+
+
 def clear_edges(ref, rows):
     zeros = jnp.zeros((PAD + 1, LANES), F32)
     for c in range(rows):
@@ -99,16 +103,18 @@
         ref[c * SPAN + PAD + FLAT : (c + 1) * SPAN, :] = zeros
 
 
-def load_kernel(corner, own, loaded, copies):
-    cells = own[...]
-    loaded[:, :CELLS] = cells
+def load_kernel(corner, own, loaded, copies, sems):
+    loads = [pltpu.make_async_copy(own, copies.at[t], sems.at[t]) for t in range(SLABS)]
+    loads.append(pltpu.make_async_copy(own, loaded.at[:, pl.ds(0, CELLS)], sems.at[SLABS]))
+    for one in loads:
+        one.start()
     lane = lanes_of((ROWS, LANES))
     mark = jnp.zeros((ROWS, LANES), F32)
     for k in range(3):
         mark = jnp.where(lane == k, corner[0, k].astype(F32), mark)
     loaded[:, CELLS:] = mark.astype(BF16)
-    for t in range(SLABS):
-        copies[t] = cells
+    for one in loads:
+        one.wait()
 
 
 def mirror_kernel(kern, upper, lowest):
@@ -179,29 +185,20 @@
                     send[s, n, quad * 2 + half] = both.astype(BF16)
 
 
-def prepare_kernel(scal, kern, upper, lowest, flip_t, cos_f, sin_f, scale_out, rowf_out, depf_out, rowb_out, depb_out):
+def prepare_kernel(scal, kern, upper, flip_t, cos_f, sin_f, scale_out, rowf_out, depf_out, rowb_out, depb_out):
     slab = scal[0]
     flip = flip_t[...]
-
-    def reversed_plane(plane):
-        return dot(dot(flip, plane).astype(BF16), flip)
-
     kern_flat = kern.reshape(GRID * WAVES, LANES)
-    first = slab == 0
     lower = slab < SLABS // 2
     for q in range(SLOTS):
         here = kern_flat[pl.ds(jnp.where(lower, q, q + 1), GRID, stride=WAVES), :]
         if q:
             there = upper[jnp.where(lower, SLOTS - q, SLOTS - 1 - q)]
-            scale_out[q] = here + reversed_plane(there)
+            scale_out[q] = here + reversed_plane(flip, there)
         else:
             here = here.astype(BF16).astype(F32)
-            low = lowest[...].astype(F32)
-            there = jnp.where(lower, low, upper[SLOTS - 1].astype(F32))
-            both = here + reversed_plane(jnp.where(first, here, there).astype(BF16))
-            top = low + reversed_plane(lowest[...])
-            scale_out[0] = jnp.where(first, 0.25 * (both + top), both)
-            scale_out[SLOTS] = jnp.where(first, 0.25 * (both - top), 0.0)
+            scale_out[0] = here + jnp.where(lower, 0.0, reversed_plane(flip, upper[SLOTS - 1]))
+            scale_out[SLOTS] = here + reversed_plane(flip, here.astype(BF16))
     half = low_half((GRID, LANES))
 
     def by_wave(shift):
@@ -224,15 +221,18 @@
         )
 
 
-def wave_kernel(got, scale_t, rowf_h, depf_h, rowb_h, depb_h, flip_h, send, zr, zi, back_s, rowf_t, depf_t, rowb_t, depb_t, flip_t, sems):
-    held = (depf_h, rowf_h, rowb_h, depb_h, flip_h)
-    local = (depf_t, rowf_t, rowb_t, depb_t, flip_t)
-    loads = [pltpu.make_async_copy(a, b, sems.at[i]) for i, (a, b) in enumerate(zip(held, local))]
-    for load in loads:
-        load.start()
-    for load in loads:
-        load.wait()
+def wave_kernel(scal, got, scale_t, lowest, rowf_t, depf_t, rowb_t, depb_t, flip_t, send, zr, zi, back_s):
+    slab = scal[0]
+    first = slab == 0
+    lower = slab < SLABS // 2
     flip = flip_t[...]
+    low = lowest[...]
+    low_back = reversed_plane(flip, low)
+    both = scale_t[SLOTS]
+    top = low.astype(F32) + low_back
+    bottom = scale_t[0] + jnp.where(lower, low_back, 0.0)
+    main = jnp.where(first, 0.25 * (both + top), bottom)
+    extra = jnp.where(first, 0.25 * (both - top), 0.0)
     for n in range(PAIRS):
         at_z = n * SLOTS * ZSPAN
         at_b = n * EDGE * BSPAN
@@ -252,13 +252,12 @@
 
         for w0 in range(0, SLOTS, 2):
             x = dot(rows_m, jnp.concatenate([plane(w0), plane(w0 + 1)], axis=1))
-            weight = jnp.concatenate([scale_t[w0], scale_t[w0 + 1]], axis=1)
+            weight = jnp.concatenate([scale_t[w0] if w0 else main, scale_t[w0 + 1]], axis=1)
             re, im = x[:GRID] * weight, x[GRID:] * weight
             if w0 == 0:
                 edge = x[:, :LANES].astype(BF16)
                 back_re = dot(dot(flip, edge[:GRID]).astype(BF16), flip)
                 back_im = dot(dot(flip, edge[GRID:]).astype(BF16), flip)
-                extra = scale_t[SLOTS]
                 re = jnp.concatenate([re[:, :LANES] + extra * back_re, re[:, LANES:]], axis=1)
                 im = jnp.concatenate([im[:, :LANES] - extra * back_im, im[:, LANES:]], axis=1)
             v = dot(rowb_t[n], jnp.concatenate([re, im], axis=0).astype(BF16)).astype(BF16)
@@ -280,7 +279,19 @@
                 send[t, n, p] = both.astype(BF16)
 
 
-def term_kernel(scal, got, there, withs, last_t, move_out, odd_out, even_out, far_s, own_s, sum_s):
+def ready_kernel(scal, last_t, tab_out):
+    for n in range(PAIRS):
+        d1 = scal[2 + 3 * n]
+        parts = [
+            last_t[pl.ds((2 * row + f) * GRID + HALF + d1 + par, FLAT, stride=2), :]
+            for row in range(2)
+            for f in range(2)
+            for par in range(2)
+        ]
+        tab_out[n] = jnp.concatenate(parts, axis=0).astype(BF16)
+
+
+def term_kernel(scal, got, there, withs, tabs, move_out, odd_out, even_out, far_s, own_s, sum_s):
     slab = scal[0]
     low = low_half((FLAT, LANES))
     scale = 1.0 / GRID**3
@@ -290,13 +301,7 @@
         sum_s[HALF + c] = blank
     for n in range(PAIRS):
         d0, d1, d2 = scal[1 + 3 * n], scal[2 + 3 * n], scal[3 + 3 * n]
-        parts = [
-            last_t[pl.ds((2 * row + f) * GRID + HALF + d1 + par, FLAT, stride=2), :]
-            for row in range(2)
-            for f in range(2)
-            for par in range(2)
-        ]
-        tab = jnp.concatenate(parts, axis=0).astype(BF16)
+        tab = tabs[n]
         for quad in range(ROWS // 4):
             data = [jnp.concatenate([got[t, n, quad * 2 + h] for t in range(SLABS)], axis=0) for h in range(2)]
             g = dot(tab, jnp.concatenate(data, axis=1))
@@ -375,7 +380,8 @@
 
 def load_call(offsets, own):
     shapes = (kept((ROWS, CELLS + LANES), BF16), kept((SLABS, ROWS, CELLS), BF16))
-    return call(load_kernel, 8, [SMEM, VMEM], shapes, (VMEM,) * 2, (), (offsets, own))
+    scratch = (pltpu.SemaphoreType.DMA((SLABS + 1,)),)
+    return call(load_kernel, 8, [SMEM, HBM], shapes, (VMEM,) * 2, scratch, (away(offsets), away(own)))
 
 
 def mirror_call(kernel):
@@ -390,35 +396,34 @@
     return call(start_kernel, 12, [SMEM] * 3 + [VMEM] * 5, shapes, (VMEM,) * 3 + (SMEM,), scratch, args)
 
 
-def prepare_call(scal, kernel, upper, lowest):
+def prepare_call(scal, kernel, upper):
     shapes = (
         kept((SLOTS + 1, GRID, LANES), F32),
-        far((PAIRS, 2 * GRID, LANES), BF16),
-        far((PAIRS, GRID, 2 * LANES), BF16),
-        far((PAIRS, GRID, 2 * LANES), BF16),
-        far((PAIRS, 2 * GRID, LANES), BF16),
+        kept((PAIRS, 2 * GRID, LANES), BF16),
+        kept((PAIRS, GRID, 2 * LANES), BF16),
+        kept((PAIRS, GRID, 2 * LANES), BF16),
+        kept((PAIRS, 2 * GRID, LANES), BF16),
     )
-    args = (scal, kernel, near(upper), near(lowest), jnp.asarray(reversal()), jnp.asarray(COS), jnp.asarray(SIN))
-    return call(prepare_kernel, 12, [SMEM] + [VMEM] * 6, shapes, (VMEM,) * 5, (), args)
-
-
-def wave_call(got, scale, tables):
+    args = (scal, kernel, near(upper), jnp.asarray(reversal()), jnp.asarray(COS), jnp.asarray(SIN))
+    return call(prepare_kernel, 12, [SMEM] + [VMEM] * 5, shapes, (VMEM,) * 5, (), args)
+
+
+def wave_call(scal, got, scale, lowest, tables):
     scratch = (
         pltpu.VMEM((PAIRS * SLOTS * ZSPAN, LANES), F32),
         pltpu.VMEM((PAIRS * SLOTS * ZSPAN, LANES), F32),
         pltpu.VMEM((PAIRS * EDGE * BSPAN, LANES), F32),
-        pltpu.VMEM((PAIRS, 2 * GRID, LANES), BF16),
-        pltpu.VMEM((PAIRS, GRID, 2 * LANES), BF16),
-        pltpu.VMEM((PAIRS, GRID, 2 * LANES), BF16),
-        pltpu.VMEM((PAIRS, 2 * GRID, LANES), BF16),
-        pltpu.VMEM((GRID, GRID), BF16),
-        pltpu.SemaphoreType.DMA((5,)),
     )
-    args = (near(got), near(scale), *(away(t) for t in tables), away(jnp.asarray(reversal())))
-    return call(wave_kernel, 16, [VMEM] * 2 + [HBM] * 5, far(PACKET, BF16), VMEM, scratch, args)
-
-
-def term_call(scal, got, there, withs):
+    args = (scal, near(got), near(scale), near(lowest), *(near(t) for t in tables), jnp.asarray(reversal()))
+    return call(wave_kernel, 12, [SMEM] + [VMEM] * 8, far(PACKET, BF16), VMEM, scratch, args)
+
+
+def ready_call(scal):
+    args = (scal, jnp.asarray(backward_last()))
+    return call(ready_kernel, 8, [SMEM, VMEM], kept((PAIRS, 2 * GRID, GRID), BF16), VMEM, (), args)
+
+
+def term_call(scal, got, there, withs, tabs):
     half = (2, ROWS, FLAT, LANES)
     shapes = (far((SLABS, ROWS, FLAT, LANES), BF16), kept(half, BF16), kept(half, BF16))
     scratch = (
@@ -426,7 +431,7 @@
         pltpu.VMEM((PAIRS * ROWS * SPAN, LANES), F32),
         pltpu.VMEM((HALF + EDGE + HALF, FLAT, LANES), F32),
     )
-    args = (scal, near(got), there, withs, jnp.asarray(backward_last()))
+    args = (scal, near(got), there, withs, near(tabs))
     return call(term_kernel, 16, [SMEM] + [VMEM] * 4, shapes, (VMEM,) * 3, scratch, args)
 
 
@@ -468,10 +473,11 @@
     send, there, withs, scal = start_call(info, partners, offsets, two, four, odd, own_box)
     got = shared(send)
     lowest = lax.ppermute(lowest, "slab", [(4, 0), (7, 1), (6, 2), (5, 3)])
-    scale, *tables = prepare_call(scal, kernel, upper, lowest)
-    send = wave_call(got, scale, tables)
+    scale, *tables = prepare_call(scal, kernel, upper)
+    send = wave_call(scal, got, scale, lowest, tables)
     got = shared(send)
-    move, odd_out, even_out = term_call(scal, got, there, withs)
+    tabs = ready_call(scal)
+    move, odd_out, even_out = term_call(scal, got, there, withs, tabs)
     crossed = other_core(odd_out)
     move = shared(move)
     by_two = even_out[0].astype(F32) + jnp.where(even_core, crossed[0], crossed[1]).astype(F32)

time: 99.5 us -> 98.3 us (0.988)
  the two profiles are of different devices: /device:TPU:10 before, /device:TPU:8 now
where the time goes in v5:
time: 98.3 us; the launch traced here: 97.5 us
  starting transfers between devices  57.8 us (59%)
  waiting for transfers between devices  25.2 us (26%)
  Pallas kernels  14.2 us (14%)
    ppermute x4, starting transfers between devices, passed_along(): lax.ppermute(block, 'orb', [((i - distance) % count, i) for i in range(co...  25.4 us
    all_to_all x4, starting transfers between devices, shared(): lax.all_to_all(block, 'slab', split_axis=0, concat_axis=0, tiled=True)  20.4 us
    pallas_call x8, Pallas kernels, call(): pl.pallas_call(kernel, out_shape=out_shape, in_specs=in_specs, out_specs=...  14.2 us
    all_to_all x4, waiting for transfers between devices, shared(): lax.all_to_all(block, 'slab', split_axis=0, concat_axis=0, tiled=True)  9.86 us
    ppermute x4, waiting for transfers between devices, passed_along(): lax.ppermute(block, 'orb', [((i - distance) % count, i) for i in range(co...  9.51 us
    ppermute x1, starting transfers between devices, per_device(): lax.ppermute(upper, 'slab', [(s, SLABS - 1 - s) for s in range(SLABS)])  4.57 us
    ppermute x2, starting transfers between devices, other_core(): return lax.ppermute(block, 'orb', [(i ^ 1, i) for i in range(count)])  3.96 us
    ppermute x1, starting transfers between devices, per_device(): lowest = lax.ppermute(lowest, 'slab', [(4, 0), (7, 1), (6, 2), (5, 3)])  3.4 us
  transfers between devices with their start and end apart: 12, of which 7 were waited for; matrix products, arithmetic and copies ran while one was open for 0% of the time, Pallas kernels for 2%

profile of v5, /device:TPU:8, one launch (start us, length us, event | category | flops | bytes accessed | tf_op | source)
XLA Modules:
  0.0 97.5 jit_solution(11142739443256776819)
XLA Ops:
  0.0 2.8 %shard_map.100 = (bf16[8,4224]{1,0:T(8,128)(2,1)S(1)}, bf16[8,8,4096]{2,1,0:T(8,128)(2,1)}) custom-call(s32[1,3]{1,0:T(1,128)} %corner.3, bf16[8,4096]{1,0:T(8,128)(2,1)} %bitcast.13), custom_call_target="tpu_custom_call" | custom-call | tf_op jit(solution)/shard_map/pallas_call | solution.py:365
  2.9 13.7 %collective-permute-start = (bf16[8,4224]{1,0:T(8,128)(2,1)S(1)}, bf16[8,4224]{1,0:T(8,128)(2,1)S(1)}, u32[]{:S(2)}, u32[]{:S(2)}) collective-permute-start(bf16[8,4224]{1,0:T(8,128)(2,1)S(1)} %get-tuple-element.21), channel_id=1, source_target_pairs={{16,0},{24,8},{32,16},{40,24},{48,32},{56,40},{64,48},{72,56},{80,... | collective-permute-start | bytes 202760 | tf_op jit(solution)/shard_map/ppermute | solution.py:447
  16.6 4.7 %collective-permute-start.1 = (bf16[8,4224]{1,0:T(8,128)(2,1)S(1)}, bf16[8,4224]{1,0:T(8,128)(2,1)S(1)}, u32[]{:S(2)}, u32[]{:S(2)}) collective-permute-start(bf16[8,4224]{1,0:T(8,128)(2,1)S(1)} %get-tuple-element.21), channel_id=1, source_target_pairs={{32,0},{40,8},{48,16},{56,24},{64,32},{72,40},{80,48},{88,56},{96,... | collective-permute-start | bytes 202760 | tf_op jit(solution)/shard_map/ppermute | solution.py:447
  21.3 0.0 copy-start.5
  21.3 0.0 copy-start.8
  21.4 0.0 copy-start.9
  21.4 5.9 %all-to-all-start = ((bf16[8,8,4096]{2,1,0:T(8,128)(2,1)}), bf16[8,8,4096]{2,1,0:T(8,128)(2,1)S(1)}, u32[]{:S(2)}, u32[]{:S(2)}) async-start(bf16[8,8,4096]{2,1,0:T(8,128)(2,1)} %get-tuple-element.22), calls=%async_computation | async-start | bytes 1048576 | tf_op jit(solution)/shard_map/all_to_all | solution.py:456
  27.3 0.0 copy-start
  27.3 0.0 collective-permute-done.two
  27.3 0.0 collective-permute-done.1.four
  27.3 2.1 %collective-permute-start.2 = (bf16[2,8,4224]{2,1,0:T(8,128)(2,1)S(1)}, bf16[2,8,4224]{2,1,0:T(8,128)(2,1)S(1)}, u32[]{:S(2)}, u32[]{:S(2)}) collective-permute-start(bf16[2,8,4224]{2,1,0:T(8,128)(2,1)S(1)} %pad_maximum_fusion), channel_id=1, source_target_pairs={{8,0},{0,8},{24,16},{16,24},{40,32},{32,40},{56,48},{48,56},{72,64... | collective-permute-start | bytes 405512 | tf_op jit(solution)/shard_map/ppermute | solution.py:452
  29.4 0.1 pad_add_fusion.info
  29.5 1.2 %collective-permute-done.2.odd = bf16[2,8,4224]{2,1,0:T(8,128)(2,1)S(1)} collective-permute-done((bf16[2,8,4224]{2,1,0:T(8,128)(2,1)S(1)}, bf16[2,8,4224]{2,1,0:T(8,128)(2,1)S(1)}, u32[]{:S(2)}, u32[]{:S(2)}) %collective-permute-start.2) | collective-permute-done | bytes 135200 | tf_op jit(solution)/shard_map/ppermute | solution.py:452
  30.7 4.6 %all-to-all-done.own_in = bf16[8,8,4096]{2,1,0:T(8,128)(2,1)S(1)} async-done(((bf16[8,8,4096]{2,1,0:T(8,128)(2,1)}), bf16[8,8,4096]{2,1,0:T(8,128)(2,1)S(1)}, u32[]{:S(2)}, u32[]{:S(2)}) %all-to-all-start) | async-done | bytes 524320 | tf_op jit(solution)/shard_map/all_to_all | solution.py:456
  35.3 0.0 copy-done.5
  35.3 0.0 copy-done.8
  35.3 0.0 copy-done.9
  35.3 2.2 %shard_map.101 = (bf16[8,2,4,16,128]{4,3,2,1,0:T(8,128)(2,1)}, bf16[2,8,32,128]{3,2,1,0:T(8,128)(2,1)}, bf16[2,8,32,128]{3,2,1,0:T(8,128)(2,1)}, s32[9]{0:T(128)S(1)}) custom-call(s32[2]{0:T(128)S(1)} %pad_add_fusion.info, s32[1,2]{1,0:T(1,128)S(1)} %copy-done.9, s32[1,3]{1,0:T(1,128)S(1)} %copy-done.8, bf16[8,4224]{1,0:T(8,128)(2,1)S(1)} %collective-permute-done.two, ...), custom_call_target="tpu_custom_call" | custom-call | tf_op jit(solution)/shard_map/pallas_call | solution.py:365
  37.6 4.4 %all-to-all-start.1 = ((bf16[8,2,4,16,128]{4,3,2,1,0:T(8,128)(2,1)}), bf16[8,2,4,16,128]{4,3,2,1,0:T(8,128)(2,1)S(1)}, u32[]{:S(2)}, u32[]{:S(2)}) async-start(bf16[8,2,4,16,128]{4,3,2,1,0:T(8,128)(2,1)} %get-tuple-element.24), calls=%async_computation.1 | async-start | bytes 524288 | tf_op jit(solution)/shard_map/all_to_all | solution.py:456
  42.0 0.0 copy-done
  42.0 0.0 copy-start.2
  42.0 0.0 copy-start.6
  42.0 0.0 copy-start.7
  42.0 0.2 shard_map.102
  42.2 4.6 %collective-permute-start.3 = (bf16[8,128,128]{2,1,0:T(8,128)(2,1)S(1)}, bf16[8,128,128]{2,1,0:T(8,128)(2,1)S(1)}, u32[]{:S(2)}, u32[]{:S(2)}) collective-permute-start(bf16[8,128,128]{2,1,0:T(8,128)(2,1)S(1)} %get-tuple-element.25), channel_id=1, source_target_pairs={{0,7},{1,6},{2,5},{3,4},{4,3},{5,2},{6,1},{7,0},{8,15},{9,14},{10,... | collective-permute-start | bytes 786440 | tf_op jit(solution)/shard_map/ppermute | solution.py:472
  46.8 3.4 %collective-permute-start.4 = (bf16[128,128]{1,0:T(8,128)(2,1)S(1)}, bf16[128,128]{1,0:T(8,128)(2,1)S(1)}, u32[]{:S(2)}, u32[]{:S(2)}) collective-permute-start(bf16[128,128]{1,0:T(8,128)(2,1)S(1)} %get-tuple-element.27), channel_id=1, source_target_pairs={{4,0},{7,1},{6,2},{5,3},{12,8},{15,9},{14,10},{13,11},{20,16},{23,... | collective-permute-start | bytes 98312 | tf_op jit(solution)/shard_map/ppermute | solution.py:475
  50.2 3.2 %collective-permute-done.3.upper = bf16[8,128,128]{2,1,0:T(8,128)(2,1)S(1)} collective-permute-done((bf16[8,128,128]{2,1,0:T(8,128)(2,1)S(1)}, bf16[8,128,128]{2,1,0:T(8,128)(2,1)S(1)}, u32[]{:S(2)}, u32[]{:S(2)}) %collective-permute-start.3) | collective-permute-done | bytes 262176 | tf_op jit(solution)/shard_map/ppermute | solution.py:472
  53.4 0.0 copy-done.2
  53.4 0.0 copy-done.6
  53.4 0.0 copy-done.7
  53.4 1.1 %shard_map.103 = (f32[9,128,128]{2,1,0:T(8,128)S(1)}, bf16[2,256,128]{2,1,0:T(8,128)(2,1)S(1)}, bf16[2,128,256]{2,1,0:T(8,128)(2,1)S(1)}, bf16[2,128,256]{2,1,0:T(8,128)(2,1)S(1)}, bf16[2,256,128]{2,1,0:T(8,128)(2,1)S(1)}) custom-call(s32[9]{0:T(128)S(1)} %get-tuple-element.23.scal, f32[128,16,128]{2,1,0:T(8,128)S(1)} %copy-done, ...), custom_call_target="tpu_custom_call" | custom-call | tf_op jit(solution)/shard_map/pallas_call | solution.py:365
  54.5 0.0 collective-permute-done.4.lowest
  54.5 0.0 all-to-all-done.1.got
  54.5 4.4 %shard_map.104 = bf16[8,2,4,16,128]{4,3,2,1,0:T(8,128)(2,1)} custom-call(s32[9]{0:T(128)S(1)} %get-tuple-element.23.scal, bf16[8,2,4,16,128]{4,3,2,1,0:T(8,128)(2,1)S(1)} %all-to-all-done.1.got, f32[9,128,128]{2,1,0:T(8,128)S(1)} %get-tuple-element.26.scale_t, bf16[128,128]{1,0:T(8,128)(2,1)S(1)} %collective-permute-done.4.lowest, ...), custom_call_target="tpu_custom_call" | custom-call | tf_op jit(solution)/shard_map/pallas_call | solution.py:365
  59.0 0.0 copy-start.1
  59.0 5.3 %all-to-all-start.2 = ((bf16[8,2,4,16,128]{4,3,2,1,0:T(8,128)(2,1)}), bf16[8,2,4,16,128]{4,3,2,1,0:T(8,128)(2,1)S(1)}, u32[]{:S(2)}, u32[]{:S(2)}) async-start(bf16[8,2,4,16,128]{4,3,2,1,0:T(8,128)(2,1)} %shard_map.104), calls=%async_computation.2 | async-start | bytes 524288 | tf_op jit(solution)/shard_map/all_to_all | solution.py:456
  64.3 0.0 copy-done.1
  64.3 0.0 copy-start.3
  64.3 0.0 copy-start.4
  64.3 0.6 shard_map.105.tabs
  64.9 5.2 %all-to-all-done.2.got = bf16[8,2,4,16,128]{4,3,2,1,0:T(8,128)(2,1)S(1)} async-done(((bf16[8,2,4,16,128]{4,3,2,1,0:T(8,128)(2,1)}), bf16[8,2,4,16,128]{4,3,2,1,0:T(8,128)(2,1)S(1)}, u32[]{:S(2)}, u32[]{:S(2)}) %all-to-all-start.2) | async-done | bytes 262176 | tf_op jit(solution)/shard_map/all_to_all | solution.py:456
  70.1 0.0 copy-done.3
  70.1 0.0 copy-done.4
  70.1 2.0 %shard_map.106 = (bf16[8,8,32,128]{3,2,1,0:T(8,128)(2,1)}, bf16[2,8,32,128]{3,2,1,0:T(8,128)(2,1)S(1)}, bf16[2,8,32,128]{3,2,1,0:T(8,128)(2,1)S(1)}) custom-call(s32[9]{0:T(128)S(1)} %get-tuple-element.23.scal, bf16[8,2,4,16,128]{4,3,2,1,0:T(8,128)(2,1)S(1)} %all-to-all-done.2.got, bf16[2,8,32,128]{3,2,1,0:T(8,128)(2,1)S(1)} %copy-done.3, ...), custom_call_target="tpu_custom_call" | custom-call | tf_op jit(solution)/shard_map/pallas_call | solution.py:365
  72.2 4.8 %all-to-all-start.3 = ((bf16[8,8,32,128]{3,2,1,0:T(8,128)(2,1)}), bf16[8,8,32,128]{3,2,1,0:T(8,128)(2,1)S(1)}, u32[]{:S(2)}, u32[]{:S(2)}) async-start(bf16[8,8,32,128]{3,2,1,0:T(8,128)(2,1)} %get-tuple-element.34), calls=%async_computation.3 | async-start | bytes 1048576 | tf_op jit(solution)/shard_map/all_to_all | solution.py:456
  77.0 1.9 %collective-permute-start.5 = (bf16[2,8,32,128]{3,2,1,0:T(8,128)(2,1)S(1)}, bf16[2,8,32,128]{3,2,1,0:T(8,128)(2,1)S(1)}, u32[]{:S(2)}, u32[]{:S(2)}) collective-permute-start(bf16[2,8,32,128]{3,2,1,0:T(8,128)(2,1)S(1)} %get-tuple-element.35), channel_id=1, source_target_pairs={{8,0},{0,8},{24,16},{16,24},{40,32},{32,40},{56,48},{48,56},{72,64... | collective-permute-start | bytes 393224 | tf_op jit(solution)/shard_map/ppermute | solution.py:452
  78.9 1.3 %collective-permute-done.5.crossed = bf16[2,8,32,128]{3,2,1,0:T(8,128)(2,1)S(1)} collective-permute-done((bf16[2,8,32,128]{3,2,1,0:T(8,128)(2,1)S(1)}, bf16[2,8,32,128]{3,2,1,0:T(8,128)(2,1)S(1)}, u32[]{:S(2)}, u32[]{:S(2)}) %collective-permute-start.5) | collective-permute-done | bytes 131104 | tf_op jit(solution)/shard_map/ppermute | solution.py:452
  80.3 3.6 %collective-permute-start.6 = (bf16[8,32,128]{2,1,0:T(8,128)(2,1)S(1)}, bf16[8,32,128]{2,1,0:T(8,128)(2,1)S(1)}, u32[]{:S(2)}, u32[]{:S(2)}) collective-permute-start(bf16[8,32,128]{2,1,0:T(8,128)(2,1)S(1)} %get-tuple-element.38), channel_id=1, source_target_pairs={{496,0},{504,8},{0,16},{8,24},{16,32},{24,40},{32,48},{40,56},{48,... | collective-permute-start | bytes 196616 | tf_op jit(solution)/shard_map/ppermute | solution.py:447
  83.9 3.4 %collective-permute-start.7 = (bf16[8,32,128]{2,1,0:T(8,128)(2,1)S(1)}, bf16[8,32,128]{2,1,0:T(8,128)(2,1)S(1)}, u32[]{:S(2)}, u32[]{:S(2)}) collective-permute-start(bf16[8,32,128]{2,1,0:T(8,128)(2,1)S(1)} %get-tuple-element.37), channel_id=1, source_target_pairs={{480,0},{488,8},{496,16},{504,24},{0,32},{8,40},{16,48},{24,56},{3... | collective-permute-start | bytes 196616 | tf_op jit(solution)/shard_map/ppermute | solution.py:447
  87.3 4.6 %collective-permute-done.6.two = bf16[8,32,128]{2,1,0:T(8,128)(2,1)S(1)} collective-permute-done((bf16[8,32,128]{2,1,0:T(8,128)(2,1)S(1)}, bf16[8,32,128]{2,1,0:T(8,128)(2,1)S(1)}, u32[]{:S(2)}, u32[]{:S(2)}) %collective-permute-start.6) | collective-permute-done | bytes 65568 | tf_op jit(solution)/shard_map/ppermute | solution.py:447
  91.9 4.9 %collective-permute-done.7.four = bf16[8,32,128]{2,1,0:T(8,128)(2,1)S(1)} collective-permute-done((bf16[8,32,128]{2,1,0:T(8,128)(2,1)S(1)}, bf16[8,32,128]{2,1,0:T(8,128)(2,1)S(1)}, u32[]{:S(2)}, u32[]{:S(2)}) %collective-permute-start.7) | collective-permute-done | bytes 65568 | tf_op jit(solution)/shard_map/ppermute | solution.py:447
  96.8 0.0 all-to-all-done.3.moved
  96.8 0.8 shard_map.107
  (3 shorter events, 0.1 us)
Async XLA Ops:
  2.9 24.4 %collective-permute-start = (bf16[8,4224]{1,0:T(8,128)(2,1)S(1)}, bf16[8,4224]{1,0:T(8,128)(2,1)S(1)}, u32[]{:S(2)}, u32[]{:S(2)}) collective-permute-start(bf16[8,4224]{1,0:T(8,128)(2,1)S(1)} %get-tuple-element.21), channel_id=1, source_target_pairs={{16,0},{24,8},{32,16},{40,24},{48,32},{56,40},{64,48},{72,56},{80,... | collective-permute-start | bytes 202760 | tf_op jit(solution)/shard_map/ppermute | solution.py:447
  16.6 10.7 %collective-permute-start.1 = (bf16[8,4224]{1,0:T(8,128)(2,1)S(1)}, bf16[8,4224]{1,0:T(8,128)(2,1)S(1)}, u32[]{:S(2)}, u32[]{:S(2)}) collective-permute-start(bf16[8,4224]{1,0:T(8,128)(2,1)S(1)} %get-tuple-element.21), channel_id=1, source_target_pairs={{32,0},{40,8},{48,16},{56,24},{64,32},{72,40},{80,48},{88,56},{96,... | collective-permute-start | bytes 202760 | tf_op jit(solution)/shard_map/ppermute | solution.py:447
  21.3 14.0 %copy-start.5 = (f32[128,128]{1,0:T(8,128)S(1)}, f32[128,128]{1,0:T(8,128)}, u32[]{:S(2)}) copy-start(f32[128,128]{1,0:T(8,128)} %constant.38.clone.first_t) | copy-start | bytes 196612
  21.3 14.0 %copy-start.8 = (s32[1,3]{1,0:T(1,128)S(1)}, s32[1,3]{1,0:T(1,128)}, u32[]{:S(2)}) copy-start(s32[1,3]{1,0:T(1,128)} %corner.3) | copy-start | bytes 40
  21.4 14.0 %copy-start.9 = (s32[1,2]{1,0:T(1,128)S(1)}, s32[1,2]{1,0:T(1,128)}, u32[]{:S(2)}) copy-start(s32[1,2]{1,0:T(1,128)} %partners.1) | copy-start | bytes 28
  21.4 14.0 %all-to-all-start = ((bf16[8,8,4096]{2,1,0:T(8,128)(2,1)}), bf16[8,8,4096]{2,1,0:T(8,128)(2,1)S(1)}, u32[]{:S(2)}, u32[]{:S(2)}) async-start(bf16[8,8,4096]{2,1,0:T(8,128)(2,1)} %get-tuple-element.22), calls=%async_computation | async-start | bytes 1048576 | tf_op jit(solution)/shard_map/all_to_all | solution.py:456
  27.3 14.7 %copy-start = (f32[128,16,128]{2,1,0:T(8,128)S(1)}, f32[128,16,128]{2,1,0:T(8,128)}, u32[]{:S(2)}) copy-start(f32[128,16,128]{2,1,0:T(8,128)} %kern.3) | copy-start | bytes 3145732
  27.3 3.4 %collective-permute-start.2 = (bf16[2,8,4224]{2,1,0:T(8,128)(2,1)S(1)}, bf16[2,8,4224]{2,1,0:T(8,128)(2,1)S(1)}, u32[]{:S(2)}, u32[]{:S(2)}) collective-permute-start(bf16[2,8,4224]{2,1,0:T(8,128)(2,1)S(1)} %pad_maximum_fusion), channel_id=1, source_target_pairs={{8,0},{0,8},{24,16},{16,24},{40,32},{32,40},{56,48},{48,56},{72,64... | collective-permute-start | bytes 405512 | tf_op jit(solution)/shard_map/ppermute | solution.py:452
  37.6 16.9 %all-to-all-start.1 = ((bf16[8,2,4,16,128]{4,3,2,1,0:T(8,128)(2,1)}), bf16[8,2,4,16,128]{4,3,2,1,0:T(8,128)(2,1)S(1)}, u32[]{:S(2)}, u32[]{:S(2)}) async-start(bf16[8,2,4,16,128]{4,3,2,1,0:T(8,128)(2,1)} %get-tuple-element.24), calls=%async_computation.1 | async-start | bytes 524288 | tf_op jit(solution)/shard_map/all_to_all | solution.py:456
  42.0 11.4 %copy-start.2 = (bf16[128,128]{1,0:T(8,128)(2,1)S(1)}, bf16[128,128]{1,0:T(8,128)(2,1)}, u32[]{:S(2)}) copy-start(bf16[128,128]{1,0:T(8,128)(2,1)} %constant.39.clone.flip_t) | copy-start | bytes 98308
  42.0 11.4 %copy-start.6 = (f32[128,128]{1,0:T(8,128)S(1)}, f32[128,128]{1,0:T(8,128)}, u32[]{:S(2)}) copy-start(f32[128,128]{1,0:T(8,128)} %constant.40.clone.cos_f) | copy-start | bytes 196612
  42.0 11.4 %copy-start.7 = (f32[128,128]{1,0:T(8,128)S(1)}, f32[128,128]{1,0:T(8,128)}, u32[]{:S(2)}) copy-start(f32[128,128]{1,0:T(8,128)} %constant.41.clone.sin_f) | copy-start | bytes 196612
  42.2 11.2 %collective-permute-start.3 = (bf16[8,128,128]{2,1,0:T(8,128)(2,1)S(1)}, bf16[8,128,128]{2,1,0:T(8,128)(2,1)S(1)}, u32[]{:S(2)}, u32[]{:S(2)}) collective-permute-start(bf16[8,128,128]{2,1,0:T(8,128)(2,1)S(1)} %get-tuple-element.25), channel_id=1, source_target_pairs={{0,7},{1,6},{2,5},{3,4},{4,3},{5,2},{6,1},{7,0},{8,15},{9,14},{10,... | collective-permute-start | bytes 786440 | tf_op jit(solution)/shard_map/ppermute | solution.py:472
  46.8 7.7 %collective-permute-start.4 = (bf16[128,128]{1,0:T(8,128)(2,1)S(1)}, bf16[128,128]{1,0:T(8,128)(2,1)S(1)}, u32[]{:S(2)}, u32[]{:S(2)}) collective-permute-start(bf16[128,128]{1,0:T(8,128)(2,1)S(1)} %get-tuple-element.27), channel_id=1, source_target_pairs={{4,0},{7,1},{6,2},{5,3},{12,8},{15,9},{14,10},{13,11},{20,16},{23,... | collective-permute-start | bytes 98312 | tf_op jit(solution)/shard_map/ppermute | solution.py:475
  59.0 5.3 %copy-start.1 = (f32[512,128]{1,0:T(8,128)S(1)}, f32[512,128]{1,0:T(8,128)}, u32[]{:S(2)}) copy-start(f32[512,128]{1,0:T(8,128)} %constant.42.clone.last_t) | copy-start | bytes 786436
  59.0 11.2 %all-to-all-start.2 = ((bf16[8,2,4,16,128]{4,3,2,1,0:T(8,128)(2,1)}), bf16[8,2,4,16,128]{4,3,2,1,0:T(8,128)(2,1)S(1)}, u32[]{:S(2)}, u32[]{:S(2)}) async-start(bf16[8,2,4,16,128]{4,3,2,1,0:T(8,128)(2,1)} %shard_map.104), calls=%async_computation.2 | async-start | bytes 524288 | tf_op jit(solution)/shard_map/all_to_all | solution.py:456
  64.3 5.8 %copy-start.3 = (bf16[2,8,32,128]{3,2,1,0:T(8,128)(2,1)S(1)}, bf16[2,8,32,128]{3,2,1,0:T(8,128)(2,1)}, u32[]{:S(2)}) copy-start(bf16[2,8,32,128]{3,2,1,0:T(8,128)(2,1)} %get-tuple-element.32.there) | copy-start | bytes 393220
  64.3 5.8 %copy-start.4 = (bf16[2,8,32,128]{3,2,1,0:T(8,128)(2,1)S(1)}, bf16[2,8,32,128]{3,2,1,0:T(8,128)(2,1)}, u32[]{:S(2)}) copy-start(bf16[2,8,32,128]{3,2,1,0:T(8,128)(2,1)} %get-tuple-element.33.withs) | copy-start | bytes 393220
  72.2 24.6 %all-to-all-start.3 = ((bf16[8,8,32,128]{3,2,1,0:T(8,128)(2,1)}), bf16[8,8,32,128]{3,2,1,0:T(8,128)(2,1)S(1)}, u32[]{:S(2)}, u32[]{:S(2)}) async-start(bf16[8,8,32,128]{3,2,1,0:T(8,128)(2,1)} %get-tuple-element.34), calls=%async_computation.3 | async-start | bytes 1048576 | tf_op jit(solution)/shard_map/all_to_all | solution.py:456
  77.0 3.2 %collective-permute-start.5 = (bf16[2,8,32,128]{3,2,1,0:T(8,128)(2,1)S(1)}, bf16[2,8,32,128]{3,2,1,0:T(8,128)(2,1)S(1)}, u32[]{:S(2)}, u32[]{:S(2)}) collective-permute-start(bf16[2,8,32,128]{3,2,1,0:T(8,128)(2,1)S(1)} %get-tuple-element.35), channel_id=1, source_target_pairs={{8,0},{0,8},{24,16},{16,24},{40,32},{32,40},{56,48},{48,56},{72,64... | collective-permute-start | bytes 393224 | tf_op jit(solution)/shard_map/ppermute | solution.py:452
  80.3 11.6 %collective-permute-start.6 = (bf16[8,32,128]{2,1,0:T(8,128)(2,1)S(1)}, bf16[8,32,128]{2,1,0:T(8,128)(2,1)S(1)}, u32[]{:S(2)}, u32[]{:S(2)}) collective-permute-start(bf16[8,32,128]{2,1,0:T(8,128)(2,1)S(1)} %get-tuple-element.38), channel_id=1, source_target_pairs={{496,0},{504,8},{0,16},{8,24},{16,32},{24,40},{32,48},{40,56},{48,... | collective-permute-start | bytes 196616 | tf_op jit(solution)/shard_map/ppermute | solution.py:447
  83.9 12.9 %collective-permute-start.7 = (bf16[8,32,128]{2,1,0:T(8,128)(2,1)S(1)}, bf16[8,32,128]{2,1,0:T(8,128)(2,1)S(1)}, u32[]{:S(2)}, u32[]{:S(2)}) collective-permute-start(bf16[8,32,128]{2,1,0:T(8,128)(2,1)S(1)} %get-tuple-element.37), channel_id=1, source_target_pairs={{480,0},{488,8},{496,16},{504,24},{0,32},{8,40},{16,48},{24,56},{3... | collective-permute-start | bytes 196616 | tf_op jit(solution)/shard_map/ppermute | solution.py:447

commit v6 on v5

--- a/solution.py
+++ b/solution.py
@@ -103,11 +103,14 @@
         ref[c * SPAN + PAD + FLAT : (c + 1) * SPAN, :] = zeros
 
 
-def load_kernel(corner, own, loaded, copies, sems):
+def load_kernel(corner_h, own, loaded, copies, corner, sems):
+    mark_load = pltpu.make_async_copy(corner_h, corner, sems.at[SLABS + 1])
+    mark_load.start()
     loads = [pltpu.make_async_copy(own, copies.at[t], sems.at[t]) for t in range(SLABS)]
     loads.append(pltpu.make_async_copy(own, loaded.at[:, pl.ds(0, CELLS)], sems.at[SLABS]))
     for one in loads:
         one.start()
+    mark_load.wait()
     lane = lanes_of((ROWS, LANES))
     mark = jnp.zeros((ROWS, LANES), F32)
     for k in range(3):
@@ -126,11 +129,7 @@
 
 def start_kernel(info, partners, corner, two, four, odd, own_in, first_t, send, there_out, with_out, scal, own_s, part_s):
     slab, orbit = info[0], info[1]
-    clear_edges(own_s, EDGE)
-    for t in range(SLABS):
-        for k in range(FLAT):
-            piece = own_in[t, :, k * LANES : (k + 1) * LANES].astype(F32)
-            own_s[pl.ds(t * ROWS * SPAN + PAD + k, ROWS, stride=SPAN), :] = piece
+    clear_edges(own_s, 2 * ROWS)
     scal[0] = slab
     low_d = low_half((FLAT, LANES))
     low_w = low_half((EDGE, LANES))
@@ -157,10 +156,16 @@
         halves = [first_t[pl.ds(HALF + d1 + par, FLAT, stride=2), :] for par in range(2)]
         first = jnp.concatenate(halves, axis=0).T.astype(BF16)
         sides = []
+        window = slab + (d0 >> 3)
+        for w in range(2):
+            t = jnp.clip(window + w, 0, SLABS - 1)
+            for k in range(FLAT):
+                piece = own_in[t, :, k * LANES : (k + 1) * LANES].astype(F32)
+                own_s[pl.ds(w * ROWS * SPAN + PAD + k, ROWS, stride=SPAN), :] = piece
         for r in range(ROWS):
             source = slab * ROWS + r + d0
             inside = jnp.logical_and(source >= 0, source < EDGE)
-            base = jnp.clip(source, 0, EDGE - 1) * SPAN + PAD
+            base = (r + (d0 & (ROWS - 1))) * SPAN + PAD
             there = jnp.where(inside, shifted(own_s, base, -d1, -d2), 0.0)
             part = part_s[r * RSPAN : r * RSPAN + FLAT, :]
             there_out[n, r] = there.astype(BF16)
@@ -329,10 +334,10 @@
             target[(e - 1) // 2, row] = value.astype(BF16)
 
 
-def final_kernel(odd_core, moved, crossed, two, four, out, total_s):
+def final_kernel(odd_core, moved, crossed, back, out, total_s):
     keep = odd_core[0] == 1
     for r in range(ROWS):
-        total = two[r].astype(F32) + four[r].astype(F32) + jnp.where(keep, crossed[0, r].astype(F32), 0.0)
+        total = back[r].astype(F32) + jnp.where(keep, crossed[0, r].astype(F32), 0.0)
         for t in range(SLABS):
             total = total + moved[t, r].astype(F32)
         total_s[r * RSPAN : r * RSPAN + FLAT, :] = total
@@ -347,10 +352,6 @@
 
 def kept(shape, dtype):
     return pltpu.VMEM(shape, dtype)
-
-
-def far(shape, dtype):
-    return pltpu.HBM(shape, dtype)
 
 
 def away(x):
@@ -380,8 +381,8 @@
 
 def load_call(offsets, own):
     shapes = (kept((ROWS, CELLS + LANES), BF16), kept((SLABS, ROWS, CELLS), BF16))
-    scratch = (pltpu.SemaphoreType.DMA((SLABS + 1,)),)
-    return call(load_kernel, 8, [SMEM, HBM], shapes, (VMEM,) * 2, scratch, (away(offsets), away(own)))
+    scratch = (pltpu.SMEM((1, 3), jnp.int32), pltpu.SemaphoreType.DMA((SLABS + 2,)))
+    return call(load_kernel, 8, [HBM, HBM], shapes, (VMEM,) * 2, scratch, (away(offsets), away(own)))
 
 
 def mirror_call(kernel):
@@ -390,8 +391,8 @@
 
 
 def start_call(info, partners, offsets, two, four, odd, own_box):
-    shapes = (far(PACKET, BF16), far(ROWBOX, BF16), far(ROWBOX, BF16), jax.ShapeDtypeStruct((9,), jnp.int32))
-    scratch = (pltpu.VMEM((EDGE * SPAN, LANES), F32), pltpu.VMEM((ROWS * RSPAN, LANES), F32))
+    shapes = (kept(PACKET, BF16), kept(ROWBOX, BF16), kept(ROWBOX, BF16), jax.ShapeDtypeStruct((9,), jnp.int32))
+    scratch = (pltpu.VMEM((2 * ROWS * SPAN, LANES), F32), pltpu.VMEM((ROWS * RSPAN, LANES), F32))
     args = (info, partners, offsets, near(two), near(four), near(odd), near(own_box), jnp.asarray(forward_first()))
     return call(start_kernel, 12, [SMEM] * 3 + [VMEM] * 5, shapes, (VMEM,) * 3 + (SMEM,), scratch, args)
 
@@ -415,7 +416,7 @@
         pltpu.VMEM((PAIRS * EDGE * BSPAN, LANES), F32),
     )
     args = (scal, near(got), near(scale), near(lowest), *(near(t) for t in tables), jnp.asarray(reversal()))
-    return call(wave_kernel, 12, [SMEM] + [VMEM] * 8, far(PACKET, BF16), VMEM, scratch, args)
+    return call(wave_kernel, 12, [SMEM] + [VMEM] * 8, kept(PACKET, BF16), VMEM, scratch, args)
 
 
 def ready_call(scal):
@@ -425,21 +426,21 @@
 
 def term_call(scal, got, there, withs, tabs):
     half = (2, ROWS, FLAT, LANES)
-    shapes = (far((SLABS, ROWS, FLAT, LANES), BF16), kept(half, BF16), kept(half, BF16))
+    shapes = (kept((SLABS, ROWS, FLAT, LANES), BF16), kept(half, BF16), kept(half, BF16))
     scratch = (
         pltpu.VMEM(ROWBOX, F32),
         pltpu.VMEM((PAIRS * ROWS * SPAN, LANES), F32),
         pltpu.VMEM((HALF + EDGE + HALF, FLAT, LANES), F32),
     )
-    args = (scal, near(got), there, withs, near(tabs))
+    args = (scal, near(got), near(there), near(withs), near(tabs))
     return call(term_kernel, 16, [SMEM] + [VMEM] * 4, shapes, (VMEM,) * 3, scratch, args)
 
 
-def final_call(odd_core, moved, crossed, two, four):
+def final_call(odd_core, moved, crossed, back):
     scratch = (pltpu.VMEM((ROWS * RSPAN, LANES), F32),)
     shape = jax.ShapeDtypeStruct((ROWS, CELLS), F32)
-    args = (odd_core, near(moved), near(crossed), near(two), near(four))
-    return call(final_kernel, 8, [SMEM] + [VMEM] * 4, shape, VMEM, scratch, args)
+    args = (odd_core, near(moved), near(crossed), near(back))
+    return call(final_kernel, 8, [SMEM] + [VMEM] * 3, shape, VMEM, scratch, args)
 
 
 def passed_along(block, distance):
@@ -463,9 +464,9 @@
     info = jnp.stack([slab, orbit])
     odd_core = (orbit % 2)[None]
     loaded, copies = load_call(offsets, orbitals[0])
-    four = passed_along(loaded, -4)
     two = passed_along(loaded, -2)
     own_box = shared(copies)
+    four = passed_along(two, -2)
     upper, lowest = mirror_call(kernel)
     given = jnp.stack([jnp.where(even_core, two, loaded), jnp.where(even_core, four, two)])
     odd = other_core(given)
@@ -482,9 +483,9 @@
     move = shared(move)
     by_two = even_out[0].astype(F32) + jnp.where(even_core, crossed[0], crossed[1]).astype(F32)
     by_four = even_out[1].astype(F32) + jnp.where(even_core, crossed[1], 0.0).astype(F32)
-    four_back = passed_along(by_four.astype(BF16), 4)
-    two_back = passed_along(by_two.astype(BF16), 2)
-    return final_call(odd_core, move, crossed, two_back, four_back)[None]
+    half_way = passed_along(by_four.astype(BF16), 2)
+    back = passed_along((by_two + half_way.astype(F32)).astype(BF16), 2)
+    return final_call(odd_core, move, crossed, back)[None]
 
 
 def solution(mesh):

time: 98.3 us -> 110 us (1.12)
  the two profiles are of different devices: /device:TPU:8 before, /device:TPU:10 now
where the time goes in v6:
time: 110 us; the launch traced here: 109 us
  starting transfers between devices  60.9 us (55%)
  waiting for transfers between devices  34.5 us (31%)
  Pallas kernels  13.5 us (12%)
    ppermute x4, starting transfers between devices, passed_along(): lax.ppermute(block, 'orb', [((i - distance) % count, i) for i in range(co...  26.1 us
    all_to_all x4, starting transfers between devices, shared(): lax.all_to_all(block, 'slab', split_axis=0, concat_axis=0, tiled=True)  23.6 us
    ppermute x4, waiting for transfers between devices, passed_along(): lax.ppermute(block, 'orb', [((i - distance) % count, i) for i in range(co...  20.2 us
    pallas_call x8, Pallas kernels, call(): pl.pallas_call(kernel, out_shape=out_shape, in_specs=in_specs, out_specs=...  13.5 us
    all_to_all x4, waiting for transfers between devices, shared(): lax.all_to_all(block, 'slab', split_axis=0, concat_axis=0, tiled=True)  8.81 us
    ppermute x1, starting transfers between devices, per_device(): lowest = lax.ppermute(lowest, 'slab', [(4, 0), (7, 1), (6, 2), (5, 3)])  3.99 us
    ppermute x2, starting transfers between devices, other_core(): return lax.ppermute(block, 'orb', [(i ^ 1, i) for i in range(count)])  3.96 us
    ppermute x1, starting transfers between devices, per_device(): lax.ppermute(upper, 'slab', [(s, SLABS - 1 - s) for s in range(SLABS)])  3.35 us
  transfers between devices with their start and end apart: 12, of which 8 were waited for; matrix products, arithmetic and copies ran while one was open for 0% of the time, Pallas kernels for 2%

profile of v6, /device:TPU:10, one launch (start us, length us, event | category | flops | bytes accessed | tf_op | source)
XLA Modules:
  0.0 109.4 jit_solution(4307333613151670866)
XLA Ops:
  0.0 2.2 %shard_map.100 = (bf16[8,4224]{1,0:T(8,128)(2,1)S(1)}, bf16[8,8,4096]{2,1,0:T(8,128)(2,1)}) custom-call(s32[1,3]{1,0:T(1,128)} %corner.1, bf16[8,4096]{1,0:T(8,128)(2,1)} %bitcast.15), custom_call_target="tpu_custom_call" | custom-call | tf_op jit(solution)/shard_map/pallas_call | solution.py:366
  2.2 13.7 %collective-permute-start = (bf16[8,4224]{1,0:T(8,128)(2,1)S(1)}, bf16[8,4224]{1,0:T(8,128)(2,1)S(1)}, u32[]{:S(2)}, u32[]{:S(2)}) collective-permute-start(bf16[8,4224]{1,0:T(8,128)(2,1)S(1)} %get-tuple-element.21), channel_id=1, source_target_pairs={{16,0},{24,8},{32,16},{40,24},{48,32},{56,40},{64,48},{72,56},{80,... | collective-permute-start | bytes 202760 | tf_op jit(solution)/shard_map/ppermute | solution.py:448
  16.0 1.9 %collective-permute-done.two = bf16[8,4224]{1,0:T(8,128)(2,1)S(1)} collective-permute-done((bf16[8,4224]{1,0:T(8,128)(2,1)S(1)}, bf16[8,4224]{1,0:T(8,128)(2,1)S(1)}, u32[]{:S(2)}, u32[]{:S(2)}) %collective-permute-start) | collective-permute-done | bytes 67616 | tf_op jit(solution)/shard_map/ppermute | solution.py:448
  17.9 8.5 %collective-permute-start.1 = (bf16[8,4224]{1,0:T(8,128)(2,1)S(1)}, bf16[8,4224]{1,0:T(8,128)(2,1)S(1)}, u32[]{:S(2)}, u32[]{:S(2)}) collective-permute-start(bf16[8,4224]{1,0:T(8,128)(2,1)S(1)} %collective-permute-done.two), channel_id=1, source_target_pairs={{16,0},{24,8},{32,16},{40,24},{48,32},{56,40},{64,48},{72,56},{80,... | collective-permute-start | bytes 202760 | tf_op jit(solution)/shard_map/ppermute | solution.py:448
  26.3 0.0 copy-start.3
  26.4 0.0 copy-start.6
  26.4 0.0 copy-start.7
  26.4 6.8 %all-to-all-start = ((bf16[8,8,4096]{2,1,0:T(8,128)(2,1)}), bf16[8,8,4096]{2,1,0:T(8,128)(2,1)S(1)}, u32[]{:S(2)}, u32[]{:S(2)}) async-start(bf16[8,8,4096]{2,1,0:T(8,128)(2,1)} %get-tuple-element.22), calls=%async_computation | async-start | bytes 1048576 | tf_op jit(solution)/shard_map/all_to_all | solution.py:457
  33.2 0.0 copy-start
  33.2 0.0 collective-permute-done.1.four
  33.2 2.1 %collective-permute-start.2 = (bf16[2,8,4224]{2,1,0:T(8,128)(2,1)S(1)}, bf16[2,8,4224]{2,1,0:T(8,128)(2,1)S(1)}, u32[]{:S(2)}, u32[]{:S(2)}) collective-permute-start(bf16[2,8,4224]{2,1,0:T(8,128)(2,1)S(1)} %pad_maximum_fusion), channel_id=1, source_target_pairs={{8,0},{0,8},{24,16},{16,24},{40,32},{32,40},{56,48},{48,56},{72,64... | collective-permute-start | bytes 405512 | tf_op jit(solution)/shard_map/ppermute | solution.py:453
  35.3 0.1 pad_add_fusion.info
  35.4 1.2 %collective-permute-done.2.odd = bf16[2,8,4224]{2,1,0:T(8,128)(2,1)S(1)} collective-permute-done((bf16[2,8,4224]{2,1,0:T(8,128)(2,1)S(1)}, bf16[2,8,4224]{2,1,0:T(8,128)(2,1)S(1)}, u32[]{:S(2)}, u32[]{:S(2)}) %collective-permute-start.2) | collective-permute-done | bytes 135200 | tf_op jit(solution)/shard_map/ppermute | solution.py:453
  36.6 4.2 %all-to-all-done.own_in = bf16[8,8,4096]{2,1,0:T(8,128)(2,1)S(1)} async-done(((bf16[8,8,4096]{2,1,0:T(8,128)(2,1)}), bf16[8,8,4096]{2,1,0:T(8,128)(2,1)S(1)}, u32[]{:S(2)}, u32[]{:S(2)}) %all-to-all-start) | async-done | bytes 524320 | tf_op jit(solution)/shard_map/all_to_all | solution.py:457
  40.8 0.0 copy-done.3
  40.8 0.0 copy-done.6
  40.8 0.0 copy-done.7
  40.8 2.2 %shard_map.101 = (bf16[8,2,4,16,128]{4,3,2,1,0:T(8,128)(2,1)}, bf16[2,8,32,128]{3,2,1,0:T(8,128)(2,1)S(1)}, bf16[2,8,32,128]{3,2,1,0:T(8,128)(2,1)S(1)}, s32[9]{0:T(128)S(1)}) custom-call(s32[2]{0:T(128)S(1)} %pad_add_fusion.info, s32[1,2]{1,0:T(1,128)S(1)} %copy-done.7, s32[1,3]{1,0:T(1,128)S(1)} %copy-done.6, ...), custom_call_target="tpu_custom_call" | custom-call | tf_op jit(solution)/shard_map/pallas_call | solution.py:366
  43.0 5.0 %all-to-all-start.1 = ((bf16[8,2,4,16,128]{4,3,2,1,0:T(8,128)(2,1)}), bf16[8,2,4,16,128]{4,3,2,1,0:T(8,128)(2,1)S(1)}, u32[]{:S(2)}, u32[]{:S(2)}) async-start(bf16[8,2,4,16,128]{4,3,2,1,0:T(8,128)(2,1)} %get-tuple-element.24), calls=%async_computation.1 | async-start | bytes 524288 | tf_op jit(solution)/shard_map/all_to_all | solution.py:457
  48.0 0.0 copy-done
  48.0 0.0 copy-start.2
  48.0 0.0 copy-start.4
  48.0 0.0 copy-start.5
  48.0 0.2 shard_map.102
  48.2 3.4 %collective-permute-start.3 = (bf16[8,128,128]{2,1,0:T(8,128)(2,1)S(1)}, bf16[8,128,128]{2,1,0:T(8,128)(2,1)S(1)}, u32[]{:S(2)}, u32[]{:S(2)}) collective-permute-start(bf16[8,128,128]{2,1,0:T(8,128)(2,1)S(1)} %get-tuple-element.25), channel_id=1, source_target_pairs={{0,7},{1,6},{2,5},{3,4},{4,3},{5,2},{6,1},{7,0},{8,15},{9,14},{10,... | collective-permute-start | bytes 786440 | tf_op jit(solution)/shard_map/ppermute | solution.py:473
  51.6 4.0 %collective-permute-start.4 = (bf16[128,128]{1,0:T(8,128)(2,1)S(1)}, bf16[128,128]{1,0:T(8,128)(2,1)S(1)}, u32[]{:S(2)}, u32[]{:S(2)}) collective-permute-start(bf16[128,128]{1,0:T(8,128)(2,1)S(1)} %get-tuple-element.27), channel_id=1, source_target_pairs={{4,0},{7,1},{6,2},{5,3},{12,8},{15,9},{14,10},{13,11},{20,16},{23,... | collective-permute-start | bytes 98312 | tf_op jit(solution)/shard_map/ppermute | solution.py:476
  55.6 3.0 %collective-permute-done.3.upper = bf16[8,128,128]{2,1,0:T(8,128)(2,1)S(1)} collective-permute-done((bf16[8,128,128]{2,1,0:T(8,128)(2,1)S(1)}, bf16[8,128,128]{2,1,0:T(8,128)(2,1)S(1)}, u32[]{:S(2)}, u32[]{:S(2)}) %collective-permute-start.3) | collective-permute-done | bytes 262176 | tf_op jit(solution)/shard_map/ppermute | solution.py:473
  58.6 0.0 copy-done.2
  58.6 0.0 copy-done.4
  58.6 0.0 copy-done.5
  58.6 1.1 shard_map.103
  59.6 0.0 collective-permute-done.4.lowest
  59.7 0.0 all-to-all-done.1.got
  59.7 4.4 %shard_map.104 = bf16[8,2,4,16,128]{4,3,2,1,0:T(8,128)(2,1)} custom-call(s32[9]{0:T(128)S(1)} %get-tuple-element.23.scal, bf16[8,2,4,16,128]{4,3,2,1,0:T(8,128)(2,1)S(1)} %all-to-all-done.1.got, f32[9,128,128]{2,1,0:T(8,128)S(1)} %get-tuple-element.26.scale_t, bf16[128,128]{1,0:T(8,128)(2,1)S(1)} %collective-permute-done.4.lowest, ...), custom_call_target="tpu_custom_call" | custom-call | tf_op jit(solution)/shard_map/pallas_call | solution.py:366
  64.1 0.0 copy-start.1
  64.1 6.3 %all-to-all-start.2 = ((bf16[8,2,4,16,128]{4,3,2,1,0:T(8,128)(2,1)}), bf16[8,2,4,16,128]{4,3,2,1,0:T(8,128)(2,1)S(1)}, u32[]{:S(2)}, u32[]{:S(2)}) async-start(bf16[8,2,4,16,128]{4,3,2,1,0:T(8,128)(2,1)} %shard_map.104), calls=%async_computation.2 | async-start | bytes 524288 | tf_op jit(solution)/shard_map/all_to_all | solution.py:457
  70.5 0.0 copy-done.1
  70.5 0.6 shard_map.105.tabs
  71.0 4.6 %all-to-all-done.2.got = bf16[8,2,4,16,128]{4,3,2,1,0:T(8,128)(2,1)S(1)} async-done(((bf16[8,2,4,16,128]{4,3,2,1,0:T(8,128)(2,1)}), bf16[8,2,4,16,128]{4,3,2,1,0:T(8,128)(2,1)S(1)}, u32[]{:S(2)}, u32[]{:S(2)}) %all-to-all-start.2) | async-done | bytes 262176 | tf_op jit(solution)/shard_map/all_to_all | solution.py:457
  75.7 2.0 %shard_map.106 = (bf16[8,8,32,128]{3,2,1,0:T(8,128)(2,1)}, bf16[2,8,32,128]{3,2,1,0:T(8,128)(2,1)S(1)}, bf16[2,8,32,128]{3,2,1,0:T(8,128)(2,1)S(1)}) custom-call(s32[9]{0:T(128)S(1)} %get-tuple-element.23.scal, bf16[8,2,4,16,128]{4,3,2,1,0:T(8,128)(2,1)S(1)} %all-to-all-done.2.got, bf16[2,8,32,128]{3,2,1,0:T(8,128)(2,1)S(1)} %get-tuple-element.32.there, ...), custom_call_target="tpu_custom_call" | custom-call | tf_op jit(solution)/shard_map/pallas_call | solution.py:366
  77.7 5.4 %all-to-all-start.3 = ((bf16[8,8,32,128]{3,2,1,0:T(8,128)(2,1)}), bf16[8,8,32,128]{3,2,1,0:T(8,128)(2,1)S(1)}, u32[]{:S(2)}, u32[]{:S(2)}) async-start(bf16[8,8,32,128]{3,2,1,0:T(8,128)(2,1)} %get-tuple-element.34), calls=%async_computation.3 | async-start | bytes 1048576 | tf_op jit(solution)/shard_map/all_to_all | solution.py:457
  83.2 1.9 %collective-permute-start.5 = (bf16[2,8,32,128]{3,2,1,0:T(8,128)(2,1)S(1)}, bf16[2,8,32,128]{3,2,1,0:T(8,128)(2,1)S(1)}, u32[]{:S(2)}, u32[]{:S(2)}) collective-permute-start(bf16[2,8,32,128]{3,2,1,0:T(8,128)(2,1)S(1)} %get-tuple-element.35), channel_id=1, source_target_pairs={{8,0},{0,8},{24,16},{16,24},{40,32},{32,40},{56,48},{48,56},{72,64... | collective-permute-start | bytes 393224 | tf_op jit(solution)/shard_map/ppermute | solution.py:453
  85.1 1.3 %collective-permute-done.5.crossed = bf16[2,8,32,128]{3,2,1,0:T(8,128)(2,1)S(1)} collective-permute-done((bf16[2,8,32,128]{3,2,1,0:T(8,128)(2,1)S(1)}, bf16[2,8,32,128]{3,2,1,0:T(8,128)(2,1)S(1)}, u32[]{:S(2)}, u32[]{:S(2)}) %collective-permute-start.5) | collective-permute-done | bytes 131104 | tf_op jit(solution)/shard_map/ppermute | solution.py:453
  86.4 1.9 %collective-permute-start.6 = (bf16[8,32,128]{2,1,0:T(8,128)(2,1)S(1)}, bf16[8,32,128]{2,1,0:T(8,128)(2,1)S(1)}, u32[]{:S(2)}, u32[]{:S(2)}) collective-permute-start(bf16[8,32,128]{2,1,0:T(8,128)(2,1)S(1)} %fusion.1), channel_id=1, source_target_pairs={{496,0},{504,8},{0,16},{8,24},{16,32},{24,40},{32,48},{40,56},{48,... | collective-permute-start | bytes 196616 | tf_op jit(solution)/shard_map/ppermute | solution.py:448
  88.3 9.7 %collective-permute-done.6 = bf16[8,32,128]{2,1,0:T(8,128)(2,1)S(1)} collective-permute-done((bf16[8,32,128]{2,1,0:T(8,128)(2,1)S(1)}, bf16[8,32,128]{2,1,0:T(8,128)(2,1)S(1)}, u32[]{:S(2)}, u32[]{:S(2)}) %collective-permute-start.6) | collective-permute-done | bytes 65568 | tf_op jit(solution)/shard_map/ppermute | solution.py:448
  98.1 1.9 %collective-permute-start.7 = (bf16[8,32,128]{2,1,0:T(8,128)(2,1)S(1)}, bf16[8,32,128]{2,1,0:T(8,128)(2,1)S(1)}, u32[]{:S(2)}, u32[]{:S(2)}) collective-permute-start(bf16[8,32,128]{2,1,0:T(8,128)(2,1)S(1)} %fusion), channel_id=1, source_target_pairs={{496,0},{504,8},{0,16},{8,24},{16,32},{24,40},{32,48},{40,56},{48,... | collective-permute-start | bytes 196616 | tf_op jit(solution)/shard_map/ppermute | solution.py:448
  100.0 8.6 %collective-permute-done.7.back = bf16[8,32,128]{2,1,0:T(8,128)(2,1)S(1)} collective-permute-done((bf16[8,32,128]{2,1,0:T(8,128)(2,1)S(1)}, bf16[8,32,128]{2,1,0:T(8,128)(2,1)S(1)}, u32[]{:S(2)}, u32[]{:S(2)}) %collective-permute-start.7) | collective-permute-done | bytes 65568 | tf_op jit(solution)/shard_map/ppermute | solution.py:448
  108.6 0.0 all-to-all-done.3.moved
  108.6 0.8 shard_map.107
  (4 shorter events, 0.1 us)
Async XLA Ops:
  2.2 15.7 %collective-permute-start = (bf16[8,4224]{1,0:T(8,128)(2,1)S(1)}, bf16[8,4224]{1,0:T(8,128)(2,1)S(1)}, u32[]{:S(2)}, u32[]{:S(2)}) collective-permute-start(bf16[8,4224]{1,0:T(8,128)(2,1)S(1)} %get-tuple-element.21), channel_id=1, source_target_pairs={{16,0},{24,8},{32,16},{40,24},{48,32},{56,40},{64,48},{72,56},{80,... | collective-permute-start | bytes 202760 | tf_op jit(solution)/shard_map/ppermute | solution.py:448
  17.9 15.3 %collective-permute-start.1 = (bf16[8,4224]{1,0:T(8,128)(2,1)S(1)}, bf16[8,4224]{1,0:T(8,128)(2,1)S(1)}, u32[]{:S(2)}, u32[]{:S(2)}) collective-permute-start(bf16[8,4224]{1,0:T(8,128)(2,1)S(1)} %collective-permute-done.two), channel_id=1, source_target_pairs={{16,0},{24,8},{32,16},{40,24},{48,32},{56,40},{64,48},{72,56},{80,... | collective-permute-start | bytes 202760 | tf_op jit(solution)/shard_map/ppermute | solution.py:448
  26.3 14.4 %copy-start.3 = (f32[128,128]{1,0:T(8,128)S(1)}, f32[128,128]{1,0:T(8,128)}, u32[]{:S(2)}) copy-start(f32[128,128]{1,0:T(8,128)} %constant.38.clone.first_t) | copy-start | bytes 196612
  26.4 14.4 %copy-start.6 = (s32[1,3]{1,0:T(1,128)S(1)}, s32[1,3]{1,0:T(1,128)}, u32[]{:S(2)}) copy-start(s32[1,3]{1,0:T(1,128)} %corner.1) | copy-start | bytes 40
  26.4 14.4 %copy-start.7 = (s32[1,2]{1,0:T(1,128)S(1)}, s32[1,2]{1,0:T(1,128)}, u32[]{:S(2)}) copy-start(s32[1,2]{1,0:T(1,128)} %partners.1) | copy-start | bytes 28
  26.4 14.4 %all-to-all-start = ((bf16[8,8,4096]{2,1,0:T(8,128)(2,1)}), bf16[8,8,4096]{2,1,0:T(8,128)(2,1)S(1)}, u32[]{:S(2)}, u32[]{:S(2)}) async-start(bf16[8,8,4096]{2,1,0:T(8,128)(2,1)} %get-tuple-element.22), calls=%async_computation | async-start | bytes 1048576 | tf_op jit(solution)/shard_map/all_to_all | solution.py:457
  33.2 14.8 %copy-start = (f32[128,16,128]{2,1,0:T(8,128)S(1)}, f32[128,16,128]{2,1,0:T(8,128)}, u32[]{:S(2)}) copy-start(f32[128,16,128]{2,1,0:T(8,128)} %kern.3) | copy-start | bytes 3145732
  33.2 3.4 %collective-permute-start.2 = (bf16[2,8,4224]{2,1,0:T(8,128)(2,1)S(1)}, bf16[2,8,4224]{2,1,0:T(8,128)(2,1)S(1)}, u32[]{:S(2)}, u32[]{:S(2)}) collective-permute-start(bf16[2,8,4224]{2,1,0:T(8,128)(2,1)S(1)} %pad_maximum_fusion), channel_id=1, source_target_pairs={{8,0},{0,8},{24,16},{16,24},{40,32},{32,40},{56,48},{48,56},{72,64... | collective-permute-start | bytes 405512 | tf_op jit(solution)/shard_map/ppermute | solution.py:453
  43.0 16.7 %all-to-all-start.1 = ((bf16[8,2,4,16,128]{4,3,2,1,0:T(8,128)(2,1)}), bf16[8,2,4,16,128]{4,3,2,1,0:T(8,128)(2,1)S(1)}, u32[]{:S(2)}, u32[]{:S(2)}) async-start(bf16[8,2,4,16,128]{4,3,2,1,0:T(8,128)(2,1)} %get-tuple-element.24), calls=%async_computation.1 | async-start | bytes 524288 | tf_op jit(solution)/shard_map/all_to_all | solution.py:457
  48.0 10.6 %copy-start.2 = (bf16[128,128]{1,0:T(8,128)(2,1)S(1)}, bf16[128,128]{1,0:T(8,128)(2,1)}, u32[]{:S(2)}) copy-start(bf16[128,128]{1,0:T(8,128)(2,1)} %constant.39.clone.flip_t) | copy-start | bytes 98308
  48.0 10.6 %copy-start.4 = (f32[128,128]{1,0:T(8,128)S(1)}, f32[128,128]{1,0:T(8,128)}, u32[]{:S(2)}) copy-start(f32[128,128]{1,0:T(8,128)} %constant.40.clone.cos_f) | copy-start | bytes 196612
  48.0 10.6 %copy-start.5 = (f32[128,128]{1,0:T(8,128)S(1)}, f32[128,128]{1,0:T(8,128)}, u32[]{:S(2)}) copy-start(f32[128,128]{1,0:T(8,128)} %constant.41.clone.sin_f) | copy-start | bytes 196612
  48.2 10.3 %collective-permute-start.3 = (bf16[8,128,128]{2,1,0:T(8,128)(2,1)S(1)}, bf16[8,128,128]{2,1,0:T(8,128)(2,1)S(1)}, u32[]{:S(2)}, u32[]{:S(2)}) collective-permute-start(bf16[8,128,128]{2,1,0:T(8,128)(2,1)S(1)} %get-tuple-element.25), channel_id=1, source_target_pairs={{0,7},{1,6},{2,5},{3,4},{4,3},{5,2},{6,1},{7,0},{8,15},{9,14},{10,... | collective-permute-start | bytes 786440 | tf_op jit(solution)/shard_map/ppermute | solution.py:473
  51.6 8.1 %collective-permute-start.4 = (bf16[128,128]{1,0:T(8,128)(2,1)S(1)}, bf16[128,128]{1,0:T(8,128)(2,1)S(1)}, u32[]{:S(2)}, u32[]{:S(2)}) collective-permute-start(bf16[128,128]{1,0:T(8,128)(2,1)S(1)} %get-tuple-element.27), channel_id=1, source_target_pairs={{4,0},{7,1},{6,2},{5,3},{12,8},{15,9},{14,10},{13,11},{20,16},{23,... | collective-permute-start | bytes 98312 | tf_op jit(solution)/shard_map/ppermute | solution.py:476
  64.1 6.4 %copy-start.1 = (f32[512,128]{1,0:T(8,128)S(1)}, f32[512,128]{1,0:T(8,128)}, u32[]{:S(2)}) copy-start(f32[512,128]{1,0:T(8,128)} %constant.42.clone.last_t) | copy-start | bytes 786436
  64.1 11.6 %all-to-all-start.2 = ((bf16[8,2,4,16,128]{4,3,2,1,0:T(8,128)(2,1)}), bf16[8,2,4,16,128]{4,3,2,1,0:T(8,128)(2,1)S(1)}, u32[]{:S(2)}, u32[]{:S(2)}) async-start(bf16[8,2,4,16,128]{4,3,2,1,0:T(8,128)(2,1)} %shard_map.104), calls=%async_computation.2 | async-start | bytes 524288 | tf_op jit(solution)/shard_map/all_to_all | solution.py:457
  77.7 30.9 %all-to-all-start.3 = ((bf16[8,8,32,128]{3,2,1,0:T(8,128)(2,1)}), bf16[8,8,32,128]{3,2,1,0:T(8,128)(2,1)S(1)}, u32[]{:S(2)}, u32[]{:S(2)}) async-start(bf16[8,8,32,128]{3,2,1,0:T(8,128)(2,1)} %get-tuple-element.34), calls=%async_computation.3 | async-start | bytes 1048576 | tf_op jit(solution)/shard_map/all_to_all | solution.py:457
  83.2 3.2 %collective-permute-start.5 = (bf16[2,8,32,128]{3,2,1,0:T(8,128)(2,1)S(1)}, bf16[2,8,32,128]{3,2,1,0:T(8,128)(2,1)S(1)}, u32[]{:S(2)}, u32[]{:S(2)}) collective-permute-start(bf16[2,8,32,128]{3,2,1,0:T(8,128)(2,1)S(1)} %get-tuple-element.35), channel_id=1, source_target_pairs={{8,0},{0,8},{24,16},{16,24},{40,32},{32,40},{56,48},{48,56},{72,64... | collective-permute-start | bytes 393224 | tf_op jit(solution)/shard_map/ppermute | solution.py:453
  86.4 11.6 %collective-permute-start.6 = (bf16[8,32,128]{2,1,0:T(8,128)(2,1)S(1)}, bf16[8,32,128]{2,1,0:T(8,128)(2,1)S(1)}, u32[]{:S(2)}, u32[]{:S(2)}) collective-permute-start(bf16[8,32,128]{2,1,0:T(8,128)(2,1)S(1)} %fusion.1), channel_id=1, source_target_pairs={{496,0},{504,8},{0,16},{8,24},{16,32},{24,40},{32,48},{40,56},{48,... | collective-permute-start | bytes 196616 | tf_op jit(solution)/shard_map/ppermute | solution.py:448
  98.1 10.5 %collective-permute-start.7 = (bf16[8,32,128]{2,1,0:T(8,128)(2,1)S(1)}, bf16[8,32,128]{2,1,0:T(8,128)(2,1)S(1)}, u32[]{:S(2)}, u32[]{:S(2)}) collective-permute-start(bf16[8,32,128]{2,1,0:T(8,128)(2,1)S(1)} %fusion), channel_id=1, source_target_pairs={{496,0},{504,8},{0,16},{8,24},{16,32},{24,40},{32,48},{40,56},{48,... | collective-permute-start | bytes 196616 | tf_op jit(solution)/shard_map/ppermute | solution.py:448

commit v7 on v6

--- a/solution.py
+++ b/solution.py
@@ -103,20 +103,25 @@
         ref[c * SPAN + PAD + FLAT : (c + 1) * SPAN, :] = zeros
 
 
-def load_kernel(corner_h, own, loaded, copies, corner, sems):
-    mark_load = pltpu.make_async_copy(corner_h, corner, sems.at[SLABS + 1])
+def load_kernel(corner_h, own, loaded, corner, sems):
+    mark_load = pltpu.make_async_copy(corner_h, corner, sems.at[0])
+    own_load = pltpu.make_async_copy(own, loaded.at[:, pl.ds(0, CELLS)], sems.at[1])
     mark_load.start()
-    loads = [pltpu.make_async_copy(own, copies.at[t], sems.at[t]) for t in range(SLABS)]
-    loads.append(pltpu.make_async_copy(own, loaded.at[:, pl.ds(0, CELLS)], sems.at[SLABS]))
-    for one in loads:
-        one.start()
+    own_load.start()
     mark_load.wait()
     lane = lanes_of((ROWS, LANES))
     mark = jnp.zeros((ROWS, LANES), F32)
     for k in range(3):
         mark = jnp.where(lane == k, corner[0, k].astype(F32), mark)
     loaded[:, CELLS:] = mark.astype(BF16)
-    for one in loads:
+    own_load.wait()
+
+
+def spread_kernel(loaded, copies, sems):
+    sends = [pltpu.make_async_copy(loaded.at[:, pl.ds(0, CELLS)], copies.at[t], sems.at[t]) for t in range(SLABS)]
+    for one in sends:
+        one.start()
+    for one in sends:
         one.wait()
 
 
@@ -155,26 +160,26 @@
         scal[7 + n] = hop
         halves = [first_t[pl.ds(HALF + d1 + par, FLAT, stride=2), :] for par in range(2)]
         first = jnp.concatenate(halves, axis=0).T.astype(BF16)
-        sides = []
         window = slab + (d0 >> 3)
         for w in range(2):
             t = jnp.clip(window + w, 0, SLABS - 1)
             for k in range(FLAT):
                 piece = own_in[t, :, k * LANES : (k + 1) * LANES].astype(F32)
                 own_s[pl.ds(w * ROWS * SPAN + PAD + k, ROWS, stride=SPAN), :] = piece
-        for r in range(ROWS):
-            source = slab * ROWS + r + d0
-            inside = jnp.logical_and(source >= 0, source < EDGE)
-            base = (r + (d0 & (ROWS - 1))) * SPAN + PAD
-            there = jnp.where(inside, shifted(own_s, base, -d1, -d2), 0.0)
-            part = part_s[r * RSPAN : r * RSPAN + FLAT, :]
-            there_out[n, r] = there.astype(BF16)
-            with_out[n, r] = part.astype(BF16)
-            sides.append(there * part)
         for quad in range(ROWS // 4):
+            sides = []
+            for r in range(quad * 4, quad * 4 + 4):
+                source = slab * ROWS + r + d0
+                inside = jnp.logical_and(source >= 0, source < EDGE)
+                base = (r + (d0 & (ROWS - 1))) * SPAN + PAD
+                there = jnp.where(inside, shifted(own_s, base, -d1, -d2), 0.0)
+                part = part_s[r * RSPAN : r * RSPAN + FLAT, :]
+                there_out[n, r] = there.astype(BF16)
+                with_out[n, r] = part.astype(BF16)
+                sides.append(there * part)
             columns = []
             for half in range(2):
-                a, b = sides[quad * 4 + half * 2], sides[quad * 4 + half * 2 + 1]
+                a, b = sides[half * 2], sides[half * 2 + 1]
                 even = jnp.where(low_d, a, swapped(b)).astype(BF16)
                 odd_part = jnp.where(low_d, swapped(a), b).astype(BF16)
                 columns.append(jnp.concatenate([even, odd_part], axis=0))
@@ -243,18 +248,18 @@
         at_b = n * EDGE * BSPAN
         depth_m = depf_t[n]
         rows_m = rowf_t[n]
-        for t in range(SLABS):
-            block = jnp.concatenate([got[t, n, p] for p in range(ROWS // 2)], axis=0)
-            z = dot(block, depth_m)
-            for r in range(ROWS):
-                part = z[r * SLOTS : (r + 1) * SLOTS]
-                zr[pl.ds(at_z + t * ROWS + r, SLOTS, stride=ZSPAN), :] = part[:, :LANES]
-                zi[pl.ds(at_z + t * ROWS + r, SLOTS, stride=ZSPAN), :] = part[:, LANES:]
+        block = jnp.concatenate([got[t, n, p] for t in range(SLABS) for p in range(ROWS // 2)], axis=0)
+        z = dot(block, depth_m)
+        for c in range(EDGE):
+            part = z[c * SLOTS : (c + 1) * SLOTS]
+            zr[pl.ds(at_z + c, SLOTS, stride=ZSPAN), :] = part[:, :LANES]
+            zi[pl.ds(at_z + c, SLOTS, stride=ZSPAN), :] = part[:, LANES:]
 
         def plane(w):
             at = slice(at_z + w * ZSPAN, at_z + w * ZSPAN + EDGE)
             return jnp.concatenate([zr[at, :], zi[at, :]], axis=0).astype(BF16)
 
+        lefts = []
         for w0 in range(0, SLOTS, 2):
             x = dot(rows_m, jnp.concatenate([plane(w0), plane(w0 + 1)], axis=1))
             weight = jnp.concatenate([scale_t[w0] if w0 else main, scale_t[w0 + 1]], axis=1)
@@ -267,16 +272,11 @@
                 im = jnp.concatenate([im[:, :LANES] - extra * back_im, im[:, LANES:]], axis=1)
             v = dot(rowb_t[n], jnp.concatenate([re, im], axis=0).astype(BF16)).astype(BF16)
             re, im = v[:EDGE], v[EDGE:]
-            left = jnp.concatenate(
-                [
-                    jnp.concatenate([re[:, :LANES], im[:, :LANES]], axis=1),
-                    jnp.concatenate([re[:, LANES:], im[:, LANES:]], axis=1),
-                ],
-                axis=0,
-            )
-            r = dot(left, depb_t[n])
-            for h in range(2):
-                back_s[pl.ds(at_b + w0 + h, EDGE, stride=BSPAN), :] = r[h * EDGE : (h + 1) * EDGE]
+            lefts.append(jnp.concatenate([re[:, :LANES], im[:, :LANES]], axis=1))
+            lefts.append(jnp.concatenate([re[:, LANES:], im[:, LANES:]], axis=1))
+        r = dot(jnp.concatenate(lefts, axis=0), depb_t[n])
+        for w in range(SLOTS):
+            back_s[pl.ds(at_b + w, EDGE, stride=BSPAN), :] = r[w * EDGE : (w + 1) * EDGE]
         for t in range(SLABS):
             for p in range(ROWS // 2):
                 at = at_b + (t * ROWS + 2 * p) * BSPAN
@@ -307,25 +307,21 @@
     for n in range(PAIRS):
         d0, d1, d2 = scal[1 + 3 * n], scal[2 + 3 * n], scal[3 + 3 * n]
         tab = tabs[n]
-        for quad in range(ROWS // 4):
-            data = [jnp.concatenate([got[t, n, quad * 2 + h] for t in range(SLABS)], axis=0) for h in range(2)]
-            g = dot(tab, jnp.concatenate(data, axis=1))
-            for h in range(2):
-                for par in range(2):
-                    r = quad * 4 + h * 2 + par
-                    part = g[par * GRID : (par + 1) * GRID, h * LANES : (h + 1) * LANES]
-                    c0, c1, s0, s1 = (part[f * FLAT : (f + 1) * FLAT] for f in range(4))
-                    pot = jnp.where(low, c0 - swapped(s0), swapped(c1) - s1) * scale
-                    far_s[n, r] = pot * there[n, r].astype(F32)
-                    base = (n * ROWS + r) * SPAN + PAD
-                    own_s[base : base + FLAT, :] = pot * withs[n, r].astype(F32)
+        for p in range(ROWS // 2):
+            g = dot(tab, jnp.concatenate([got[t, n, p] for t in range(SLABS)], axis=0))
+            for par in range(2):
+                r = p * 2 + par
+                c0, c1, s0, s1 = (g[par * GRID + f * FLAT : par * GRID + (f + 1) * FLAT] for f in range(4))
+                pot = jnp.where(low, c0 - swapped(s0), swapped(c1) - s1) * scale
+                far_s[n, r] = pot * there[n, r].astype(F32)
+                base = (n * ROWS + r) * SPAN + PAD
+                own_s[base : base + FLAT, :] = pot * withs[n, r].astype(F32)
         for r in range(ROWS):
             base = (n * ROWS + r) * SPAN + PAD
             at = HALF + slab * ROWS + r + d0
             sum_s[at] = sum_s[at] + shifted(own_s, base, d1, d2)
-    for t in range(SLABS):
-        for r in range(ROWS):
-            move_out[t, r] = sum_s[HALF + t * ROWS + r].astype(BF16)
+    for c in range(EDGE):
+        move_out[c] = sum_s[HALF + c].astype(BF16)
     hops = [scal[7 + n] for n in range(PAIRS)]
     for e in range(1, 5):
         target = odd_out if e % 2 else even_out
@@ -334,10 +330,10 @@
             target[(e - 1) // 2, row] = value.astype(BF16)
 
 
-def final_kernel(odd_core, moved, crossed, back, out, total_s):
+def final_kernel(odd_core, moved, crossed, two, four, out, total_s):
     keep = odd_core[0] == 1
     for r in range(ROWS):
-        total = back[r].astype(F32) + jnp.where(keep, crossed[0, r].astype(F32), 0.0)
+        total = two[r].astype(F32) + four[r].astype(F32) + jnp.where(keep, crossed[0, r].astype(F32), 0.0)
         for t in range(SLABS):
             total = total + moved[t, r].astype(F32)
         total_s[r * RSPAN : r * RSPAN + FLAT, :] = total
@@ -352,6 +348,10 @@
 
 def kept(shape, dtype):
     return pltpu.VMEM(shape, dtype)
+
+
+def far(shape, dtype):
+    return pltpu.HBM(shape, dtype)
 
 
 def away(x):
@@ -380,9 +380,15 @@
 
 
 def load_call(offsets, own):
-    shapes = (kept((ROWS, CELLS + LANES), BF16), kept((SLABS, ROWS, CELLS), BF16))
-    scratch = (pltpu.SMEM((1, 3), jnp.int32), pltpu.SemaphoreType.DMA((SLABS + 2,)))
-    return call(load_kernel, 8, [HBM, HBM], shapes, (VMEM,) * 2, scratch, (away(offsets), away(own)))
+    scratch = (pltpu.SMEM((1, 3), jnp.int32), pltpu.SemaphoreType.DMA((2,)))
+    shape = kept((ROWS, CELLS + LANES), BF16)
+    return call(load_kernel, 8, [HBM, HBM], shape, VMEM, scratch, (away(offsets), away(own)))
+
+
+def spread_call(loaded):
+    scratch = (pltpu.SemaphoreType.DMA((SLABS,)),)
+    shape = far((SLABS, ROWS, CELLS), BF16)
+    return call(spread_kernel, 8, [VMEM], shape, HBM, scratch, (near(loaded),))
 
 
 def mirror_call(kernel):
@@ -426,7 +432,7 @@
 
 def term_call(scal, got, there, withs, tabs):
     half = (2, ROWS, FLAT, LANES)
-    shapes = (kept((SLABS, ROWS, FLAT, LANES), BF16), kept(half, BF16), kept(half, BF16))
+    shapes = (kept((EDGE, FLAT, LANES), BF16), kept(half, BF16), kept(half, BF16))
     scratch = (
         pltpu.VMEM(ROWBOX, F32),
         pltpu.VMEM((PAIRS * ROWS * SPAN, LANES), F32),
@@ -436,11 +442,11 @@
     return call(term_kernel, 16, [SMEM] + [VMEM] * 4, shapes, (VMEM,) * 3, scratch, args)
 
 
-def final_call(odd_core, moved, crossed, back):
+def final_call(odd_core, moved, crossed, two, four):
     scratch = (pltpu.VMEM((ROWS * RSPAN, LANES), F32),)
     shape = jax.ShapeDtypeStruct((ROWS, CELLS), F32)
-    args = (odd_core, near(moved), near(crossed), near(back))
-    return call(final_kernel, 8, [SMEM] + [VMEM] * 3, shape, VMEM, scratch, args)
+    args = (odd_core, near(moved), near(crossed), near(two), near(four))
+    return call(final_kernel, 8, [SMEM] + [VMEM] * 4, shape, VMEM, scratch, args)
 
 
 def passed_along(block, distance):
@@ -463,10 +469,11 @@
     even_core = orbit % 2 == 0
     info = jnp.stack([slab, orbit])
     odd_core = (orbit % 2)[None]
-    loaded, copies = load_call(offsets, orbitals[0])
+    loaded = load_call(offsets, orbitals[0])
+    four = passed_along(loaded, -4)
     two = passed_along(loaded, -2)
+    copies = spread_call(loaded)
     own_box = shared(copies)
-    four = passed_along(two, -2)
     upper, lowest = mirror_call(kernel)
     given = jnp.stack([jnp.where(even_core, two, loaded), jnp.where(even_core, four, two)])
     odd = other_core(given)
@@ -480,12 +487,12 @@
     tabs = ready_call(scal)
     move, odd_out, even_out = term_call(scal, got, there, withs, tabs)
     crossed = other_core(odd_out)
-    move = shared(move)
+    move = shared(move.reshape(SLABS, ROWS, FLAT, LANES))
     by_two = even_out[0].astype(F32) + jnp.where(even_core, crossed[0], crossed[1]).astype(F32)
     by_four = even_out[1].astype(F32) + jnp.where(even_core, crossed[1], 0.0).astype(F32)
-    half_way = passed_along(by_four.astype(BF16), 2)
-    back = passed_along((by_two + half_way.astype(F32)).astype(BF16), 2)
-    return final_call(odd_core, move, crossed, back)[None]
+    four_back = passed_along(by_four.astype(BF16), 4)
+    two_back = passed_along(by_two.astype(BF16), 2)
+    return final_call(odd_core, move, crossed, two_back, four_back)[None]
 
 
 def solution(mesh):

time: 110 us -> 96.7 us (0.88)
  the two profiles are of different devices: /device:TPU:10 before, /device:TPU:8 now
where the time goes in v7:
time: 96.7 us; the launch traced here: 95.9 us
  starting transfers between devices  57.8 us (60%)
  waiting for transfers between devices  25.2 us (26%)
  Pallas kernels  12.5 us (13%)
    ppermute x4, starting transfers between devices, passed_along(): lax.ppermute(block, 'orb', [((i - distance) % count, i) for i in range(co...  25.4 us
    all_to_all x4, starting transfers between devices, shared(): lax.all_to_all(block, 'slab', split_axis=0, concat_axis=0, tiled=True)  20.5 us
    pallas_call x9, Pallas kernels, call(): pl.pallas_call(kernel, out_shape=out_shape, in_specs=in_specs, out_specs=...  12.5 us
    all_to_all x4, waiting for transfers between devices, shared(): lax.all_to_all(block, 'slab', split_axis=0, concat_axis=0, tiled=True)  9.87 us
    ppermute x4, waiting for transfers between devices, passed_along(): lax.ppermute(block, 'orb', [((i - distance) % count, i) for i in range(co...  9.52 us
    ppermute x1, starting transfers between devices, per_device(): lax.ppermute(upper, 'slab', [(s, SLABS - 1 - s) for s in range(SLABS)])  4.57 us
    ppermute x2, starting transfers between devices, other_core(): return lax.ppermute(block, 'orb', [(i ^ 1, i) for i in range(count)])  3.96 us
    ppermute x1, starting transfers between devices, per_device(): lowest = lax.ppermute(lowest, 'slab', [(4, 0), (7, 1), (6, 2), (5, 3)])  3.4 us
  transfers between devices with their start and end apart: 12, of which 7 were waited for; matrix products, arithmetic and copies ran while one was open for 0% of the time, Pallas kernels for 3%

profile of v7, /device:TPU:8, one launch (start us, length us, event | category | flops | bytes accessed | tf_op | source)
XLA Modules:
  0.0 95.9 jit_solution(2867767686876477370)
XLA Ops:
  0.0 0.9 shard_map.100.loaded
  0.9 13.7 %collective-permute-start = (bf16[8,4224]{1,0:T(8,128)(2,1)S(1)}, bf16[8,4224]{1,0:T(8,128)(2,1)S(1)}, u32[]{:S(2)}, u32[]{:S(2)}) collective-permute-start(bf16[8,4224]{1,0:T(8,128)(2,1)S(1)} %shard_map.100.loaded), channel_id=1, source_target_pairs={{16,0},{24,8},{32,16},{40,24},{48,32},{56,40},{64,48},{72,56},{80,... | collective-permute-start | bytes 202760 | tf_op jit(solution)/shard_map/ppermute | solution.py:454
  14.6 4.7 %collective-permute-start.1 = (bf16[8,4224]{1,0:T(8,128)(2,1)S(1)}, bf16[8,4224]{1,0:T(8,128)(2,1)S(1)}, u32[]{:S(2)}, u32[]{:S(2)}) collective-permute-start(bf16[8,4224]{1,0:T(8,128)(2,1)S(1)} %shard_map.100.loaded), channel_id=1, source_target_pairs={{32,0},{40,8},{48,16},{56,24},{64,32},{72,40},{80,48},{88,56},{96,... | collective-permute-start | bytes 202760 | tf_op jit(solution)/shard_map/ppermute | solution.py:454
  19.3 0.9 shard_map.101
  20.2 0.0 copy-start.3
  20.2 0.0 copy-start.6
  20.2 0.0 copy-start.7
  20.3 5.9 %all-to-all-start = ((bf16[8,8,4096]{2,1,0:T(8,128)(2,1)}), bf16[8,8,4096]{2,1,0:T(8,128)(2,1)S(1)}, u32[]{:S(2)}, u32[]{:S(2)}) async-start(bf16[8,8,4096]{2,1,0:T(8,128)(2,1)} %shard_map.101), calls=%async_computation | async-start | bytes 1048576 | tf_op jit(solution)/shard_map/all_to_all | solution.py:463
  26.2 0.0 copy-start
  26.2 0.0 collective-permute-done.two
  26.2 0.0 collective-permute-done.1.four
  26.2 2.1 %collective-permute-start.2 = (bf16[2,8,4224]{2,1,0:T(8,128)(2,1)S(1)}, bf16[2,8,4224]{2,1,0:T(8,128)(2,1)S(1)}, u32[]{:S(2)}, u32[]{:S(2)}) collective-permute-start(bf16[2,8,4224]{2,1,0:T(8,128)(2,1)S(1)} %pad_maximum_fusion), channel_id=1, source_target_pairs={{8,0},{0,8},{24,16},{16,24},{40,32},{32,40},{56,48},{48,56},{72,64... | collective-permute-start | bytes 405512 | tf_op jit(solution)/shard_map/ppermute | solution.py:459
  28.3 0.1 pad_add_fusion.info
  28.4 1.2 %collective-permute-done.2.odd = bf16[2,8,4224]{2,1,0:T(8,128)(2,1)S(1)} collective-permute-done((bf16[2,8,4224]{2,1,0:T(8,128)(2,1)S(1)}, bf16[2,8,4224]{2,1,0:T(8,128)(2,1)S(1)}, u32[]{:S(2)}, u32[]{:S(2)}) %collective-permute-start.2) | collective-permute-done | bytes 135200 | tf_op jit(solution)/shard_map/ppermute | solution.py:459
  29.6 4.6 %all-to-all-done.own_in = bf16[8,8,4096]{2,1,0:T(8,128)(2,1)S(1)} async-done(((bf16[8,8,4096]{2,1,0:T(8,128)(2,1)}), bf16[8,8,4096]{2,1,0:T(8,128)(2,1)S(1)}, u32[]{:S(2)}, u32[]{:S(2)}) %all-to-all-start) | async-done | bytes 524320 | tf_op jit(solution)/shard_map/all_to_all | solution.py:463
  34.2 0.0 copy-done.3
  34.2 0.0 copy-done.6
  34.2 0.0 copy-done.7
  34.2 2.0 %shard_map.102 = (bf16[8,2,4,16,128]{4,3,2,1,0:T(8,128)(2,1)}, bf16[2,8,32,128]{3,2,1,0:T(8,128)(2,1)S(1)}, bf16[2,8,32,128]{3,2,1,0:T(8,128)(2,1)S(1)}, s32[9]{0:T(128)S(1)}) custom-call(s32[2]{0:T(128)S(1)} %pad_add_fusion.info, s32[1,2]{1,0:T(1,128)S(1)} %copy-done.7, s32[1,3]{1,0:T(1,128)S(1)} %copy-done.6, ...), custom_call_target="tpu_custom_call" | custom-call | tf_op jit(solution)/shard_map/pallas_call | solution.py:366
  36.3 4.4 %all-to-all-start.1 = ((bf16[8,2,4,16,128]{4,3,2,1,0:T(8,128)(2,1)}), bf16[8,2,4,16,128]{4,3,2,1,0:T(8,128)(2,1)S(1)}, u32[]{:S(2)}, u32[]{:S(2)}) async-start(bf16[8,2,4,16,128]{4,3,2,1,0:T(8,128)(2,1)} %get-tuple-element.20), calls=%async_computation.1 | async-start | bytes 524288 | tf_op jit(solution)/shard_map/all_to_all | solution.py:463
  40.7 0.0 copy-done
  40.7 0.0 copy-start.2
  40.7 0.0 copy-start.4
  40.7 0.0 copy-start.5
  40.7 0.2 shard_map.103
  40.9 4.6 %collective-permute-start.3 = (bf16[8,128,128]{2,1,0:T(8,128)(2,1)S(1)}, bf16[8,128,128]{2,1,0:T(8,128)(2,1)S(1)}, u32[]{:S(2)}, u32[]{:S(2)}) collective-permute-start(bf16[8,128,128]{2,1,0:T(8,128)(2,1)S(1)} %get-tuple-element.21), channel_id=1, source_target_pairs={{0,7},{1,6},{2,5},{3,4},{4,3},{5,2},{6,1},{7,0},{8,15},{9,14},{10,... | collective-permute-start | bytes 786440 | tf_op jit(solution)/shard_map/ppermute | solution.py:480
  45.5 3.4 %collective-permute-start.4 = (bf16[128,128]{1,0:T(8,128)(2,1)S(1)}, bf16[128,128]{1,0:T(8,128)(2,1)S(1)}, u32[]{:S(2)}, u32[]{:S(2)}) collective-permute-start(bf16[128,128]{1,0:T(8,128)(2,1)S(1)} %get-tuple-element.23), channel_id=1, source_target_pairs={{4,0},{7,1},{6,2},{5,3},{12,8},{15,9},{14,10},{13,11},{20,16},{23,... | collective-permute-start | bytes 98312 | tf_op jit(solution)/shard_map/ppermute | solution.py:483
  48.9 3.2 %collective-permute-done.3.upper = bf16[8,128,128]{2,1,0:T(8,128)(2,1)S(1)} collective-permute-done((bf16[8,128,128]{2,1,0:T(8,128)(2,1)S(1)}, bf16[8,128,128]{2,1,0:T(8,128)(2,1)S(1)}, u32[]{:S(2)}, u32[]{:S(2)}) %collective-permute-start.3) | collective-permute-done | bytes 262176 | tf_op jit(solution)/shard_map/ppermute | solution.py:480
  52.1 0.0 copy-done.2
  52.1 0.0 copy-done.4
  52.1 0.0 copy-done.5
  52.1 1.1 %shard_map.104 = (f32[9,128,128]{2,1,0:T(8,128)S(1)}, bf16[2,256,128]{2,1,0:T(8,128)(2,1)S(1)}, bf16[2,128,256]{2,1,0:T(8,128)(2,1)S(1)}, bf16[2,128,256]{2,1,0:T(8,128)(2,1)S(1)}, bf16[2,256,128]{2,1,0:T(8,128)(2,1)S(1)}) custom-call(s32[9]{0:T(128)S(1)} %get-tuple-element.19.scal, f32[128,16,128]{2,1,0:T(8,128)S(1)} %copy-done, ...), custom_call_target="tpu_custom_call" | custom-call | tf_op jit(solution)/shard_map/pallas_call | solution.py:366
  53.2 0.0 collective-permute-done.4.lowest
  53.2 0.0 all-to-all-done.1.got
  53.2 4.2 %shard_map.105 = bf16[8,2,4,16,128]{4,3,2,1,0:T(8,128)(2,1)} custom-call(s32[9]{0:T(128)S(1)} %get-tuple-element.19.scal, bf16[8,2,4,16,128]{4,3,2,1,0:T(8,128)(2,1)S(1)} %all-to-all-done.1.got, f32[9,128,128]{2,1,0:T(8,128)S(1)} %get-tuple-element.22.scale_t, bf16[128,128]{1,0:T(8,128)(2,1)S(1)} %collective-permute-done.4.lowest, ...), custom_call_target="tpu_custom_call" | custom-call | tf_op jit(solution)/shard_map/pallas_call | solution.py:366
  57.4 0.0 copy-start.1
  57.4 5.3 %all-to-all-start.2 = ((bf16[8,2,4,16,128]{4,3,2,1,0:T(8,128)(2,1)}), bf16[8,2,4,16,128]{4,3,2,1,0:T(8,128)(2,1)S(1)}, u32[]{:S(2)}, u32[]{:S(2)}) async-start(bf16[8,2,4,16,128]{4,3,2,1,0:T(8,128)(2,1)} %shard_map.105), calls=%async_computation.2 | async-start | bytes 524288 | tf_op jit(solution)/shard_map/all_to_all | solution.py:463
  62.7 0.0 copy-done.1
  62.7 0.6 shard_map.106.tabs
  63.3 5.3 %all-to-all-done.2.got = bf16[8,2,4,16,128]{4,3,2,1,0:T(8,128)(2,1)S(1)} async-done(((bf16[8,2,4,16,128]{4,3,2,1,0:T(8,128)(2,1)}), bf16[8,2,4,16,128]{4,3,2,1,0:T(8,128)(2,1)S(1)}, u32[]{:S(2)}, u32[]{:S(2)}) %all-to-all-start.2) | async-done | bytes 262176 | tf_op jit(solution)/shard_map/all_to_all | solution.py:463
  68.5 2.0 %shard_map.107 = (bf16[64,32,128]{2,1,0:T(8,128)(2,1)}, bf16[2,8,32,128]{3,2,1,0:T(8,128)(2,1)S(1)}, bf16[2,8,32,128]{3,2,1,0:T(8,128)(2,1)S(1)}) custom-call(s32[9]{0:T(128)S(1)} %get-tuple-element.19.scal, bf16[8,2,4,16,128]{4,3,2,1,0:T(8,128)(2,1)S(1)} %all-to-all-done.2.got, bf16[2,8,32,128]{3,2,1,0:T(8,128)(2,1)S(1)} %get-tuple-element.28.there, ...), custom_call_target="tpu_custom_call" | custom-call | tf_op jit(solution)/shard_map/pallas_call | solution.py:366
  70.6 4.8 %all-to-all-start.3 = ((bf16[8,8,32,128]{3,2,1,0:T(8,128)(2,1)}), bf16[8,8,32,128]{3,2,1,0:T(8,128)(2,1)S(1)}, u32[]{:S(2)}, u32[]{:S(2)}) async-start(bf16[8,8,32,128]{3,2,1,0:T(8,128)(2,1)} %bitcast.6), calls=%async_computation.3 | async-start | bytes 1048576 | tf_op jit(solution)/shard_map/all_to_all | solution.py:463
  75.4 1.9 %collective-permute-start.5 = (bf16[2,8,32,128]{3,2,1,0:T(8,128)(2,1)S(1)}, bf16[2,8,32,128]{3,2,1,0:T(8,128)(2,1)S(1)}, u32[]{:S(2)}, u32[]{:S(2)}) collective-permute-start(bf16[2,8,32,128]{3,2,1,0:T(8,128)(2,1)S(1)} %get-tuple-element.31), channel_id=1, source_target_pairs={{8,0},{0,8},{24,16},{16,24},{40,32},{32,40},{56,48},{48,56},{72,64... | collective-permute-start | bytes 393224 | tf_op jit(solution)/shard_map/ppermute | solution.py:459
  77.3 1.3 %collective-permute-done.5.crossed = bf16[2,8,32,128]{3,2,1,0:T(8,128)(2,1)S(1)} collective-permute-done((bf16[2,8,32,128]{3,2,1,0:T(8,128)(2,1)S(1)}, bf16[2,8,32,128]{3,2,1,0:T(8,128)(2,1)S(1)}, u32[]{:S(2)}, u32[]{:S(2)}) %collective-permute-start.5) | collective-permute-done | bytes 131104 | tf_op jit(solution)/shard_map/ppermute | solution.py:459
  78.7 3.6 %collective-permute-start.6 = (bf16[8,32,128]{2,1,0:T(8,128)(2,1)S(1)}, bf16[8,32,128]{2,1,0:T(8,128)(2,1)S(1)}, u32[]{:S(2)}, u32[]{:S(2)}) collective-permute-start(bf16[8,32,128]{2,1,0:T(8,128)(2,1)S(1)} %get-tuple-element.34), channel_id=1, source_target_pairs={{496,0},{504,8},{0,16},{8,24},{16,32},{24,40},{32,48},{40,56},{48,... | collective-permute-start | bytes 196616 | tf_op jit(solution)/shard_map/ppermute | solution.py:454
  82.3 3.4 %collective-permute-start.7 = (bf16[8,32,128]{2,1,0:T(8,128)(2,1)S(1)}, bf16[8,32,128]{2,1,0:T(8,128)(2,1)S(1)}, u32[]{:S(2)}, u32[]{:S(2)}) collective-permute-start(bf16[8,32,128]{2,1,0:T(8,128)(2,1)S(1)} %get-tuple-element.33), channel_id=1, source_target_pairs={{480,0},{488,8},{496,16},{504,24},{0,32},{8,40},{16,48},{24,56},{3... | collective-permute-start | bytes 196616 | tf_op jit(solution)/shard_map/ppermute | solution.py:454
  85.6 4.2 %collective-permute-done.6.two = bf16[8,32,128]{2,1,0:T(8,128)(2,1)S(1)} collective-permute-done((bf16[8,32,128]{2,1,0:T(8,128)(2,1)S(1)}, bf16[8,32,128]{2,1,0:T(8,128)(2,1)S(1)}, u32[]{:S(2)}, u32[]{:S(2)}) %collective-permute-start.6) | collective-permute-done | bytes 65568 | tf_op jit(solution)/shard_map/ppermute | solution.py:454
  89.9 5.3 %collective-permute-done.7.four = bf16[8,32,128]{2,1,0:T(8,128)(2,1)S(1)} collective-permute-done((bf16[8,32,128]{2,1,0:T(8,128)(2,1)S(1)}, bf16[8,32,128]{2,1,0:T(8,128)(2,1)S(1)}, u32[]{:S(2)}, u32[]{:S(2)}) %collective-permute-start.7) | collective-permute-done | bytes 65568 | tf_op jit(solution)/shard_map/ppermute | solution.py:454
  95.1 0.0 all-to-all-done.3.moved
  95.1 0.8 shard_map.108
  (3 shorter events, 0.1 us)
Async XLA Ops:
  0.9 25.3 %collective-permute-start = (bf16[8,4224]{1,0:T(8,128)(2,1)S(1)}, bf16[8,4224]{1,0:T(8,128)(2,1)S(1)}, u32[]{:S(2)}, u32[]{:S(2)}) collective-permute-start(bf16[8,4224]{1,0:T(8,128)(2,1)S(1)} %shard_map.100.loaded), channel_id=1, source_target_pairs={{16,0},{24,8},{32,16},{40,24},{48,32},{56,40},{64,48},{72,56},{80,... | collective-permute-start | bytes 202760 | tf_op jit(solution)/shard_map/ppermute | solution.py:454
  14.6 11.6 %collective-permute-start.1 = (bf16[8,4224]{1,0:T(8,128)(2,1)S(1)}, bf16[8,4224]{1,0:T(8,128)(2,1)S(1)}, u32[]{:S(2)}, u32[]{:S(2)}) collective-permute-start(bf16[8,4224]{1,0:T(8,128)(2,1)S(1)} %shard_map.100.loaded), channel_id=1, source_target_pairs={{32,0},{40,8},{48,16},{56,24},{64,32},{72,40},{80,48},{88,56},{96,... | collective-permute-start | bytes 202760 | tf_op jit(solution)/shard_map/ppermute | solution.py:454
  20.2 14.0 %copy-start.3 = (f32[128,128]{1,0:T(8,128)S(1)}, f32[128,128]{1,0:T(8,128)}, u32[]{:S(2)}) copy-start(f32[128,128]{1,0:T(8,128)} %constant.38.clone.first_t) | copy-start | bytes 196612
  20.2 14.0 %copy-start.6 = (s32[1,3]{1,0:T(1,128)S(1)}, s32[1,3]{1,0:T(1,128)}, u32[]{:S(2)}) copy-start(s32[1,3]{1,0:T(1,128)} %corner.1) | copy-start | bytes 40
  20.2 14.0 %copy-start.7 = (s32[1,2]{1,0:T(1,128)S(1)}, s32[1,2]{1,0:T(1,128)}, u32[]{:S(2)}) copy-start(s32[1,2]{1,0:T(1,128)} %partners.1) | copy-start | bytes 28
  20.3 14.0 %all-to-all-start = ((bf16[8,8,4096]{2,1,0:T(8,128)(2,1)}), bf16[8,8,4096]{2,1,0:T(8,128)(2,1)S(1)}, u32[]{:S(2)}, u32[]{:S(2)}) async-start(bf16[8,8,4096]{2,1,0:T(8,128)(2,1)} %shard_map.101), calls=%async_computation | async-start | bytes 1048576 | tf_op jit(solution)/shard_map/all_to_all | solution.py:463
  26.2 14.5 %copy-start = (f32[128,16,128]{2,1,0:T(8,128)S(1)}, f32[128,16,128]{2,1,0:T(8,128)}, u32[]{:S(2)}) copy-start(f32[128,16,128]{2,1,0:T(8,128)} %kern.3) | copy-start | bytes 3145732
  26.2 3.4 %collective-permute-start.2 = (bf16[2,8,4224]{2,1,0:T(8,128)(2,1)S(1)}, bf16[2,8,4224]{2,1,0:T(8,128)(2,1)S(1)}, u32[]{:S(2)}, u32[]{:S(2)}) collective-permute-start(bf16[2,8,4224]{2,1,0:T(8,128)(2,1)S(1)} %pad_maximum_fusion), channel_id=1, source_target_pairs={{8,0},{0,8},{24,16},{16,24},{40,32},{32,40},{56,48},{48,56},{72,64... | collective-permute-start | bytes 405512 | tf_op jit(solution)/shard_map/ppermute | solution.py:459
  36.3 16.9 %all-to-all-start.1 = ((bf16[8,2,4,16,128]{4,3,2,1,0:T(8,128)(2,1)}), bf16[8,2,4,16,128]{4,3,2,1,0:T(8,128)(2,1)S(1)}, u32[]{:S(2)}, u32[]{:S(2)}) async-start(bf16[8,2,4,16,128]{4,3,2,1,0:T(8,128)(2,1)} %get-tuple-element.20), calls=%async_computation.1 | async-start | bytes 524288 | tf_op jit(solution)/shard_map/all_to_all | solution.py:463
  40.7 11.4 %copy-start.2 = (bf16[128,128]{1,0:T(8,128)(2,1)S(1)}, bf16[128,128]{1,0:T(8,128)(2,1)}, u32[]{:S(2)}) copy-start(bf16[128,128]{1,0:T(8,128)(2,1)} %constant.39.clone.flip_t) | copy-start | bytes 98308
  40.7 11.4 %copy-start.4 = (f32[128,128]{1,0:T(8,128)S(1)}, f32[128,128]{1,0:T(8,128)}, u32[]{:S(2)}) copy-start(f32[128,128]{1,0:T(8,128)} %constant.40.clone.cos_f) | copy-start | bytes 196612
  40.7 11.4 %copy-start.5 = (f32[128,128]{1,0:T(8,128)S(1)}, f32[128,128]{1,0:T(8,128)}, u32[]{:S(2)}) copy-start(f32[128,128]{1,0:T(8,128)} %constant.41.clone.sin_f) | copy-start | bytes 196612
  40.9 11.2 %collective-permute-start.3 = (bf16[8,128,128]{2,1,0:T(8,128)(2,1)S(1)}, bf16[8,128,128]{2,1,0:T(8,128)(2,1)S(1)}, u32[]{:S(2)}, u32[]{:S(2)}) collective-permute-start(bf16[8,128,128]{2,1,0:T(8,128)(2,1)S(1)} %get-tuple-element.21), channel_id=1, source_target_pairs={{0,7},{1,6},{2,5},{3,4},{4,3},{5,2},{6,1},{7,0},{8,15},{9,14},{10,... | collective-permute-start | bytes 786440 | tf_op jit(solution)/shard_map/ppermute | solution.py:480
  45.5 7.7 %collective-permute-start.4 = (bf16[128,128]{1,0:T(8,128)(2,1)S(1)}, bf16[128,128]{1,0:T(8,128)(2,1)S(1)}, u32[]{:S(2)}, u32[]{:S(2)}) collective-permute-start(bf16[128,128]{1,0:T(8,128)(2,1)S(1)} %get-tuple-element.23), channel_id=1, source_target_pairs={{4,0},{7,1},{6,2},{5,3},{12,8},{15,9},{14,10},{13,11},{20,16},{23,... | collective-permute-start | bytes 98312 | tf_op jit(solution)/shard_map/ppermute | solution.py:483
  57.4 5.3 %copy-start.1 = (f32[512,128]{1,0:T(8,128)S(1)}, f32[512,128]{1,0:T(8,128)}, u32[]{:S(2)}) copy-start(f32[512,128]{1,0:T(8,128)} %constant.42.clone.last_t) | copy-start | bytes 786436
  57.4 11.2 %all-to-all-start.2 = ((bf16[8,2,4,16,128]{4,3,2,1,0:T(8,128)(2,1)}), bf16[8,2,4,16,128]{4,3,2,1,0:T(8,128)(2,1)S(1)}, u32[]{:S(2)}, u32[]{:S(2)}) async-start(bf16[8,2,4,16,128]{4,3,2,1,0:T(8,128)(2,1)} %shard_map.105), calls=%async_computation.2 | async-start | bytes 524288 | tf_op jit(solution)/shard_map/all_to_all | solution.py:463
  70.6 24.6 %all-to-all-start.3 = ((bf16[8,8,32,128]{3,2,1,0:T(8,128)(2,1)}), bf16[8,8,32,128]{3,2,1,0:T(8,128)(2,1)S(1)}, u32[]{:S(2)}, u32[]{:S(2)}) async-start(bf16[8,8,32,128]{3,2,1,0:T(8,128)(2,1)} %bitcast.6), calls=%async_computation.3 | async-start | bytes 1048576 | tf_op jit(solution)/shard_map/all_to_all | solution.py:463
  75.4 3.2 %collective-permute-start.5 = (bf16[2,8,32,128]{3,2,1,0:T(8,128)(2,1)S(1)}, bf16[2,8,32,128]{3,2,1,0:T(8,128)(2,1)S(1)}, u32[]{:S(2)}, u32[]{:S(2)}) collective-permute-start(bf16[2,8,32,128]{3,2,1,0:T(8,128)(2,1)S(1)} %get-tuple-element.31), channel_id=1, source_target_pairs={{8,0},{0,8},{24,16},{16,24},{40,32},{32,40},{56,48},{48,56},{72,64... | collective-permute-start | bytes 393224 | tf_op jit(solution)/shard_map/ppermute | solution.py:459
  78.7 11.2 %collective-permute-start.6 = (bf16[8,32,128]{2,1,0:T(8,128)(2,1)S(1)}, bf16[8,32,128]{2,1,0:T(8,128)(2,1)S(1)}, u32[]{:S(2)}, u32[]{:S(2)}) collective-permute-start(bf16[8,32,128]{2,1,0:T(8,128)(2,1)S(1)} %get-tuple-element.34), channel_id=1, source_target_pairs={{496,0},{504,8},{0,16},{8,24},{16,32},{24,40},{32,48},{40,56},{48,... | collective-permute-start | bytes 196616 | tf_op jit(solution)/shard_map/ppermute | solution.py:454
  82.3 12.9 %collective-permute-start.7 = (bf16[8,32,128]{2,1,0:T(8,128)(2,1)S(1)}, bf16[8,32,128]{2,1,0:T(8,128)(2,1)S(1)}, u32[]{:S(2)}, u32[]{:S(2)}) collective-permute-start(bf16[8,32,128]{2,1,0:T(8,128)(2,1)S(1)} %get-tuple-element.33), channel_id=1, source_target_pairs={{480,0},{488,8},{496,16},{504,24},{0,32},{8,40},{16,48},{24,56},{3... | collective-permute-start | bytes 196616 | tf_op jit(solution)/shard_map/ppermute | solution.py:454

commit v8 on v7

--- a/solution.py
+++ b/solution.py
@@ -266,8 +266,9 @@
             re, im = x[:GRID] * weight, x[GRID:] * weight
             if w0 == 0:
                 edge = x[:, :LANES].astype(BF16)
-                back_re = dot(dot(flip, edge[:GRID]).astype(BF16), flip)
-                back_im = dot(dot(flip, edge[GRID:]).astype(BF16), flip)
+                turned = dot(flip, jnp.concatenate([edge[:GRID], edge[GRID:]], axis=1)).astype(BF16)
+                turned = dot(jnp.concatenate([turned[:, :LANES], turned[:, LANES:]], axis=0), flip)
+                back_re, back_im = turned[:GRID], turned[GRID:]
                 re = jnp.concatenate([re[:, :LANES] + extra * back_re, re[:, LANES:]], axis=1)
                 im = jnp.concatenate([im[:, :LANES] - extra * back_im, im[:, LANES:]], axis=1)
             v = dot(rowb_t[n], jnp.concatenate([re, im], axis=0).astype(BF16)).astype(BF16)

time: 96.7 us -> 96.6 us (level)
  no operation moved by 1% of the time
where the time goes in v8:
time: 96.6 us; the launch traced here: 95.8 us
  starting transfers between devices  57.8 us (60%)
  waiting for transfers between devices  25.2 us (26%)
  Pallas kernels  12.4 us (13%)
    ppermute x4, starting transfers between devices, passed_along(): lax.ppermute(block, 'orb', [((i - distance) % count, i) for i in range(co...  25.4 us
    all_to_all x4, starting transfers between devices, shared(): lax.all_to_all(block, 'slab', split_axis=0, concat_axis=0, tiled=True)  20.4 us
    pallas_call x9, Pallas kernels, call(): pl.pallas_call(kernel, out_shape=out_shape, in_specs=in_specs, out_specs=...  12.4 us
    all_to_all x4, waiting for transfers between devices, shared(): lax.all_to_all(block, 'slab', split_axis=0, concat_axis=0, tiled=True)  9.87 us
    ppermute x4, waiting for transfers between devices, passed_along(): lax.ppermute(block, 'orb', [((i - distance) % count, i) for i in range(co...  9.52 us
    ppermute x1, starting transfers between devices, per_device(): lax.ppermute(upper, 'slab', [(s, SLABS - 1 - s) for s in range(SLABS)])  4.57 us
    ppermute x2, starting transfers between devices, other_core(): return lax.ppermute(block, 'orb', [(i ^ 1, i) for i in range(count)])  3.96 us
    ppermute x1, starting transfers between devices, per_device(): lowest = lax.ppermute(lowest, 'slab', [(4, 0), (7, 1), (6, 2), (5, 3)])  3.4 us
  transfers between devices with their start and end apart: 12, of which 7 were waited for; matrix products, arithmetic and copies ran while one was open for 0% of the time, Pallas kernels for 3%

profile of v8, /device:TPU:8, one launch (start us, length us, event | category | flops | bytes accessed | tf_op | source)
XLA Modules:
  0.0 95.8 jit_solution(10883963901285238693)
XLA Ops:
  0.0 0.9 shard_map.100.loaded
  0.9 13.7 %collective-permute-start = (bf16[8,4224]{1,0:T(8,128)(2,1)S(1)}, bf16[8,4224]{1,0:T(8,128)(2,1)S(1)}, u32[]{:S(2)}, u32[]{:S(2)}) collective-permute-start(bf16[8,4224]{1,0:T(8,128)(2,1)S(1)} %shard_map.100.loaded), channel_id=1, source_target_pairs={{16,0},{24,8},{32,16},{40,24},{48,32},{56,40},{64,48},{72,56},{80,... | collective-permute-start | bytes 202760 | tf_op jit(solution)/shard_map/ppermute | solution.py:455
  14.6 4.7 %collective-permute-start.1 = (bf16[8,4224]{1,0:T(8,128)(2,1)S(1)}, bf16[8,4224]{1,0:T(8,128)(2,1)S(1)}, u32[]{:S(2)}, u32[]{:S(2)}) collective-permute-start(bf16[8,4224]{1,0:T(8,128)(2,1)S(1)} %shard_map.100.loaded), channel_id=1, source_target_pairs={{32,0},{40,8},{48,16},{56,24},{64,32},{72,40},{80,48},{88,56},{96,... | collective-permute-start | bytes 202760 | tf_op jit(solution)/shard_map/ppermute | solution.py:455
  19.3 0.9 shard_map.101
  20.2 0.0 copy-start.3
  20.2 0.0 copy-start.6
  20.2 0.0 copy-start.7
  20.3 5.9 %all-to-all-start = ((bf16[8,8,4096]{2,1,0:T(8,128)(2,1)}), bf16[8,8,4096]{2,1,0:T(8,128)(2,1)S(1)}, u32[]{:S(2)}, u32[]{:S(2)}) async-start(bf16[8,8,4096]{2,1,0:T(8,128)(2,1)} %shard_map.101), calls=%async_computation | async-start | bytes 1048576 | tf_op jit(solution)/shard_map/all_to_all | solution.py:464
  26.2 0.0 copy-start
  26.2 0.0 collective-permute-done.two
  26.2 0.0 collective-permute-done.1.four
  26.2 2.1 %collective-permute-start.2 = (bf16[2,8,4224]{2,1,0:T(8,128)(2,1)S(1)}, bf16[2,8,4224]{2,1,0:T(8,128)(2,1)S(1)}, u32[]{:S(2)}, u32[]{:S(2)}) collective-permute-start(bf16[2,8,4224]{2,1,0:T(8,128)(2,1)S(1)} %pad_maximum_fusion), channel_id=1, source_target_pairs={{8,0},{0,8},{24,16},{16,24},{40,32},{32,40},{56,48},{48,56},{72,64... | collective-permute-start | bytes 405512 | tf_op jit(solution)/shard_map/ppermute | solution.py:460
  28.3 0.1 pad_add_fusion.info
  28.4 1.2 %collective-permute-done.2.odd = bf16[2,8,4224]{2,1,0:T(8,128)(2,1)S(1)} collective-permute-done((bf16[2,8,4224]{2,1,0:T(8,128)(2,1)S(1)}, bf16[2,8,4224]{2,1,0:T(8,128)(2,1)S(1)}, u32[]{:S(2)}, u32[]{:S(2)}) %collective-permute-start.2) | collective-permute-done | bytes 135200 | tf_op jit(solution)/shard_map/ppermute | solution.py:460
  29.6 4.6 %all-to-all-done.own_in = bf16[8,8,4096]{2,1,0:T(8,128)(2,1)S(1)} async-done(((bf16[8,8,4096]{2,1,0:T(8,128)(2,1)}), bf16[8,8,4096]{2,1,0:T(8,128)(2,1)S(1)}, u32[]{:S(2)}, u32[]{:S(2)}) %all-to-all-start) | async-done | bytes 524320 | tf_op jit(solution)/shard_map/all_to_all | solution.py:464
  34.2 0.0 copy-done.3
  34.2 0.0 copy-done.6
  34.2 0.0 copy-done.7
  34.2 2.0 %shard_map.102 = (bf16[8,2,4,16,128]{4,3,2,1,0:T(8,128)(2,1)}, bf16[2,8,32,128]{3,2,1,0:T(8,128)(2,1)S(1)}, bf16[2,8,32,128]{3,2,1,0:T(8,128)(2,1)S(1)}, s32[9]{0:T(128)S(1)}) custom-call(s32[2]{0:T(128)S(1)} %pad_add_fusion.info, s32[1,2]{1,0:T(1,128)S(1)} %copy-done.7, s32[1,3]{1,0:T(1,128)S(1)} %copy-done.6, ...), custom_call_target="tpu_custom_call" | custom-call | tf_op jit(solution)/shard_map/pallas_call | solution.py:367
  36.3 4.4 %all-to-all-start.1 = ((bf16[8,2,4,16,128]{4,3,2,1,0:T(8,128)(2,1)}), bf16[8,2,4,16,128]{4,3,2,1,0:T(8,128)(2,1)S(1)}, u32[]{:S(2)}, u32[]{:S(2)}) async-start(bf16[8,2,4,16,128]{4,3,2,1,0:T(8,128)(2,1)} %get-tuple-element.20), calls=%async_computation.1 | async-start | bytes 524288 | tf_op jit(solution)/shard_map/all_to_all | solution.py:464
  40.7 0.0 copy-done
  40.7 0.0 copy-start.2
  40.7 0.0 copy-start.4
  40.7 0.0 copy-start.5
  40.7 0.2 shard_map.103
  40.9 4.6 %collective-permute-start.3 = (bf16[8,128,128]{2,1,0:T(8,128)(2,1)S(1)}, bf16[8,128,128]{2,1,0:T(8,128)(2,1)S(1)}, u32[]{:S(2)}, u32[]{:S(2)}) collective-permute-start(bf16[8,128,128]{2,1,0:T(8,128)(2,1)S(1)} %get-tuple-element.21), channel_id=1, source_target_pairs={{0,7},{1,6},{2,5},{3,4},{4,3},{5,2},{6,1},{7,0},{8,15},{9,14},{10,... | collective-permute-start | bytes 786440 | tf_op jit(solution)/shard_map/ppermute | solution.py:481
  45.5 3.4 %collective-permute-start.4 = (bf16[128,128]{1,0:T(8,128)(2,1)S(1)}, bf16[128,128]{1,0:T(8,128)(2,1)S(1)}, u32[]{:S(2)}, u32[]{:S(2)}) collective-permute-start(bf16[128,128]{1,0:T(8,128)(2,1)S(1)} %get-tuple-element.23), channel_id=1, source_target_pairs={{4,0},{7,1},{6,2},{5,3},{12,8},{15,9},{14,10},{13,11},{20,16},{23,... | collective-permute-start | bytes 98312 | tf_op jit(solution)/shard_map/ppermute | solution.py:484
  48.9 3.2 %collective-permute-done.3.upper = bf16[8,128,128]{2,1,0:T(8,128)(2,1)S(1)} collective-permute-done((bf16[8,128,128]{2,1,0:T(8,128)(2,1)S(1)}, bf16[8,128,128]{2,1,0:T(8,128)(2,1)S(1)}, u32[]{:S(2)}, u32[]{:S(2)}) %collective-permute-start.3) | collective-permute-done | bytes 262176 | tf_op jit(solution)/shard_map/ppermute | solution.py:481
  52.1 0.0 copy-done.2
  52.1 0.0 copy-done.4
  52.1 0.0 copy-done.5
  52.1 1.1 %shard_map.104 = (f32[9,128,128]{2,1,0:T(8,128)S(1)}, bf16[2,256,128]{2,1,0:T(8,128)(2,1)S(1)}, bf16[2,128,256]{2,1,0:T(8,128)(2,1)S(1)}, bf16[2,128,256]{2,1,0:T(8,128)(2,1)S(1)}, bf16[2,256,128]{2,1,0:T(8,128)(2,1)S(1)}) custom-call(s32[9]{0:T(128)S(1)} %get-tuple-element.19.scal, f32[128,16,128]{2,1,0:T(8,128)S(1)} %copy-done, ...), custom_call_target="tpu_custom_call" | custom-call | tf_op jit(solution)/shard_map/pallas_call | solution.py:367
  53.2 0.0 collective-permute-done.4.lowest
  53.2 0.0 all-to-all-done.1.got
  53.2 4.0 %shard_map.105 = bf16[8,2,4,16,128]{4,3,2,1,0:T(8,128)(2,1)} custom-call(s32[9]{0:T(128)S(1)} %get-tuple-element.19.scal, bf16[8,2,4,16,128]{4,3,2,1,0:T(8,128)(2,1)S(1)} %all-to-all-done.1.got, f32[9,128,128]{2,1,0:T(8,128)S(1)} %get-tuple-element.22.scale_t, bf16[128,128]{1,0:T(8,128)(2,1)S(1)} %collective-permute-done.4.lowest, ...), custom_call_target="tpu_custom_call" | custom-call | tf_op jit(solution)/shard_map/pallas_call | solution.py:367
  57.2 0.0 copy-start.1
  57.2 5.3 %all-to-all-start.2 = ((bf16[8,2,4,16,128]{4,3,2,1,0:T(8,128)(2,1)}), bf16[8,2,4,16,128]{4,3,2,1,0:T(8,128)(2,1)S(1)}, u32[]{:S(2)}, u32[]{:S(2)}) async-start(bf16[8,2,4,16,128]{4,3,2,1,0:T(8,128)(2,1)} %shard_map.105), calls=%async_computation.2 | async-start | bytes 524288 | tf_op jit(solution)/shard_map/all_to_all | solution.py:464
  62.6 0.0 copy-done.1
  62.6 0.6 shard_map.106.tabs
  63.1 5.3 %all-to-all-done.2.got = bf16[8,2,4,16,128]{4,3,2,1,0:T(8,128)(2,1)S(1)} async-done(((bf16[8,2,4,16,128]{4,3,2,1,0:T(8,128)(2,1)}), bf16[8,2,4,16,128]{4,3,2,1,0:T(8,128)(2,1)S(1)}, u32[]{:S(2)}, u32[]{:S(2)}) %all-to-all-start.2) | async-done | bytes 262176 | tf_op jit(solution)/shard_map/all_to_all | solution.py:464
  68.4 2.0 %shard_map.107 = (bf16[64,32,128]{2,1,0:T(8,128)(2,1)}, bf16[2,8,32,128]{3,2,1,0:T(8,128)(2,1)S(1)}, bf16[2,8,32,128]{3,2,1,0:T(8,128)(2,1)S(1)}) custom-call(s32[9]{0:T(128)S(1)} %get-tuple-element.19.scal, bf16[8,2,4,16,128]{4,3,2,1,0:T(8,128)(2,1)S(1)} %all-to-all-done.2.got, bf16[2,8,32,128]{3,2,1,0:T(8,128)(2,1)S(1)} %get-tuple-element.28.there, ...), custom_call_target="tpu_custom_call" | custom-call | tf_op jit(solution)/shard_map/pallas_call | solution.py:367
  70.4 4.8 %all-to-all-start.3 = ((bf16[8,8,32,128]{3,2,1,0:T(8,128)(2,1)}), bf16[8,8,32,128]{3,2,1,0:T(8,128)(2,1)S(1)}, u32[]{:S(2)}, u32[]{:S(2)}) async-start(bf16[8,8,32,128]{3,2,1,0:T(8,128)(2,1)} %bitcast.6), calls=%async_computation.3 | async-start | bytes 1048576 | tf_op jit(solution)/shard_map/all_to_all | solution.py:464
  75.2 1.9 %collective-permute-start.5 = (bf16[2,8,32,128]{3,2,1,0:T(8,128)(2,1)S(1)}, bf16[2,8,32,128]{3,2,1,0:T(8,128)(2,1)S(1)}, u32[]{:S(2)}, u32[]{:S(2)}) collective-permute-start(bf16[2,8,32,128]{3,2,1,0:T(8,128)(2,1)S(1)} %get-tuple-element.31), channel_id=1, source_target_pairs={{8,0},{0,8},{24,16},{16,24},{40,32},{32,40},{56,48},{48,56},{72,64... | collective-permute-start | bytes 393224 | tf_op jit(solution)/shard_map/ppermute | solution.py:460
  77.2 1.3 %collective-permute-done.5.crossed = bf16[2,8,32,128]{3,2,1,0:T(8,128)(2,1)S(1)} collective-permute-done((bf16[2,8,32,128]{3,2,1,0:T(8,128)(2,1)S(1)}, bf16[2,8,32,128]{3,2,1,0:T(8,128)(2,1)S(1)}, u32[]{:S(2)}, u32[]{:S(2)}) %collective-permute-start.5) | collective-permute-done | bytes 131104 | tf_op jit(solution)/shard_map/ppermute | solution.py:460
  78.5 3.6 %collective-permute-start.6 = (bf16[8,32,128]{2,1,0:T(8,128)(2,1)S(1)}, bf16[8,32,128]{2,1,0:T(8,128)(2,1)S(1)}, u32[]{:S(2)}, u32[]{:S(2)}) collective-permute-start(bf16[8,32,128]{2,1,0:T(8,128)(2,1)S(1)} %get-tuple-element.34), channel_id=1, source_target_pairs={{496,0},{504,8},{0,16},{8,24},{16,32},{24,40},{32,48},{40,56},{48,... | collective-permute-start | bytes 196616 | tf_op jit(solution)/shard_map/ppermute | solution.py:455
  82.1 3.4 %collective-permute-start.7 = (bf16[8,32,128]{2,1,0:T(8,128)(2,1)S(1)}, bf16[8,32,128]{2,1,0:T(8,128)(2,1)S(1)}, u32[]{:S(2)}, u32[]{:S(2)}) collective-permute-start(bf16[8,32,128]{2,1,0:T(8,128)(2,1)S(1)} %get-tuple-element.33), channel_id=1, source_target_pairs={{480,0},{488,8},{496,16},{504,24},{0,32},{8,40},{16,48},{24,56},{3... | collective-permute-start | bytes 196616 | tf_op jit(solution)/shard_map/ppermute | solution.py:455
  85.5 4.2 %collective-permute-done.6.two = bf16[8,32,128]{2,1,0:T(8,128)(2,1)S(1)} collective-permute-done((bf16[8,32,128]{2,1,0:T(8,128)(2,1)S(1)}, bf16[8,32,128]{2,1,0:T(8,128)(2,1)S(1)}, u32[]{:S(2)}, u32[]{:S(2)}) %collective-permute-start.6) | collective-permute-done | bytes 65568 | tf_op jit(solution)/shard_map/ppermute | solution.py:455
  89.7 5.3 %collective-permute-done.7.four = bf16[8,32,128]{2,1,0:T(8,128)(2,1)S(1)} collective-permute-done((bf16[8,32,128]{2,1,0:T(8,128)(2,1)S(1)}, bf16[8,32,128]{2,1,0:T(8,128)(2,1)S(1)}, u32[]{:S(2)}, u32[]{:S(2)}) %collective-permute-start.7) | collective-permute-done | bytes 65568 | tf_op jit(solution)/shard_map/ppermute | solution.py:455
  95.0 0.0 all-to-all-done.3.moved
  95.0 0.8 shard_map.108
  (3 shorter events, 0.1 us)
Async XLA Ops:
  0.9 25.3 %collective-permute-start = (bf16[8,4224]{1,0:T(8,128)(2,1)S(1)}, bf16[8,4224]{1,0:T(8,128)(2,1)S(1)}, u32[]{:S(2)}, u32[]{:S(2)}) collective-permute-start(bf16[8,4224]{1,0:T(8,128)(2,1)S(1)} %shard_map.100.loaded), channel_id=1, source_target_pairs={{16,0},{24,8},{32,16},{40,24},{48,32},{56,40},{64,48},{72,56},{80,... | collective-permute-start | bytes 202760 | tf_op jit(solution)/shard_map/ppermute | solution.py:455
  14.6 11.6 %collective-permute-start.1 = (bf16[8,4224]{1,0:T(8,128)(2,1)S(1)}, bf16[8,4224]{1,0:T(8,128)(2,1)S(1)}, u32[]{:S(2)}, u32[]{:S(2)}) collective-permute-start(bf16[8,4224]{1,0:T(8,128)(2,1)S(1)} %shard_map.100.loaded), channel_id=1, source_target_pairs={{32,0},{40,8},{48,16},{56,24},{64,32},{72,40},{80,48},{88,56},{96,... | collective-permute-start | bytes 202760 | tf_op jit(solution)/shard_map/ppermute | solution.py:455
  20.2 14.0 %copy-start.3 = (f32[128,128]{1,0:T(8,128)S(1)}, f32[128,128]{1,0:T(8,128)}, u32[]{:S(2)}) copy-start(f32[128,128]{1,0:T(8,128)} %constant.38.clone.first_t) | copy-start | bytes 196612
  20.2 14.0 %copy-start.6 = (s32[1,3]{1,0:T(1,128)S(1)}, s32[1,3]{1,0:T(1,128)}, u32[]{:S(2)}) copy-start(s32[1,3]{1,0:T(1,128)} %corner.1) | copy-start | bytes 40
  20.2 14.0 %copy-start.7 = (s32[1,2]{1,0:T(1,128)S(1)}, s32[1,2]{1,0:T(1,128)}, u32[]{:S(2)}) copy-start(s32[1,2]{1,0:T(1,128)} %partners.1) | copy-start | bytes 28
  20.3 14.0 %all-to-all-start = ((bf16[8,8,4096]{2,1,0:T(8,128)(2,1)}), bf16[8,8,4096]{2,1,0:T(8,128)(2,1)S(1)}, u32[]{:S(2)}, u32[]{:S(2)}) async-start(bf16[8,8,4096]{2,1,0:T(8,128)(2,1)} %shard_map.101), calls=%async_computation | async-start | bytes 1048576 | tf_op jit(solution)/shard_map/all_to_all | solution.py:464
  26.2 14.5 %copy-start = (f32[128,16,128]{2,1,0:T(8,128)S(1)}, f32[128,16,128]{2,1,0:T(8,128)}, u32[]{:S(2)}) copy-start(f32[128,16,128]{2,1,0:T(8,128)} %kern.3) | copy-start | bytes 3145732
  26.2 3.4 %collective-permute-start.2 = (bf16[2,8,4224]{2,1,0:T(8,128)(2,1)S(1)}, bf16[2,8,4224]{2,1,0:T(8,128)(2,1)S(1)}, u32[]{:S(2)}, u32[]{:S(2)}) collective-permute-start(bf16[2,8,4224]{2,1,0:T(8,128)(2,1)S(1)} %pad_maximum_fusion), channel_id=1, source_target_pairs={{8,0},{0,8},{24,16},{16,24},{40,32},{32,40},{56,48},{48,56},{72,64... | collective-permute-start | bytes 405512 | tf_op jit(solution)/shard_map/ppermute | solution.py:460
  36.3 16.9 %all-to-all-start.1 = ((bf16[8,2,4,16,128]{4,3,2,1,0:T(8,128)(2,1)}), bf16[8,2,4,16,128]{4,3,2,1,0:T(8,128)(2,1)S(1)}, u32[]{:S(2)}, u32[]{:S(2)}) async-start(bf16[8,2,4,16,128]{4,3,2,1,0:T(8,128)(2,1)} %get-tuple-element.20), calls=%async_computation.1 | async-start | bytes 524288 | tf_op jit(solution)/shard_map/all_to_all | solution.py:464
  40.7 11.4 %copy-start.2 = (bf16[128,128]{1,0:T(8,128)(2,1)S(1)}, bf16[128,128]{1,0:T(8,128)(2,1)}, u32[]{:S(2)}) copy-start(bf16[128,128]{1,0:T(8,128)(2,1)} %constant.39.clone.flip_t) | copy-start | bytes 98308
  40.7 11.4 %copy-start.4 = (f32[128,128]{1,0:T(8,128)S(1)}, f32[128,128]{1,0:T(8,128)}, u32[]{:S(2)}) copy-start(f32[128,128]{1,0:T(8,128)} %constant.40.clone.cos_f) | copy-start | bytes 196612
  40.7 11.4 %copy-start.5 = (f32[128,128]{1,0:T(8,128)S(1)}, f32[128,128]{1,0:T(8,128)}, u32[]{:S(2)}) copy-start(f32[128,128]{1,0:T(8,128)} %constant.41.clone.sin_f) | copy-start | bytes 196612
  40.9 11.2 %collective-permute-start.3 = (bf16[8,128,128]{2,1,0:T(8,128)(2,1)S(1)}, bf16[8,128,128]{2,1,0:T(8,128)(2,1)S(1)}, u32[]{:S(2)}, u32[]{:S(2)}) collective-permute-start(bf16[8,128,128]{2,1,0:T(8,128)(2,1)S(1)} %get-tuple-element.21), channel_id=1, source_target_pairs={{0,7},{1,6},{2,5},{3,4},{4,3},{5,2},{6,1},{7,0},{8,15},{9,14},{10,... | collective-permute-start | bytes 786440 | tf_op jit(solution)/shard_map/ppermute | solution.py:481
  45.5 7.7 %collective-permute-start.4 = (bf16[128,128]{1,0:T(8,128)(2,1)S(1)}, bf16[128,128]{1,0:T(8,128)(2,1)S(1)}, u32[]{:S(2)}, u32[]{:S(2)}) collective-permute-start(bf16[128,128]{1,0:T(8,128)(2,1)S(1)} %get-tuple-element.23), channel_id=1, source_target_pairs={{4,0},{7,1},{6,2},{5,3},{12,8},{15,9},{14,10},{13,11},{20,16},{23,... | collective-permute-start | bytes 98312 | tf_op jit(solution)/shard_map/ppermute | solution.py:484
  57.2 5.3 %copy-start.1 = (f32[512,128]{1,0:T(8,128)S(1)}, f32[512,128]{1,0:T(8,128)}, u32[]{:S(2)}) copy-start(f32[512,128]{1,0:T(8,128)} %constant.42.clone.last_t) | copy-start | bytes 786436
  57.2 11.2 %all-to-all-start.2 = ((bf16[8,2,4,16,128]{4,3,2,1,0:T(8,128)(2,1)}), bf16[8,2,4,16,128]{4,3,2,1,0:T(8,128)(2,1)S(1)}, u32[]{:S(2)}, u32[]{:S(2)}) async-start(bf16[8,2,4,16,128]{4,3,2,1,0:T(8,128)(2,1)} %shard_map.105), calls=%async_computation.2 | async-start | bytes 524288 | tf_op jit(solution)/shard_map/all_to_all | solution.py:464
  70.4 24.6 %all-to-all-start.3 = ((bf16[8,8,32,128]{3,2,1,0:T(8,128)(2,1)}), bf16[8,8,32,128]{3,2,1,0:T(8,128)(2,1)S(1)}, u32[]{:S(2)}, u32[]{:S(2)}) async-start(bf16[8,8,32,128]{3,2,1,0:T(8,128)(2,1)} %bitcast.6), calls=%async_computation.3 | async-start | bytes 1048576 | tf_op jit(solution)/shard_map/all_to_all | solution.py:464
  75.2 3.2 %collective-permute-start.5 = (bf16[2,8,32,128]{3,2,1,0:T(8,128)(2,1)S(1)}, bf16[2,8,32,128]{3,2,1,0:T(8,128)(2,1)S(1)}, u32[]{:S(2)}, u32[]{:S(2)}) collective-permute-start(bf16[2,8,32,128]{3,2,1,0:T(8,128)(2,1)S(1)} %get-tuple-element.31), channel_id=1, source_target_pairs={{8,0},{0,8},{24,16},{16,24},{40,32},{32,40},{56,48},{48,56},{72,64... | collective-permute-start | bytes 393224 | tf_op jit(solution)/shard_map/ppermute | solution.py:460
  78.5 11.2 %collective-permute-start.6 = (bf16[8,32,128]{2,1,0:T(8,128)(2,1)S(1)}, bf16[8,32,128]{2,1,0:T(8,128)(2,1)S(1)}, u32[]{:S(2)}, u32[]{:S(2)}) collective-permute-start(bf16[8,32,128]{2,1,0:T(8,128)(2,1)S(1)} %get-tuple-element.34), channel_id=1, source_target_pairs={{496,0},{504,8},{0,16},{8,24},{16,32},{24,40},{32,48},{40,56},{48,... | collective-permute-start | bytes 196616 | tf_op jit(solution)/shard_map/ppermute | solution.py:455
  82.1 12.9 %collective-permute-start.7 = (bf16[8,32,128]{2,1,0:T(8,128)(2,1)S(1)}, bf16[8,32,128]{2,1,0:T(8,128)(2,1)S(1)}, u32[]{:S(2)}, u32[]{:S(2)}) collective-permute-start(bf16[8,32,128]{2,1,0:T(8,128)(2,1)S(1)} %get-tuple-element.33), channel_id=1, source_target_pairs={{480,0},{488,8},{496,16},{504,24},{0,32},{8,40},{16,48},{24,56},{3... | collective-permute-start | bytes 196616 | tf_op jit(solution)/shard_map/ppermute | solution.py:455

commit v9 on v8

--- a/solution.py
+++ b/solution.py
@@ -297,14 +297,14 @@
         tab_out[n] = jnp.concatenate(parts, axis=0).astype(BF16)
 
 
-def term_kernel(scal, got, there, withs, tabs, move_out, odd_out, even_out, far_s, own_s, sum_s):
+def term_kernel(scal, got, there, withs, tabs, move_h, odd_out, even_out, far_s, own_s, row_s, move_s, sem):
     slab = scal[0]
     low = low_half((FLAT, LANES))
     scale = 1.0 / GRID**3
     clear_edges(own_s, PAIRS * ROWS)
-    blank = jnp.zeros((FLAT, LANES), F32)
+    blank = jnp.zeros((FLAT, LANES), BF16)
     for c in range(EDGE):
-        sum_s[HALF + c] = blank
+        move_s[HALF + c] = blank
     for n in range(PAIRS):
         d0, d1, d2 = scal[1 + 3 * n], scal[2 + 3 * n], scal[3 + 3 * n]
         tab = tabs[n]
@@ -320,15 +320,23 @@
         for r in range(ROWS):
             base = (n * ROWS + r) * SPAN + PAD
             at = HALF + slab * ROWS + r + d0
-            sum_s[at] = sum_s[at] + shifted(own_s, base, d1, d2)
-    for c in range(EDGE):
-        move_out[c] = sum_s[HALF + c].astype(BF16)
+            value = shifted(own_s, base, d1, d2)
+            if n == 0:
+                row_s[r] = value
+            else:
+                other = r + d0 - scal[1]
+                meets = jnp.logical_and(other >= 0, other < ROWS)
+                value = value + jnp.where(meets, row_s[jnp.clip(other, 0, ROWS - 1)], 0.0)
+            move_s[at] = value.astype(BF16)
+    copy = pltpu.make_async_copy(move_s.at[pl.ds(HALF, EDGE)], move_h, sem)
+    copy.start()
     hops = [scal[7 + n] for n in range(PAIRS)]
     for e in range(1, 5):
         target = odd_out if e % 2 else even_out
         for row in range(ROWS):
             value = sum(jnp.where(hops[n] == e, far_s[n, row], 0.0) for n in range(PAIRS))
             target[(e - 1) // 2, row] = value.astype(BF16)
+    copy.wait()
 
 
 def final_kernel(odd_core, moved, crossed, two, four, out, total_s):
@@ -433,14 +441,16 @@
 
 def term_call(scal, got, there, withs, tabs):
     half = (2, ROWS, FLAT, LANES)
-    shapes = (kept((EDGE, FLAT, LANES), BF16), kept(half, BF16), kept(half, BF16))
+    shapes = (far((EDGE, FLAT, LANES), BF16), kept(half, BF16), kept(half, BF16))
     scratch = (
         pltpu.VMEM(ROWBOX, F32),
         pltpu.VMEM((PAIRS * ROWS * SPAN, LANES), F32),
-        pltpu.VMEM((HALF + EDGE + HALF, FLAT, LANES), F32),
+        pltpu.VMEM((ROWS, FLAT, LANES), F32),
+        pltpu.VMEM((HALF + EDGE + HALF, FLAT, LANES), BF16),
+        pltpu.SemaphoreType.DMA,
     )
     args = (scal, near(got), near(there), near(withs), near(tabs))
-    return call(term_kernel, 16, [SMEM] + [VMEM] * 4, shapes, (VMEM,) * 3, scratch, args)
+    return call(term_kernel, 16, [SMEM] + [VMEM] * 4, shapes, (HBM, VMEM, VMEM), scratch, args)
 
 
 def final_call(odd_core, moved, crossed, two, four):

time: 96.6 us -> 96.5 us (level)
  no operation moved by 1% of the time
where the time goes in v9:
time: 96.5 us; the launch traced here: 95.7 us
  starting transfers between devices  57.8 us (60%)
  waiting for transfers between devices  25.2 us (26%)
  Pallas kernels  12.3 us (13%)
    ppermute x4, starting transfers between devices, passed_along(): lax.ppermute(block, 'orb', [((i - distance) % count, i) for i in range(co...  25.4 us
    all_to_all x4, starting transfers between devices, shared(): lax.all_to_all(block, 'slab', split_axis=0, concat_axis=0, tiled=True)  20.5 us
    pallas_call x9, Pallas kernels, call(): pl.pallas_call(kernel, out_shape=out_shape, in_specs=in_specs, out_specs=...  12.3 us
    all_to_all x4, waiting for transfers between devices, shared(): lax.all_to_all(block, 'slab', split_axis=0, concat_axis=0, tiled=True)  9.87 us
    ppermute x4, waiting for transfers between devices, passed_along(): lax.ppermute(block, 'orb', [((i - distance) % count, i) for i in range(co...  9.52 us
    ppermute x1, starting transfers between devices, per_device(): lax.ppermute(upper, 'slab', [(s, SLABS - 1 - s) for s in range(SLABS)])  4.57 us
    ppermute x2, starting transfers between devices, other_core(): return lax.ppermute(block, 'orb', [(i ^ 1, i) for i in range(count)])  3.96 us
    ppermute x1, starting transfers between devices, per_device(): lowest = lax.ppermute(lowest, 'slab', [(4, 0), (7, 1), (6, 2), (5, 3)])  3.4 us
  transfers between devices with their start and end apart: 12, of which 7 were waited for; matrix products, arithmetic and copies ran while one was open for 0% of the time, Pallas kernels for 3%

profile of v9, /device:TPU:8, one launch (start us, length us, event | category | flops | bytes accessed | tf_op | source)
XLA Modules:
  0.0 95.7 jit_solution(512970357971204781)
XLA Ops:
  0.0 0.9 shard_map.100.loaded
  0.9 13.7 %collective-permute-start = (bf16[8,4224]{1,0:T(8,128)(2,1)S(1)}, bf16[8,4224]{1,0:T(8,128)(2,1)S(1)}, u32[]{:S(2)}, u32[]{:S(2)}) collective-permute-start(bf16[8,4224]{1,0:T(8,128)(2,1)S(1)} %shard_map.100.loaded), channel_id=1, source_target_pairs={{16,0},{24,8},{32,16},{40,24},{48,32},{56,40},{64,48},{72,56},{80,... | collective-permute-start | bytes 202760 | tf_op jit(solution)/shard_map/ppermute | solution.py:465
  14.6 4.7 %collective-permute-start.1 = (bf16[8,4224]{1,0:T(8,128)(2,1)S(1)}, bf16[8,4224]{1,0:T(8,128)(2,1)S(1)}, u32[]{:S(2)}, u32[]{:S(2)}) collective-permute-start(bf16[8,4224]{1,0:T(8,128)(2,1)S(1)} %shard_map.100.loaded), channel_id=1, source_target_pairs={{32,0},{40,8},{48,16},{56,24},{64,32},{72,40},{80,48},{88,56},{96,... | collective-permute-start | bytes 202760 | tf_op jit(solution)/shard_map/ppermute | solution.py:465
  19.3 0.9 shard_map.101
  20.2 0.0 copy-start.3
  20.2 0.0 copy-start.6
  20.2 0.0 copy-start.7
  20.3 5.9 %all-to-all-start = ((bf16[8,8,4096]{2,1,0:T(8,128)(2,1)}), bf16[8,8,4096]{2,1,0:T(8,128)(2,1)S(1)}, u32[]{:S(2)}, u32[]{:S(2)}) async-start(bf16[8,8,4096]{2,1,0:T(8,128)(2,1)} %shard_map.101), calls=%async_computation | async-start | bytes 1048576 | tf_op jit(solution)/shard_map/all_to_all | solution.py:474
  26.2 0.0 copy-start
  26.2 0.0 collective-permute-done.two
  26.2 0.0 collective-permute-done.1.four
  26.2 2.1 %collective-permute-start.2 = (bf16[2,8,4224]{2,1,0:T(8,128)(2,1)S(1)}, bf16[2,8,4224]{2,1,0:T(8,128)(2,1)S(1)}, u32[]{:S(2)}, u32[]{:S(2)}) collective-permute-start(bf16[2,8,4224]{2,1,0:T(8,128)(2,1)S(1)} %pad_maximum_fusion), channel_id=1, source_target_pairs={{8,0},{0,8},{24,16},{16,24},{40,32},{32,40},{56,48},{48,56},{72,64... | collective-permute-start | bytes 405512 | tf_op jit(solution)/shard_map/ppermute | solution.py:470
  28.3 0.1 pad_add_fusion.info
  28.4 1.2 %collective-permute-done.2.odd = bf16[2,8,4224]{2,1,0:T(8,128)(2,1)S(1)} collective-permute-done((bf16[2,8,4224]{2,1,0:T(8,128)(2,1)S(1)}, bf16[2,8,4224]{2,1,0:T(8,128)(2,1)S(1)}, u32[]{:S(2)}, u32[]{:S(2)}) %collective-permute-start.2) | collective-permute-done | bytes 135200 | tf_op jit(solution)/shard_map/ppermute | solution.py:470
  29.6 4.6 %all-to-all-done.own_in = bf16[8,8,4096]{2,1,0:T(8,128)(2,1)S(1)} async-done(((bf16[8,8,4096]{2,1,0:T(8,128)(2,1)}), bf16[8,8,4096]{2,1,0:T(8,128)(2,1)S(1)}, u32[]{:S(2)}, u32[]{:S(2)}) %all-to-all-start) | async-done | bytes 524320 | tf_op jit(solution)/shard_map/all_to_all | solution.py:474
  34.2 0.0 copy-done.3
  34.2 0.0 copy-done.6
  34.2 0.0 copy-done.7
  34.2 2.0 %shard_map.102 = (bf16[8,2,4,16,128]{4,3,2,1,0:T(8,128)(2,1)}, bf16[2,8,32,128]{3,2,1,0:T(8,128)(2,1)S(1)}, bf16[2,8,32,128]{3,2,1,0:T(8,128)(2,1)S(1)}, s32[9]{0:T(128)S(1)}) custom-call(s32[2]{0:T(128)S(1)} %pad_add_fusion.info, s32[1,2]{1,0:T(1,128)S(1)} %copy-done.7, s32[1,3]{1,0:T(1,128)S(1)} %copy-done.6, ...), custom_call_target="tpu_custom_call" | custom-call | tf_op jit(solution)/shard_map/pallas_call | solution.py:375
  36.3 4.4 %all-to-all-start.1 = ((bf16[8,2,4,16,128]{4,3,2,1,0:T(8,128)(2,1)}), bf16[8,2,4,16,128]{4,3,2,1,0:T(8,128)(2,1)S(1)}, u32[]{:S(2)}, u32[]{:S(2)}) async-start(bf16[8,2,4,16,128]{4,3,2,1,0:T(8,128)(2,1)} %get-tuple-element.20), calls=%async_computation.1 | async-start | bytes 524288 | tf_op jit(solution)/shard_map/all_to_all | solution.py:474
  40.7 0.0 copy-done
  40.7 0.0 copy-start.2
  40.7 0.0 copy-start.4
  40.7 0.0 copy-start.5
  40.7 0.2 shard_map.103
  40.9 4.6 %collective-permute-start.3 = (bf16[8,128,128]{2,1,0:T(8,128)(2,1)S(1)}, bf16[8,128,128]{2,1,0:T(8,128)(2,1)S(1)}, u32[]{:S(2)}, u32[]{:S(2)}) collective-permute-start(bf16[8,128,128]{2,1,0:T(8,128)(2,1)S(1)} %get-tuple-element.21), channel_id=1, source_target_pairs={{0,7},{1,6},{2,5},{3,4},{4,3},{5,2},{6,1},{7,0},{8,15},{9,14},{10,... | collective-permute-start | bytes 786440 | tf_op jit(solution)/shard_map/ppermute | solution.py:491
  45.5 3.4 %collective-permute-start.4 = (bf16[128,128]{1,0:T(8,128)(2,1)S(1)}, bf16[128,128]{1,0:T(8,128)(2,1)S(1)}, u32[]{:S(2)}, u32[]{:S(2)}) collective-permute-start(bf16[128,128]{1,0:T(8,128)(2,1)S(1)} %get-tuple-element.23), channel_id=1, source_target_pairs={{4,0},{7,1},{6,2},{5,3},{12,8},{15,9},{14,10},{13,11},{20,16},{23,... | collective-permute-start | bytes 98312 | tf_op jit(solution)/shard_map/ppermute | solution.py:494
  48.9 3.2 %collective-permute-done.3.upper = bf16[8,128,128]{2,1,0:T(8,128)(2,1)S(1)} collective-permute-done((bf16[8,128,128]{2,1,0:T(8,128)(2,1)S(1)}, bf16[8,128,128]{2,1,0:T(8,128)(2,1)S(1)}, u32[]{:S(2)}, u32[]{:S(2)}) %collective-permute-start.3) | collective-permute-done | bytes 262176 | tf_op jit(solution)/shard_map/ppermute | solution.py:491
  52.1 0.0 copy-done.2
  52.1 0.0 copy-done.4
  52.1 0.0 copy-done.5
  52.1 1.1 %shard_map.104 = (f32[9,128,128]{2,1,0:T(8,128)S(1)}, bf16[2,256,128]{2,1,0:T(8,128)(2,1)S(1)}, bf16[2,128,256]{2,1,0:T(8,128)(2,1)S(1)}, bf16[2,128,256]{2,1,0:T(8,128)(2,1)S(1)}, bf16[2,256,128]{2,1,0:T(8,128)(2,1)S(1)}) custom-call(s32[9]{0:T(128)S(1)} %get-tuple-element.19.scal, f32[128,16,128]{2,1,0:T(8,128)S(1)} %copy-done, ...), custom_call_target="tpu_custom_call" | custom-call | tf_op jit(solution)/shard_map/pallas_call | solution.py:375
  53.2 0.0 collective-permute-done.4.lowest
  53.2 0.0 all-to-all-done.1.got
  53.2 4.0 %shard_map.105 = bf16[8,2,4,16,128]{4,3,2,1,0:T(8,128)(2,1)} custom-call(s32[9]{0:T(128)S(1)} %get-tuple-element.19.scal, bf16[8,2,4,16,128]{4,3,2,1,0:T(8,128)(2,1)S(1)} %all-to-all-done.1.got, f32[9,128,128]{2,1,0:T(8,128)S(1)} %get-tuple-element.22.scale_t, bf16[128,128]{1,0:T(8,128)(2,1)S(1)} %collective-permute-done.4.lowest, ...), custom_call_target="tpu_custom_call" | custom-call | tf_op jit(solution)/shard_map/pallas_call | solution.py:375
  57.2 0.0 copy-start.1
  57.2 5.3 %all-to-all-start.2 = ((bf16[8,2,4,16,128]{4,3,2,1,0:T(8,128)(2,1)}), bf16[8,2,4,16,128]{4,3,2,1,0:T(8,128)(2,1)S(1)}, u32[]{:S(2)}, u32[]{:S(2)}) async-start(bf16[8,2,4,16,128]{4,3,2,1,0:T(8,128)(2,1)} %shard_map.105), calls=%async_computation.2 | async-start | bytes 524288 | tf_op jit(solution)/shard_map/all_to_all | solution.py:474
  62.6 0.0 copy-done.1
  62.6 0.6 shard_map.106.tabs
  63.1 5.3 %all-to-all-done.2.got = bf16[8,2,4,16,128]{4,3,2,1,0:T(8,128)(2,1)S(1)} async-done(((bf16[8,2,4,16,128]{4,3,2,1,0:T(8,128)(2,1)}), bf16[8,2,4,16,128]{4,3,2,1,0:T(8,128)(2,1)S(1)}, u32[]{:S(2)}, u32[]{:S(2)}) %all-to-all-start.2) | async-done | bytes 262176 | tf_op jit(solution)/shard_map/all_to_all | solution.py:474
  68.4 2.0 %shard_map.107 = (bf16[64,32,128]{2,1,0:T(8,128)(2,1)}, bf16[2,8,32,128]{3,2,1,0:T(8,128)(2,1)S(1)}, bf16[2,8,32,128]{3,2,1,0:T(8,128)(2,1)S(1)}) custom-call(s32[9]{0:T(128)S(1)} %get-tuple-element.19.scal, bf16[8,2,4,16,128]{4,3,2,1,0:T(8,128)(2,1)S(1)} %all-to-all-done.2.got, bf16[2,8,32,128]{3,2,1,0:T(8,128)(2,1)S(1)} %get-tuple-element.28.there, ...), custom_call_target="tpu_custom_call" | custom-call | tf_op jit(solution)/shard_map/pallas_call | solution.py:375
  70.4 4.8 %all-to-all-start.3 = ((bf16[8,8,32,128]{3,2,1,0:T(8,128)(2,1)}), bf16[8,8,32,128]{3,2,1,0:T(8,128)(2,1)S(1)}, u32[]{:S(2)}, u32[]{:S(2)}) async-start(bf16[8,8,32,128]{3,2,1,0:T(8,128)(2,1)} %bitcast.14), calls=%async_computation.3 | async-start | bytes 1048576 | tf_op jit(solution)/shard_map/all_to_all | solution.py:474
  75.2 1.9 %collective-permute-start.5 = (bf16[2,8,32,128]{3,2,1,0:T(8,128)(2,1)S(1)}, bf16[2,8,32,128]{3,2,1,0:T(8,128)(2,1)S(1)}, u32[]{:S(2)}, u32[]{:S(2)}) collective-permute-start(bf16[2,8,32,128]{3,2,1,0:T(8,128)(2,1)S(1)} %get-tuple-element.31), channel_id=1, source_target_pairs={{8,0},{0,8},{24,16},{16,24},{40,32},{32,40},{56,48},{48,56},{72,64... | collective-permute-start | bytes 393224 | tf_op jit(solution)/shard_map/ppermute | solution.py:470
  77.1 1.3 %collective-permute-done.5.crossed = bf16[2,8,32,128]{3,2,1,0:T(8,128)(2,1)S(1)} collective-permute-done((bf16[2,8,32,128]{3,2,1,0:T(8,128)(2,1)S(1)}, bf16[2,8,32,128]{3,2,1,0:T(8,128)(2,1)S(1)}, u32[]{:S(2)}, u32[]{:S(2)}) %collective-permute-start.5) | collective-permute-done | bytes 131104 | tf_op jit(solution)/shard_map/ppermute | solution.py:470
  78.5 3.6 %collective-permute-start.6 = (bf16[8,32,128]{2,1,0:T(8,128)(2,1)S(1)}, bf16[8,32,128]{2,1,0:T(8,128)(2,1)S(1)}, u32[]{:S(2)}, u32[]{:S(2)}) collective-permute-start(bf16[8,32,128]{2,1,0:T(8,128)(2,1)S(1)} %get-tuple-element.34), channel_id=1, source_target_pairs={{496,0},{504,8},{0,16},{8,24},{16,32},{24,40},{32,48},{40,56},{48,... | collective-permute-start | bytes 196616 | tf_op jit(solution)/shard_map/ppermute | solution.py:465
  82.1 3.4 %collective-permute-start.7 = (bf16[8,32,128]{2,1,0:T(8,128)(2,1)S(1)}, bf16[8,32,128]{2,1,0:T(8,128)(2,1)S(1)}, u32[]{:S(2)}, u32[]{:S(2)}) collective-permute-start(bf16[8,32,128]{2,1,0:T(8,128)(2,1)S(1)} %get-tuple-element.33), channel_id=1, source_target_pairs={{480,0},{488,8},{496,16},{504,24},{0,32},{8,40},{16,48},{24,56},{3... | collective-permute-start | bytes 196616 | tf_op jit(solution)/shard_map/ppermute | solution.py:465
  85.5 4.2 %collective-permute-done.6.two = bf16[8,32,128]{2,1,0:T(8,128)(2,1)S(1)} collective-permute-done((bf16[8,32,128]{2,1,0:T(8,128)(2,1)S(1)}, bf16[8,32,128]{2,1,0:T(8,128)(2,1)S(1)}, u32[]{:S(2)}, u32[]{:S(2)}) %collective-permute-start.6) | collective-permute-done | bytes 65568 | tf_op jit(solution)/shard_map/ppermute | solution.py:465
  89.7 5.3 %collective-permute-done.7.four = bf16[8,32,128]{2,1,0:T(8,128)(2,1)S(1)} collective-permute-done((bf16[8,32,128]{2,1,0:T(8,128)(2,1)S(1)}, bf16[8,32,128]{2,1,0:T(8,128)(2,1)S(1)}, u32[]{:S(2)}, u32[]{:S(2)}) %collective-permute-start.7) | collective-permute-done | bytes 65568 | tf_op jit(solution)/shard_map/ppermute | solution.py:465
  95.0 0.0 all-to-all-done.3.moved
  95.0 0.8 shard_map.108
  (3 shorter events, 0.1 us)
Async XLA Ops:
  0.9 25.3 %collective-permute-start = (bf16[8,4224]{1,0:T(8,128)(2,1)S(1)}, bf16[8,4224]{1,0:T(8,128)(2,1)S(1)}, u32[]{:S(2)}, u32[]{:S(2)}) collective-permute-start(bf16[8,4224]{1,0:T(8,128)(2,1)S(1)} %shard_map.100.loaded), channel_id=1, source_target_pairs={{16,0},{24,8},{32,16},{40,24},{48,32},{56,40},{64,48},{72,56},{80,... | collective-permute-start | bytes 202760 | tf_op jit(solution)/shard_map/ppermute | solution.py:465
  14.6 11.6 %collective-permute-start.1 = (bf16[8,4224]{1,0:T(8,128)(2,1)S(1)}, bf16[8,4224]{1,0:T(8,128)(2,1)S(1)}, u32[]{:S(2)}, u32[]{:S(2)}) collective-permute-start(bf16[8,4224]{1,0:T(8,128)(2,1)S(1)} %shard_map.100.loaded), channel_id=1, source_target_pairs={{32,0},{40,8},{48,16},{56,24},{64,32},{72,40},{80,48},{88,56},{96,... | collective-permute-start | bytes 202760 | tf_op jit(solution)/shard_map/ppermute | solution.py:465
  20.2 14.0 %copy-start.3 = (f32[128,128]{1,0:T(8,128)S(1)}, f32[128,128]{1,0:T(8,128)}, u32[]{:S(2)}) copy-start(f32[128,128]{1,0:T(8,128)} %constant.38.clone.first_t) | copy-start | bytes 196612
  20.2 14.0 %copy-start.6 = (s32[1,3]{1,0:T(1,128)S(1)}, s32[1,3]{1,0:T(1,128)}, u32[]{:S(2)}) copy-start(s32[1,3]{1,0:T(1,128)} %corner.1) | copy-start | bytes 40
  20.2 14.0 %copy-start.7 = (s32[1,2]{1,0:T(1,128)S(1)}, s32[1,2]{1,0:T(1,128)}, u32[]{:S(2)}) copy-start(s32[1,2]{1,0:T(1,128)} %partners.1) | copy-start | bytes 28
  20.3 14.0 %all-to-all-start = ((bf16[8,8,4096]{2,1,0:T(8,128)(2,1)}), bf16[8,8,4096]{2,1,0:T(8,128)(2,1)S(1)}, u32[]{:S(2)}, u32[]{:S(2)}) async-start(bf16[8,8,4096]{2,1,0:T(8,128)(2,1)} %shard_map.101), calls=%async_computation | async-start | bytes 1048576 | tf_op jit(solution)/shard_map/all_to_all | solution.py:474
  26.2 14.5 %copy-start = (f32[128,16,128]{2,1,0:T(8,128)S(1)}, f32[128,16,128]{2,1,0:T(8,128)}, u32[]{:S(2)}) copy-start(f32[128,16,128]{2,1,0:T(8,128)} %kern.3) | copy-start | bytes 3145732
  26.2 3.4 %collective-permute-start.2 = (bf16[2,8,4224]{2,1,0:T(8,128)(2,1)S(1)}, bf16[2,8,4224]{2,1,0:T(8,128)(2,1)S(1)}, u32[]{:S(2)}, u32[]{:S(2)}) collective-permute-start(bf16[2,8,4224]{2,1,0:T(8,128)(2,1)S(1)} %pad_maximum_fusion), channel_id=1, source_target_pairs={{8,0},{0,8},{24,16},{16,24},{40,32},{32,40},{56,48},{48,56},{72,64... | collective-permute-start | bytes 405512 | tf_op jit(solution)/shard_map/ppermute | solution.py:470
  36.3 16.9 %all-to-all-start.1 = ((bf16[8,2,4,16,128]{4,3,2,1,0:T(8,128)(2,1)}), bf16[8,2,4,16,128]{4,3,2,1,0:T(8,128)(2,1)S(1)}, u32[]{:S(2)}, u32[]{:S(2)}) async-start(bf16[8,2,4,16,128]{4,3,2,1,0:T(8,128)(2,1)} %get-tuple-element.20), calls=%async_computation.1 | async-start | bytes 524288 | tf_op jit(solution)/shard_map/all_to_all | solution.py:474
  40.7 11.4 %copy-start.2 = (bf16[128,128]{1,0:T(8,128)(2,1)S(1)}, bf16[128,128]{1,0:T(8,128)(2,1)}, u32[]{:S(2)}) copy-start(bf16[128,128]{1,0:T(8,128)(2,1)} %constant.39.clone.flip_t) | copy-start | bytes 98308
  40.7 11.4 %copy-start.4 = (f32[128,128]{1,0:T(8,128)S(1)}, f32[128,128]{1,0:T(8,128)}, u32[]{:S(2)}) copy-start(f32[128,128]{1,0:T(8,128)} %constant.40.clone.cos_f) | copy-start | bytes 196612
  40.7 11.4 %copy-start.5 = (f32[128,128]{1,0:T(8,128)S(1)}, f32[128,128]{1,0:T(8,128)}, u32[]{:S(2)}) copy-start(f32[128,128]{1,0:T(8,128)} %constant.41.clone.sin_f) | copy-start | bytes 196612
  40.9 11.2 %collective-permute-start.3 = (bf16[8,128,128]{2,1,0:T(8,128)(2,1)S(1)}, bf16[8,128,128]{2,1,0:T(8,128)(2,1)S(1)}, u32[]{:S(2)}, u32[]{:S(2)}) collective-permute-start(bf16[8,128,128]{2,1,0:T(8,128)(2,1)S(1)} %get-tuple-element.21), channel_id=1, source_target_pairs={{0,7},{1,6},{2,5},{3,4},{4,3},{5,2},{6,1},{7,0},{8,15},{9,14},{10,... | collective-permute-start | bytes 786440 | tf_op jit(solution)/shard_map/ppermute | solution.py:491
  45.5 7.7 %collective-permute-start.4 = (bf16[128,128]{1,0:T(8,128)(2,1)S(1)}, bf16[128,128]{1,0:T(8,128)(2,1)S(1)}, u32[]{:S(2)}, u32[]{:S(2)}) collective-permute-start(bf16[128,128]{1,0:T(8,128)(2,1)S(1)} %get-tuple-element.23), channel_id=1, source_target_pairs={{4,0},{7,1},{6,2},{5,3},{12,8},{15,9},{14,10},{13,11},{20,16},{23,... | collective-permute-start | bytes 98312 | tf_op jit(solution)/shard_map/ppermute | solution.py:494
  57.2 5.3 %copy-start.1 = (f32[512,128]{1,0:T(8,128)S(1)}, f32[512,128]{1,0:T(8,128)}, u32[]{:S(2)}) copy-start(f32[512,128]{1,0:T(8,128)} %constant.42.clone.last_t) | copy-start | bytes 786436
  57.2 11.2 %all-to-all-start.2 = ((bf16[8,2,4,16,128]{4,3,2,1,0:T(8,128)(2,1)}), bf16[8,2,4,16,128]{4,3,2,1,0:T(8,128)(2,1)S(1)}, u32[]{:S(2)}, u32[]{:S(2)}) async-start(bf16[8,2,4,16,128]{4,3,2,1,0:T(8,128)(2,1)} %shard_map.105), calls=%async_computation.2 | async-start | bytes 524288 | tf_op jit(solution)/shard_map/all_to_all | solution.py:474
  70.4 24.6 %all-to-all-start.3 = ((bf16[8,8,32,128]{3,2,1,0:T(8,128)(2,1)}), bf16[8,8,32,128]{3,2,1,0:T(8,128)(2,1)S(1)}, u32[]{:S(2)}, u32[]{:S(2)}) async-start(bf16[8,8,32,128]{3,2,1,0:T(8,128)(2,1)} %bitcast.14), calls=%async_computation.3 | async-start | bytes 1048576 | tf_op jit(solution)/shard_map/all_to_all | solution.py:474
  75.2 3.2 %collective-permute-start.5 = (bf16[2,8,32,128]{3,2,1,0:T(8,128)(2,1)S(1)}, bf16[2,8,32,128]{3,2,1,0:T(8,128)(2,1)S(1)}, u32[]{:S(2)}, u32[]{:S(2)}) collective-permute-start(bf16[2,8,32,128]{3,2,1,0:T(8,128)(2,1)S(1)} %get-tuple-element.31), channel_id=1, source_target_pairs={{8,0},{0,8},{24,16},{16,24},{40,32},{32,40},{56,48},{48,56},{72,64... | collective-permute-start | bytes 393224 | tf_op jit(solution)/shard_map/ppermute | solution.py:470
  78.5 11.2 %collective-permute-start.6 = (bf16[8,32,128]{2,1,0:T(8,128)(2,1)S(1)}, bf16[8,32,128]{2,1,0:T(8,128)(2,1)S(1)}, u32[]{:S(2)}, u32[]{:S(2)}) collective-permute-start(bf16[8,32,128]{2,1,0:T(8,128)(2,1)S(1)} %get-tuple-element.34), channel_id=1, source_target_pairs={{496,0},{504,8},{0,16},{8,24},{16,32},{24,40},{32,48},{40,56},{48,... | collective-permute-start | bytes 196616 | tf_op jit(solution)/shard_map/ppermute | solution.py:465
  82.1 12.9 %collective-permute-start.7 = (bf16[8,32,128]{2,1,0:T(8,128)(2,1)S(1)}, bf16[8,32,128]{2,1,0:T(8,128)(2,1)S(1)}, u32[]{:S(2)}, u32[]{:S(2)}) collective-permute-start(bf16[8,32,128]{2,1,0:T(8,128)(2,1)S(1)} %get-tuple-element.33), channel_id=1, source_target_pairs={{480,0},{488,8},{496,16},{504,24},{0,32},{8,40},{16,48},{24,56},{3... | collective-permute-start | bytes 196616 | tf_op jit(solution)/shard_map/ppermute | solution.py:465
